TPU v7x, 32 devices: a whole 2x2x4 slice. The times are simulated.
32 devices in a mesh: clu: 8 (over z, x), col: 4 (over y, core).
Axes of the slice: x: 2, y: 2, z: 4, core: 2. Of those that a mesh axis runs over, the one named last changes fastest.
Arguments:
- features: bfloat16 [65536, 2048], P('clu', 'col'), may hold values from -6 to 6
- weight: bfloat16 [2048, 2048], P(None, 'col'), may hold values from -0.125 to 0.125
- bias: bfloat16 [2048], P('col'), may hold values from -3 to 3
- adjacency: int32 [65536, 128], P('clu'), may hold values from 0 to 1, as said below
- segments: int32 [512, 128], P('clu'), may hold values from 0 to 3, never falling along the last dimension, each value on 1 to 48 neighbouring positions
- cotangent: bfloat16 [65536, 2048], P('clu', 'col'), may hold values from -6 to 6
Outputs:
- activations: bfloat16 [65536, 2048], P('clu', 'col')
- grad_features: float32 [65536, 2048], P('clu', 'col')
- grad_weight: float32 [2048, 2048], P(None, 'col')
- grad_bias: float32 [2048], P('col')
Inputs may be any that keep to these rules, and one draw needn't show every extreme that they name: `adjacency`: 0 or 1; within each block of 128 nodes the links are symmetric and a node has no link to itself.
All inputs are finite; a program needn't handle non-finite values.
Results may differ from a plain program's by a relative error of at most 0.0065.
The roundings to bfloat16 on the way count: a program that leaves them out, or rounds other values in their place, can miss the bound.
Values may be sent and summed in bfloat16 or wider, within the bound.
A program may use at most 256 MiB of HBM per device.

v0:
```python
import jax
import jax.numpy as jnp
from jax import lax
from jax.sharding import PartitionSpec as P


def local(features, weight, bias, adjacency, segments, cotangent):
    node_rows = features.shape[0]
    blocks = node_rows // 128
    linked = adjacency.reshape(blocks, 128, 128)
    same_cluster = segments[:, :, None] == segments[:, None, :]
    links = jnp.where(same_cluster, linked, 0).astype(jnp.float32)
    degree = jnp.sum(links, axis=-1).reshape(-1, 1)
    inverse = 1.0 / (degree + 1.0)
    eye = jnp.eye(128, dtype=jnp.float32)
    stencil = (links + 2.0 * eye[None, :, :]).astype(jnp.bfloat16)
    grouped = features.reshape(blocks, 128, -1)
    summed = jnp.einsum(
        "bij,bjf->bif", stencil, grouped, preferred_element_type=jnp.float32
    ).reshape(node_rows, -1)
    aggregated = (summed * inverse).astype(jnp.bfloat16)
    gathered = lax.all_gather(aggregated, "col", axis=1, tiled=True)
    preact = (
        jnp.dot(gathered, weight, preferred_element_type=jnp.float32)
        + bias.astype(jnp.float32)[None, :]
    )
    output = jnp.maximum(preact, 0.0).astype(jnp.bfloat16)
    grad_preact = jnp.where(preact > 0.0, cotangent.astype(jnp.float32), 0.0).astype(jnp.bfloat16)
    partials = lax.dot_general(
        grad_preact, weight, (((1,), (1,)), ((), ())), preferred_element_type=jnp.float32
    )
    grad_aggregated = lax.psum_scatter(partials, "col", scatter_dimension=1, tiled=True).astype(
        jnp.bfloat16
    )
    grad_weight = lax.dot_general(
        gathered, grad_preact, (((0,), (0,)), ((), ())), preferred_element_type=jnp.float32
    )
    grad_bias = jnp.sum(grad_preact.astype(jnp.float32), axis=0)
    grad_weight, grad_bias = lax.psum((grad_weight, grad_bias), "clu")
    grad_summed = (grad_aggregated.astype(jnp.float32) * inverse).astype(jnp.bfloat16)
    grad_feats = jnp.einsum(
        "bji,bjf->bif",
        stencil,
        grad_summed.reshape(blocks, 128, -1),
        preferred_element_type=jnp.float32,
    ).reshape(node_rows, -1)
    return (output, grad_feats, grad_weight, grad_bias)


def solution(mesh):
    return jax.shard_map(
        local,
        mesh=mesh,
        in_specs=(
            P("clu", "col"),
            P(None, "col"),
            P("col"),
            P("clu", None),
            P("clu", None),
            P("clu", "col"),
        ),
        out_specs=(P("clu", "col"), P("clu", "col"), P(None, "col"), P("col")),
        check_vma=False,
    )
```

profile of v0, /device:TPU:0, one launch (start us, length us, event | category | flops | bytes accessed | tf_op | source)
XLA Modules:
  0.0 915.6 jit_solution(2399170666423392285)
XLA Ops:
  7.2 0.0 copy-start
  7.2 0.0 copy-start.3
  7.2 0.0 all-gather.2.cloned.1.call-start
  7.3 4.6 convert_reduce_fusion.1
  11.9 5.6 copy.10
  17.5 0.0 copy-done.3
  17.5 7.3 fusion.2
  24.8 4.8 fusion
  29.6 0.0 copy-start.4
  29.6 0.0 all-gather.2.cloned.1.call-update
  29.7 0.2 reduce-scatter.2.cloned.1.call-start
  29.9 0.4 copy-done.4
  30.3 203.7 %all-gather.2.cloned.1.call-done = bf16[8192,2048]{1,0:T(8,128)(2,1)} async-done(((bf16[8192,512]{1,0:T(8,128)(2,1)}), bf16[8192,2048]{1,0:T(8,128)(2,1)}) %all-gather.2.cloned.1.call-update) | async-done | bytes 33554448 | tf_op jit(solution)/shard_map/all_gather | solution.py:22
  234.1 0.0 copy-done
  234.1 28.2 %convert_reduce_fusion = (f32[512]{0:T(512)S(1)}, bf16[8192,512]{1,0:T(8,128)(2,1)}, bf16[8192,512]{1,0:T(8,128)(2,1)}) fusion(bf16[8192,512]{1,0:T(8,128)(2,1)} %param.11, f32[512]{0:T(512)S(1)} %convert_element_type.42, bf16[8192,2048]{1,0:T(8,128)(2,1)} %all-gather.2.cloned.1.call-done, bf16[2048,512]{1,0:T(8,128)(2,1)S(1)} %copy-done), kind=kOutput, calls=%fused_computation.2 | convolution fusion | flops 17217617920 | bytes 60821504 | tf_op jit(solution)/shard_map/dot_general | solution.py:24
  262.2 29.1 %fusion.6 = f32[8192,2048]{1,0:T(8,128)} fusion(bf16[8192,512]{1,0:T(8,128)(2,1)} %get-tuple-element.5, bf16[2048,512]{1,0:T(8,128)(2,1)S(1)} %copy-done), kind=kOutput, calls=%fused_computation.16 | convolution fusion | flops 17179869184 | bytes 77594624 | tf_op jit(solution)/shard_map/dot_general | solution.py:29
  291.4 0.0 reduce-scatter.2.cloned.1.call-update
  291.4 0.3 all-reduce.2.cloned.1.call-start
  291.6 26.9 %fusion.7 = f32[2048,512]{1,0:T(8,128)} fusion(bf16[8192,2048]{1,0:T(8,128)(2,1)} %all-gather.2.cloned.1.call-done, bf16[8192,512]{1,0:T(8,128)(2,1)} %get-tuple-element.5), kind=kOutput, calls=%fused_computation.17 | convolution fusion | flops 17179869184 | bytes 46137344 | tf_op jit(solution)/shard_map/dot_general | solution.py:35
  318.6 0.0 all-reduce.2.cloned.1.call-update
  318.6 21.5 %psum.15 = f32[512]{0:T(512)} all-reduce(f32[512]{0:T(512)S(1)} %get-tuple-element.4), channel_id=1, replica_groups=mesh['clu'=8,'col'=4] {'clu'}, use_global_device_ids=true, to_apply=%region_4.5 | all-reduce | flops 512 | bytes 4096 | tf_op jit(solution)/shard_map/psum | solution.py:39
  340.1 403.8 %reduce-scatter.2.cloned.1.call-done = f32[8192,512]{1,0:T(8,128)} async-done(((f32[8192,2048]{1,0:T(8,128)}), f32[8192,512]{1,0:T(8,128)}) %reduce-scatter.2.cloned.1.call-update) | async-done | bytes 16777232 | tf_op jit(solution)/shard_map/reduce_scatter | solution.py:32
  743.9 0.0 copy-start.2
  743.9 6.7 multiply_convert_fusion
  750.7 0.3 copy-done.2
  751.0 0.0 copy-start.1
  751.0 7.2 fusion.1
  758.1 146.3 %all-reduce.2.cloned.1.call-done = f32[2048,512]{1,0:T(8,128)} async-done(((f32[2048,512]{1,0:T(8,128)}), f32[2048,512]{1,0:T(8,128)}) %all-reduce.2.cloned.1.call-update) | async-done | bytes 4194320 | tf_op jit(solution)/shard_map/psum | solution.py:39
  904.4 4.6 copy.17
  909.0 0.0 copy-done.1
  (3 shorter events, 0.0 us)
Async XLA Ops:
  7.2 226.9 %copy-start = (bf16[2048,512]{1,0:T(8,128)(2,1)S(1)}, bf16[2048,512]{1,0:T(8,128)(2,1)}, u32[]{:S(2)}) copy-start(bf16[2048,512]{1,0:T(8,128)(2,1)} %param.7) | copy-start | bytes 6291460
  7.2 10.3 %copy-start.3 = (s32[64,128]{1,0:T(8,128)S(1)}, s32[64,128]{1,0:T(8,128)}, u32[]{:S(2)}) copy-start(s32[64,128]{1,0:T(8,128)} %param.10) | copy-start | bytes 98308
  7.2 226.9 %all-gather.2.cloned.1.call-start = ((), (), s32[]{:S(2)}) async-start(), calls=%async_computation.1 | async-start | bytes 41943040 | tf_op jit(solution)/shard_map/all_gather | solution.py:22
  29.6 0.7 copy-start.4
  29.7 714.3 %reduce-scatter.2.cloned.1.call-start = ((), (), s32[]{:S(2)}) async-start(), calls=%async_computation.2 | async-start | bytes 83886080 | tf_op jit(solution)/shard_map/reduce_scatter | solution.py:32
  291.4 613.0 %all-reduce.2.cloned.1.call-start = ((), (), s32[]{:S(2)}) async-start(), calls=%async_computation.3 | async-start | bytes 8388608 | tf_op jit(solution)/shard_map/psum | solution.py:39
  743.9 7.0 copy-start.2
  751.0 158.1 %copy-start.1 = (bf16[2048,512]{1,0:T(8,128)(2,1)S(1)}, bf16[2048,512]{1,0:T(8,128)(2,1)}, u32[]{:S(2)}) copy-start(bf16[2048,512]{1,0:T(8,128)(2,1)} %param.7) | copy-start | bytes 6291460
Sparse Core Ops, SparseCore 0:
  29.8 204.2 all-gather.1
  291.5 452.3 reduce-scatter.1
  748.1 156.2 all-reduce.1
where the time goes:
time: 916 us
  waiting for transfers between devices  754 us (82%)
  matrix products  98.8 us (11%)
  blocking collectives  21.5 us (2%)
  other arithmetic  16.2 us (2%)
  between operations  13.8 us (2%)
  local copies, waits for them, and re-layouts  11 us (1%)
    reduce_scatter x1, waiting for transfers between devices, local(): lax.psum_scatter(partials, 'col', scatter_dimension=1, tiled=True)  404 us
    all_gather x1, waiting for transfers between devices, local(): gathered = lax.all_gather(aggregated, 'col', axis=1, tiled=True)  204 us
    psum x1, waiting for transfers between devices, local(): grad_weight, grad_bias = lax.psum((grad_weight, grad_bias), 'clu')  146 us
    dot_general x1, matrix products, local(): lax.dot_general(grad_preact, weight, (((1,), (1,)), ((), ())), preferred_...  29.1 us
    dot_general x1, matrix products, local(): jnp.dot(gathered, weight, preferred_element_type=jnp.float32)  28.2 us
    dot_general x1, matrix products, local(): lax.dot_general(gathered, grad_preact, (((0,), (0,)), ((), ())), preferre...  26.9 us
    psum x1, blocking collectives, local(): grad_weight, grad_bias = lax.psum((grad_weight, grad_bias), 'clu')  21.5 us
  transfers between devices with their start and end apart: 3, of which 3 were waited for; matrix products, arithmetic and copies ran while one was open for 4% of the time, Pallas kernels for 0%

commit v1 on v0

v1 whole, which is shorter than its diff:
```python
import functools

import jax
import jax.numpy as jnp
from jax import lax
from jax.experimental import pallas as pl
from jax.experimental.pallas import tpu as pltpu
from jax.sharding import PartitionSpec as P

BLOCK = 128
F32 = jnp.float32
BF16 = jnp.bfloat16
ANY = pl.BlockSpec(memory_space=pl.ANY)


def params(mib):
    return pltpu.CompilerParams(dimension_semantics=("arbitrary",), vmem_limit_bytes=mib << 20)


def whole(shape):
    return pl.BlockSpec(shape, lambda *_: (0,) * len(shape))


def stencil_of(adjacency, segment):
    columns = jnp.broadcast_to(segment, (BLOCK, BLOCK))
    links = jnp.where(columns == columns.T, adjacency, 0).astype(F32)
    inverse = 1.0 / (jnp.sum(links, axis=1, keepdims=True) + 1.0)
    row = lax.broadcasted_iota(jnp.int32, (BLOCK, BLOCK), 0)
    column = lax.broadcasted_iota(jnp.int32, (BLOCK, BLOCK), 1)
    return (links + jnp.where(row == column, 2.0, 0.0)).astype(BF16), inverse


def aggregate_kernel(first, tile, features, adjacency, segments, out):
    step = pl.program_id(0)
    for b in range(tile // BLOCK):
        rows = pl.ds(b * BLOCK, BLOCK)
        index = first // BLOCK + step * (tile // BLOCK) + b
        stencil, inverse = stencil_of(adjacency[rows, :], segments[pl.ds(index, 1), :])
        summed = jnp.dot(stencil, features[rows, :], preferred_element_type=F32)
        out[rows, :] = (summed * inverse).astype(BF16)


def aggregate(features, adjacency, segments, first, size):
    width, tile = features.shape[1], min(size, 512)
    offset = first // tile
    return pl.pallas_call(
        functools.partial(aggregate_kernel, first, tile),
        grid=(size // tile,),
        in_specs=[
            pl.BlockSpec((tile, width), lambda i: (offset + i, 0)),
            pl.BlockSpec((tile, BLOCK), lambda i: (offset + i, 0)),
            whole(segments.shape),
        ],
        out_specs=pl.BlockSpec((tile, width), lambda i: (i, 0)),
        out_shape=jax.ShapeDtypeStruct((size, width), BF16),
        cost_estimate=pl.CostEstimate(
            flops=2 * size * BLOCK * width, bytes_accessed=size * (4 * width + 4 * BLOCK), transcendentals=0
        ),
        compiler_params=params(32),
    )(features, adjacency, segments)


def forward_kernel(n, start, tile, order, *refs):
    pieces, (weight, bias, cotangent) = refs[:n], refs[n : n + 3]
    if start:
        out, grad, total, total_bias = refs[n + 3 :]
        total_in = total_bias_in = None
    else:
        total_in, total_bias_in, _, out, grad, total, total_bias = refs[n + 3 :]
    width = weight.shape[1]

    @pl.when(pl.program_id(0) == 0)
    def _():
        total[...] = jnp.zeros_like(total) if start else total_in[...]
        total_bias[...] = jnp.zeros_like(total_bias) if start else total_bias_in[...]

    preact = None
    for p in range(n):
        rows = pl.ds(pl.multiple_of(order[p] * width, width), width)
        term = jnp.dot(pieces[p][...], weight[rows, :], preferred_element_type=F32)
        preact = term if preact is None else preact + term
    preact = preact + bias[...].astype(F32)
    out[...] = jnp.maximum(preact, 0.0).astype(BF16)
    grad_preact = jnp.where(preact > 0.0, cotangent[...].astype(F32), 0.0)
    total_bias[...] += jnp.sum(grad_preact.reshape(tile // 8, 8, width), axis=0)
    grad_preact = grad_preact.astype(BF16)
    grad[...] = grad_preact
    for p in range(n):
        rows = pl.ds(pl.multiple_of(order[p] * width, width), width)
        total[rows, :] += lax.dot_general(
            pieces[p][...], grad_preact, (((0,), (0,)), ((), ())), preferred_element_type=F32
        )


def forward(order, pieces, weight, bias, cotangent, carried, first):
    n, (size, width) = len(pieces), pieces[0].shape
    rows, depth = cotangent.shape[0], weight.shape[0]
    tile = min(size, 512)
    offset = first // tile
    start = carried is None
    small = lambda shape: pl.BlockSpec(shape, lambda i, order: (0,) * len(shape))
    here = pl.BlockSpec((tile, width), lambda i, order: (i, 0))
    there = pl.BlockSpec((tile, width), lambda i, order: (offset + i, 0))
    in_specs = [here] * n + [small((depth, width)), small((1, width)), there]
    operands = list(pieces) + [weight, bias, cotangent]
    aliases = {}
    if not start:
        in_specs += [small((depth, width)), small((8, width)), ANY]
        operands += list(carried)
        aliases = {n + 4: 2, n + 5: 3, n + 6: 0}
    out, grad, total, total_bias = pl.pallas_call(
        functools.partial(forward_kernel, n, start, tile),
        grid_spec=pltpu.PrefetchScalarGridSpec(
            num_scalar_prefetch=1,
            grid=(size // tile,),
            in_specs=in_specs,
            out_specs=[there, here, small((depth, width)), small((8, width))],
        ),
        out_shape=[
            jax.ShapeDtypeStruct((rows, width), BF16),
            jax.ShapeDtypeStruct((size, width), BF16),
            jax.ShapeDtypeStruct((depth, width), F32),
            jax.ShapeDtypeStruct((8, width), F32),
        ],
        input_output_aliases=aliases,
        cost_estimate=pl.CostEstimate(
            flops=4 * size * depth * width,
            bytes_accessed=size * (2 * depth + 6 * width) + depth * width * 10,
            transcendentals=0,
        ),
        compiler_params=params(44),
    )(order, *operands)
    return grad, (total, total_bias, out)


def backward_kernel(n, first, tile, *refs):
    grads, weights, (adjacency, segments), out = refs[:n], refs[n : 2 * n], refs[2 * n : 2 * n + 2], refs[-1]
    step = pl.program_id(0)
    grad = None
    for p in range(n):
        term = lax.dot_general(
            grads[p][...], weights[p][...], (((1,), (1,)), ((), ())), preferred_element_type=F32
        )
        grad = term if grad is None else grad + term
    grad = grad.astype(BF16)
    for b in range(tile // BLOCK):
        rows = pl.ds(b * BLOCK, BLOCK)
        index = first // BLOCK + step * (tile // BLOCK) + b
        stencil, inverse = stencil_of(adjacency[rows, :], segments[pl.ds(index, 1), :])
        summed = (grad[b * BLOCK : (b + 1) * BLOCK].astype(F32) * inverse).astype(BF16)
        out[rows, :] = jnp.dot(stencil, summed, preferred_element_type=F32)


def backward(grads, weights, adjacency, segments, carried, first):
    n, (size, width) = len(grads), grads[0].shape
    rows = adjacency.shape[0]
    tile = min(size, 512)
    offset = first // tile
    here = pl.BlockSpec((tile, width), lambda i: (i, 0))
    in_specs = (
        [here] * n
        + [whole(w.shape) for w in weights]
        + [pl.BlockSpec((tile, BLOCK), lambda i: (offset + i, 0)), whole(segments.shape)]
    )
    operands = list(grads) + list(weights) + [adjacency, segments]
    aliases = {}
    if carried is not None:
        in_specs.append(ANY)
        aliases = {len(operands): 0}
        operands.append(carried)
    return pl.pallas_call(
        functools.partial(backward_kernel, n, first, tile),
        grid=(size // tile,),
        in_specs=in_specs,
        out_specs=pl.BlockSpec((tile, width), lambda i: (offset + i, 0)),
        out_shape=jax.ShapeDtypeStruct((rows, width), F32),
        input_output_aliases=aliases,
        cost_estimate=pl.CostEstimate(
            flops=2 * size * width * (n * width + BLOCK),
            bytes_accessed=size * (2 * n * width + 4 * width + 4 * BLOCK) + n * width * width * 2,
            transcendentals=0,
        ),
        compiler_params=params(32),
    )(*operands)


def chunk_sizes(rows):
    sizes = [512] + [1024] * ((rows - 1024) // 1024) + [256, 256]
    return sizes if sum(sizes) == rows else [rows]


def build(n, clusters):
    outer = n // 2

    def device(chip, core):
        return (chip % outer) * 2 + core

    def from_chip(x, shift):
        pairs = [(device(chip + shift, core), device(chip, core)) for chip in range(outer) for core in range(2)]
        return lax.ppermute(x, "col", pairs)

    def from_sibling(x):
        return lax.ppermute(x, "col", [(i, i ^ 1) for i in range(n)])

    def after(x, *others):
        return lax.optimization_barrier((x,) + others)[0]

    def sum_clusters(x):
        if clusters & (clusters - 1):
            return lax.psum(x, "clu")
        step = 1
        while step < clusters:
            x = x + lax.ppermute(x, "clu", [(i, i ^ step) for i in range(clusters)])
            step *= 2
        return x

    def gather_weight(weight, order, width):
        me = lax.axis_index("col")
        chip, core = me // 2, me % 2
        mine = lambda c: lax.dynamic_slice_in_dim(weight, c * width, width, 0)
        blocks = [mine(me), from_sibling(mine(me ^ 1))]
        part = 2 * width // clusters
        for shift in range(1, outer):
            base = ((chip - shift + outer) % outer) * 2 * width + lax.axis_index("clu") * part
            piece = from_chip(lax.dynamic_slice_in_dim(weight, base, part, 0), shift)
            rows = lax.all_gather(piece, "clu", axis=0, tiled=True)
            own = lax.dynamic_slice_in_dim(rows, core * width, width, 0)
            other = lax.dynamic_slice_in_dim(rows, (1 - core) * width, width, 0)
            blocks += [own, from_sibling(other)]
        return blocks

    def local(features, weight, bias, adjacency, segments, cotangent):
        rows, width = features.shape
        me = lax.axis_index("col")
        chip, core = me // 2, me % 2
        order = jnp.stack(
            [((chip + p // 2) % outer) * 2 + (core if p % 2 == 0 else 1 - core) for p in range(n)]
        ).astype(jnp.int32)
        bias = bias.reshape(1, width)
        sizes = chunk_sizes(rows)
        starts = [sum(sizes[:k]) for k in range(len(sizes))]
        window = 3
        arrived = []

        def send(x):
            if len(arrived) >= window:
                x = after(x, *arrived[-window])
            got = [from_chip(x, shift) for shift in range(1, outer)]
            arrived.append(got)
            return got

        def spread(own, got):
            pieces = []
            for x in [own] + got:
                pieces += [x, from_sibling(x)]
            return pieces

        aggregated, received = [], []
        for first, size in zip(starts, sizes):
            aggregated.append(aggregate(features, adjacency, segments, first, size))
            received.append(send(aggregated[-1]))
        own_weights = gather_weight(weight, order, width)
        grads, carried = [], None
        for k, first in enumerate(starts):
            grad, carried = forward(
                order, spread(aggregated[k], received[k]), weight, bias, cotangent, carried, first
            )
            grads.append(grad)
        total, total_bias, out = carried
        grad_weight = lax.psum(total, "clu")
        grad_bias = sum_clusters(jnp.sum(total_bias, axis=0))
        grad_features = None
        received = [send(grad) for grad in grads]
        for k, first in enumerate(starts):
            grad_features = backward(
                spread(grads[k], received[k]), own_weights, adjacency, segments, grad_features, first
            )
        return (out, grad_features, grad_weight, grad_bias)

    return local


def solution(mesh):
    return jax.shard_map(
        build(mesh.shape["col"], mesh.shape["clu"]),
        mesh=mesh,
        in_specs=(
            P("clu", "col"),
            P(None, "col"),
            P("col"),
            P("clu", None),
            P("clu", None),
            P("clu", "col"),
        ),
        out_specs=(P("clu", "col"), P("clu", "col"), P(None, "col"), P("col")),
        check_vma=False,
    )
```

time: 916 us -> 474 us (0.52)
  waiting for transfers between devices: 754 us -> 218 us
  Pallas kernels: 0 us -> 142 us
  matrix products: 98.8 us -> 0 us
  local copies, waits for them, and re-layouts: 11 us -> 53.1 us
  starting transfers between devices: 0.52 us -> 39.1 us
  blocking collectives: 21.5 us -> 0 us
  other arithmetic: 16.2 us -> 0.68 us
    reduce_scatter x1 -> x0, waiting for transfers between devices: 404 us -> none  [local(): lax.psum_scatter(partials, 'col', scatter_dimension=1, tiled=True)]
    ppermute x0 -> x66, waiting for transfers between devices: none -> 218 us  [the longest x21 209 us: from_chip(): return lax.ppermute(x, 'col', pairs)]
    all_gather x1, waiting for transfers between devices: 204 us -> 0.01 us  [gather_weight(): rows = lax.all_gather(piece, 'clu', axis=0, tiled=True)]
    psum x1, waiting for transfers between devices: 146 us -> 0.01 us  [local(): grad_weight = lax.psum(total, 'clu')]
    pallas_call x0 -> x30, Pallas kernels: none -> 142 us  [the longest x10 90.4 us: forward(): pl.pallas_call(functools.partial(forward_kernel, n, start, tile), grid_sp...]
    dot_general x5 -> x0, matrix products: 98.8 us -> none  [the longest x1 29.1 us: local(): lax.dot_general(grad_preact, weight, (((1,), (1,)), ((), ())), preferred_...]
    unnamed x11 -> x105, local copies, waits for them, and re-layouts: 5.36 us -> 51.8 us
    ppermute x0 -> x66, starting transfers between devices: none -> 39 us  [the longest x21 24.9 us: from_chip(): return lax.ppermute(x, 'col', pairs)]
  transfers between devices with their start and end apart: 3 -> 68, of which waited for: 3 -> 18; matrix products, arithmetic and copies ran while one was open for 4% -> 0% of each run, Pallas kernels for 0% -> 30%
where the time goes in v1:
time: 474 us; the launch traced here: 467 us
  waiting for transfers between devices  218 us (46%)
  Pallas kernels  142 us (30%)
  local copies, waits for them, and re-layouts  53.1 us (11%)
  starting transfers between devices  39.1 us (8%)
  between operations  14.9 us (3%)
    ppermute x21, waiting for transfers between devices, from_chip(): return lax.ppermute(x, 'col', pairs)  209 us
    pallas_call x10, Pallas kernels, forward(): pl.pallas_call(functools.partial(forward_kernel, n, start, tile), grid_sp...  90.4 us
    unnamed x105, local copies, waits for them, and re-layouts  51.8 us
    pallas_call x10, Pallas kernels, backward(): pl.pallas_call(functools.partial(backward_kernel, n, first, tile), grid=(...  39.7 us
    ppermute x21, starting transfers between devices, from_chip(): return lax.ppermute(x, 'col', pairs)  24.9 us
    pallas_call x10, Pallas kernels, aggregate(): pl.pallas_call(functools.partial(aggregate_kernel, first, tile), grid=(si...  11.4 us
  transfers between devices with their start and end apart: 68, of which 18 were waited for; matrix products, arithmetic and copies ran while one was open for 0% of the time, Pallas kernels for 30%

profile of v1, /device:TPU:0, one launch (start us, length us, event | category | flops | bytes accessed | tf_op | source)
XLA Modules:
  0.0 466.8 jit_solution(15615760625985207511)
XLA Ops:
  7.2 2.2 copy-done
  9.4 3.4 copy-done.5
  13.9 3.0 collective-permute-start.1
  18.2 2.2 copy-done.1
  20.4 3.4 copy-done.6
  24.6 1.5 shard_map.102.refs_0_
  27.0 2.2 copy-done.2
  29.2 3.4 copy-done.7
  36.1 2.2 copy-done.3
  38.3 3.4 copy-done.8
  43.7 1.6 shard_map.95.refs_0_
  46.5 1.5 shard_map.101.refs_0_
  48.0 7.1 %collective-permute-done.12.refs_2_ = bf16[1024,512]{1,0:T(8,128)(2,1)} collective-permute-done((bf16[1024,512]{1,0:T(8,128)(2,1)}, bf16[1024,512]{1,0:T(8,128)(2,1)}, u32[]{:S(2)}, u32[]{:S(2)}) %collective-permute-start.12) | collective-permute-done | bytes 1048608 | tf_op jit(solution)/shard_map/ppermute | solution.py:200
  55.1 1.5 shard_map.98.refs_0_
  57.2 19.5 %collective-permute-done.7.refs_2_ = bf16[1024,512]{1,0:T(8,128)(2,1)} collective-permute-done((bf16[1024,512]{1,0:T(8,128)(2,1)S(1)}, bf16[1024,512]{1,0:T(8,128)(2,1)}, u32[]{:S(2)}, u32[]{:S(2)}) %collective-permute-start.7) | collective-permute-done | bytes 1048608 | tf_op jit(solution)/shard_map/ppermute | solution.py:200
  76.7 1.7 collective-permute-start.2
  78.5 1.5 shard_map.94.refs_0_
  80.0 1.5 shard_map.100.refs_0_
  84.5 1.7 collective-permute-start.8
  87.3 5.2 %shard_map.103 = (bf16[8192,512]{1,0:T(8,128)(2,1)}, bf16[512,512]{1,0:T(8,128)(2,1)}, f32[2048,512]{1,0:T(8,128)S(1)}, f32[8,512]{1,0:T(8,128)S(1)}) custom-call(s32[4]{0:T(128)S(1)} %pad_add_fusion.order, bf16[512,512]{1,0:T(8,128)(2,1)S(1)} %shard_map.96.refs_0_, bf16[512,512]{1,0:T(8,128)(2,1)} %collective-permute-done.28.refs_1_, ...), custom_call_target="tpu_custom_call" | custom-call | flops 2147483648 | bytes 14155776 | tf_op jit(solution)/shard_map/pallas_call | solution.py:111
  92.5 2.0 copy-done.9
  94.6 8.6 %collective-permute-done.2.refs_2_ = bf16[1024,512]{1,0:T(8,128)(2,1)} collective-permute-done((bf16[1024,512]{1,0:T(8,128)(2,1)}, bf16[1024,512]{1,0:T(8,128)(2,1)}, u32[]{:S(2)}, u32[]{:S(2)}) %collective-permute-start.2) | collective-permute-done | bytes 1048608 | tf_op jit(solution)/shard_map/ppermute | solution.py:200
  103.6 1.7 collective-permute-start.3
  106.8 18.8 %collective-permute-done.13.refs_2_ = bf16[1024,512]{1,0:T(8,128)(2,1)} collective-permute-done((bf16[1024,512]{1,0:T(8,128)(2,1)}, bf16[1024,512]{1,0:T(8,128)(2,1)}, u32[]{:S(2)}, u32[]{:S(2)}) %collective-permute-start.13) | collective-permute-done | bytes 1048608 | tf_op jit(solution)/shard_map/ppermute | solution.py:200
  125.6 22.5 %collective-permute-done.8.refs_2_ = bf16[1024,512]{1,0:T(8,128)(2,1)} collective-permute-done((bf16[1024,512]{1,0:T(8,128)(2,1)}, bf16[1024,512]{1,0:T(8,128)(2,1)}, u32[]{:S(2)}, u32[]{:S(2)}) %collective-permute-start.8) | collective-permute-done | bytes 1048608 | tf_op jit(solution)/shard_map/ppermute | solution.py:200
  148.1 1.7 collective-permute-start.14
  151.4 19.1 %collective-permute-done.3.refs_2_ = bf16[1024,512]{1,0:T(8,128)(2,1)} collective-permute-done((bf16[1024,512]{1,0:T(8,128)(2,1)}, bf16[1024,512]{1,0:T(8,128)(2,1)}, u32[]{:S(2)}, u32[]{:S(2)}) %collective-permute-start.3) | collective-permute-done | bytes 1048608 | tf_op jit(solution)/shard_map/ppermute | solution.py:200
  171.8 11.3 %shard_map.104 = (bf16[8192,512]{1,0:T(8,128)(2,1)}, bf16[1024,512]{1,0:T(8,128)(2,1)}, f32[2048,512]{1,0:T(8,128)}, f32[8,512]{1,0:T(8,128)S(1)}) custom-call(s32[4]{0:T(128)S(1)} %pad_add_fusion.order, bf16[1024,512]{1,0:T(8,128)(2,1)} %shard_map.102.refs_0_, ...), custom_call_target="tpu_custom_call", output_to_operand_aliasing={{2}: (8, {}), {3}: (9, {}), {0}: (10, {})} | custom-call | flops 4294967296 | bytes 17825792 | tf_op jit(solution)/shard_map/pallas_call | solution.py:111
  183.6 13.1 %collective-permute-done.9.refs_2_ = bf16[256,512]{1,0:T(8,128)(2,1)S(1)} collective-permute-done((bf16[256,512]{1,0:T(8,128)(2,1)S(1)}, bf16[256,512]{1,0:T(8,128)(2,1)S(1)}, u32[]{:S(2)}, u32[]{:S(2)}) %collective-permute-start.9) | collective-permute-done | bytes 262176 | tf_op jit(solution)/shard_map/ppermute | solution.py:200
  198.2 11.0 %shard_map.105 = (bf16[8192,512]{1,0:T(8,128)(2,1)}, bf16[1024,512]{1,0:T(8,128)(2,1)}, f32[2048,512]{1,0:T(8,128)}, f32[8,512]{1,0:T(8,128)S(1)}) custom-call(s32[4]{0:T(128)S(1)} %pad_add_fusion.order, bf16[1024,512]{1,0:T(8,128)(2,1)S(1)} %copy-done.21, ...), custom_call_target="tpu_custom_call", output_to_operand_aliasing={{2}: (8, {}), {3}: (9, {}), {0}: (10, {})} | custom-call | flops 4294967296 | bytes 17825792 | tf_op jit(solution)/shard_map/pallas_call | solution.py:111
  209.8 11.1 %shard_map.106 = (bf16[8192,512]{1,0:T(8,128)(2,1)}, bf16[1024,512]{1,0:T(8,128)(2,1)}, f32[2048,512]{1,0:T(8,128)}, f32[8,512]{1,0:T(8,128)S(1)}) custom-call(s32[4]{0:T(128)S(1)} %pad_add_fusion.order, bf16[1024,512]{1,0:T(8,128)(2,1)} %shard_map.95.refs_0_, ...), custom_call_target="tpu_custom_call", output_to_operand_aliasing={{2}: (8, {}), {3}: (9, {}), {0}: (10, {})} | custom-call | flops 4294967296 | bytes 17825792 | tf_op jit(solution)/shard_map/pallas_call | solution.py:111
  221.7 11.1 %shard_map.107 = (bf16[8192,512]{1,0:T(8,128)(2,1)}, bf16[1024,512]{1,0:T(8,128)(2,1)}, f32[2048,512]{1,0:T(8,128)}, f32[8,512]{1,0:T(8,128)S(1)}) custom-call(s32[4]{0:T(128)S(1)} %pad_add_fusion.order, bf16[1024,512]{1,0:T(8,128)(2,1)} %shard_map.101.refs_0_, ...), custom_call_target="tpu_custom_call", output_to_operand_aliasing={{2}: (8, {}), {3}: (9, {}), {0}: (10, {})} | custom-call | flops 4294967296 | bytes 17825792 | tf_op jit(solution)/shard_map/pallas_call | solution.py:111
  233.2 11.1 %shard_map.108 = (bf16[8192,512]{1,0:T(8,128)(2,1)}, bf16[1024,512]{1,0:T(8,128)(2,1)S(1)}, f32[2048,512]{1,0:T(8,128)}, f32[8,512]{1,0:T(8,128)S(1)}) custom-call(s32[4]{0:T(128)S(1)} %pad_add_fusion.order, bf16[1024,512]{1,0:T(8,128)(2,1)} %shard_map.98.refs_0_, ...), custom_call_target="tpu_custom_call", output_to_operand_aliasing={{2}: (8, {}), {3}: (9, {}), {0}: (10, {})} | custom-call | flops 4294967296 | bytes 17825792 | tf_op jit(solution)/shard_map/pallas_call | solution.py:111
  246.0 11.3 %shard_map.109 = (bf16[8192,512]{1,0:T(8,128)(2,1)}, bf16[1024,512]{1,0:T(8,128)(2,1)S(1)}, f32[2048,512]{1,0:T(8,128)}, f32[8,512]{1,0:T(8,128)S(1)}) custom-call(s32[4]{0:T(128)S(1)} %pad_add_fusion.order, bf16[1024,512]{1,0:T(8,128)(2,1)} %shard_map.94.refs_0_, ...), custom_call_target="tpu_custom_call", output_to_operand_aliasing={{2}: (8, {}), {3}: (9, {}), {0}: (10, {})} | custom-call | flops 4294967296 | bytes 17825792 | tf_op jit(solution)/shard_map/pallas_call | solution.py:111
  260.3 11.1 %shard_map.110 = (bf16[8192,512]{1,0:T(8,128)(2,1)}, bf16[1024,512]{1,0:T(8,128)(2,1)S(1)}, f32[2048,512]{1,0:T(8,128)}, f32[8,512]{1,0:T(8,128)S(1)}) custom-call(s32[4]{0:T(128)S(1)} %pad_add_fusion.order, bf16[1024,512]{1,0:T(8,128)(2,1)} %shard_map.100.refs_0_, ...), custom_call_target="tpu_custom_call", output_to_operand_aliasing={{2}: (8, {}), {3}: (9, {}), {0}: (10, {})} | custom-call | flops 4294967296 | bytes 17825792 | tf_op jit(solution)/shard_map/pallas_call | solution.py:111
  271.5 2.6 copy-done.10
  274.0 3.6 shard_map.111
  278.3 3.6 shard_map.112
  281.9 2.0 copy-done.11
  284.5 20.2 %collective-permute-done.31.refs_2_ = bf16[512,512]{1,0:T(8,128)(2,1)} collective-permute-done((bf16[512,512]{1,0:T(8,128)(2,1)}, bf16[512,512]{1,0:T(8,128)(2,1)}, u32[]{:S(2)}, u32[]{:S(2)}) %collective-permute-start.31) | collective-permute-done | bytes 524320 | tf_op jit(solution)/shard_map/ppermute | solution.py:200
  305.3 1.5 collective-permute-start.63
  306.8 2.2 collective-permute-done.63
  311.2 1.6 collective-permute-start.64
  312.8 2.2 collective-permute-done.64
  316.0 2.6 collective-permute-start.65
  318.6 2.2 collective-permute-done.65
  320.8 10.2 %collective-permute-done.32.refs_2_ = bf16[1024,512]{1,0:T(8,128)(2,1)} collective-permute-done((bf16[1024,512]{1,0:T(8,128)(2,1)}, bf16[1024,512]{1,0:T(8,128)(2,1)}, u32[]{:S(2)}, u32[]{:S(2)}) %collective-permute-start.32) | collective-permute-done | bytes 1048608 | tf_op jit(solution)/shard_map/ppermute | solution.py:200
  331.6 21.8 %collective-permute-done.46.refs_2_ = bf16[1024,512]{1,0:T(8,128)(2,1)S(1)} collective-permute-done((bf16[1024,512]{1,0:T(8,128)(2,1)}, bf16[1024,512]{1,0:T(8,128)(2,1)S(1)}, u32[]{:S(2)}, u32[]{:S(2)}) %collective-permute-start.46) | collective-permute-done | bytes 1048608 | tf_op jit(solution)/shard_map/ppermute | solution.py:200
  355.9 19.9 %collective-permute-done.41.refs_2_ = bf16[1024,512]{1,0:T(8,128)(2,1)S(1)} collective-permute-done((bf16[1024,512]{1,0:T(8,128)(2,1)}, bf16[1024,512]{1,0:T(8,128)(2,1)S(1)}, u32[]{:S(2)}, u32[]{:S(2)}) %collective-permute-start.41) | collective-permute-done | bytes 1048608 | tf_op jit(solution)/shard_map/ppermute | solution.py:200
  375.8 2.2 copy-done.4
  382.2 3.7 shard_map.113.refs_10_
  386.5 11.7 %collective-permute-done.33.refs_2_ = bf16[1024,512]{1,0:T(8,128)(2,1)S(1)} collective-permute-done((bf16[1024,512]{1,0:T(8,128)(2,1)}, bf16[1024,512]{1,0:T(8,128)(2,1)S(1)}, u32[]{:S(2)}, u32[]{:S(2)}) %collective-permute-start.33) | collective-permute-done | bytes 1048608 | tf_op jit(solution)/shard_map/ppermute | solution.py:200
  398.3 5.1 %shard_map.114.refs_10_ = f32[8192,512]{1,0:T(8,128)} custom-call(bf16[1024,512]{1,0:T(8,128)(2,1)} %get-tuple-element.113.refs_0_, bf16[1024,512]{1,0:T(8,128)(2,1)S(1)} %copy-done.29, bf16[1024,512]{1,0:T(8,128)(2,1)} %collective-permute-done.45.refs_2_, bf16[1024,512]{1,0:T(8,128)(2,1)S(1)} %collective-permute-done.60.refs_3_, ...), custom_call_target="tpu_custom_call", output_to_operand_aliasing={{}: (10, {})} | custom-call | flops 2281701376 | bytes 8912896 | tf_op jit(solution)/shard_map/pallas_call | solution.py:171
  403.4 16.9 %collective-permute-done.47.refs_2_ = bf16[1024,512]{1,0:T(8,128)(2,1)S(1)} collective-permute-done((bf16[1024,512]{1,0:T(8,128)(2,1)}, bf16[1024,512]{1,0:T(8,128)(2,1)S(1)}, u32[]{:S(2)}, u32[]{:S(2)}) %collective-permute-start.47) | collective-permute-done | bytes 1048608 | tf_op jit(solution)/shard_map/ppermute | solution.py:200
  420.9 5.4 %shard_map.115.refs_10_ = f32[8192,512]{1,0:T(8,128)} custom-call(bf16[1024,512]{1,0:T(8,128)(2,1)} %get-tuple-element.107.refs_0_, bf16[1024,512]{1,0:T(8,128)(2,1)S(1)} %copy-done.23, bf16[1024,512]{1,0:T(8,128)(2,1)} %collective-permute-done.40.refs_2_, bf16[1024,512]{1,0:T(8,128)(2,1)S(1)} %collective-permute-done.58.refs_3_, ...), custom_call_target="tpu_custom_call", output_to_operand_aliasing={{}: (10, {})} | custom-call | flops 2281701376 | bytes 8912896 | tf_op jit(solution)/shard_map/pallas_call | solution.py:171
  426.2 5.3 %shard_map.116.refs_10_ = f32[8192,512]{1,0:T(8,128)} custom-call(bf16[1024,512]{1,0:T(8,128)(2,1)} %get-tuple-element.101.refs_0_, bf16[1024,512]{1,0:T(8,128)(2,1)} %collective-permute-done.55.refs_1_, bf16[1024,512]{1,0:T(8,128)(2,1)} %collective-permute-done.32.refs_2_, ...), custom_call_target="tpu_custom_call", output_to_operand_aliasing={{}: (10, {})} | custom-call | flops 2281701376 | bytes 8912896 | tf_op jit(solution)/shard_map/pallas_call | solution.py:171
  432.2 5.1 %shard_map.117.refs_10_ = f32[8192,512]{1,0:T(8,128)} custom-call(bf16[1024,512]{1,0:T(8,128)(2,1)} %get-tuple-element.114.refs_0_, bf16[1024,512]{1,0:T(8,128)(2,1)} %collective-permute-done.53.refs_1_, bf16[1024,512]{1,0:T(8,128)(2,1)S(1)} %collective-permute-done.46.refs_2_, ...), custom_call_target="tpu_custom_call", output_to_operand_aliasing={{}: (10, {})} | custom-call | flops 2281701376 | bytes 8912896 | tf_op jit(solution)/shard_map/pallas_call | solution.py:171
  437.3 1.5 collective-permute-start.34
  438.8 3.9 shard_map.118.refs_10_
  443.2 3.9 shard_map.119.refs_10_
  447.6 3.9 shard_map.120.refs_10_
  451.5 1.7 shard_map.121.refs_10_
  453.2 1.7 shard_map.122
  454.9 4.6 copy.83
  (218 shorter events, 44.1 us)
Async XLA Ops:
  7.2 142.6 %all-gather.2.cloned.1.call-start = ((), (), s32[]{:S(2)}) async-start(), calls=%async_computation | async-start | bytes 1179648 | tf_op jit(solution)/shard_map/all_gather | solution.py:226
  13.9 21.0 %collective-permute-start.1 = (bf16[512,512]{1,0:T(8,128)(2,1)S(1)}, bf16[512,512]{1,0:T(8,128)(2,1)}, u32[]{:S(2)}, u32[]{:S(2)}) collective-permute-start(bf16[512,512]{1,0:T(8,128)(2,1)S(1)} %shard_map.96.refs_0_), channel_id=1, source_target_pairs={{2,0},{3,1},{0,2},{1,3},{6,4},{7,5},{4,6},{5,7},{10,8},{11,9},{8,1... | collective-permute-start | bytes 1572872 | tf_op jit(solution)/shard_map/ppermute | solution.py:200
  17.0 16.6 %collective-permute-start.37 = (bf16[128,512]{1,0:T(8,128)(2,1)S(1)}, bf16[128,512]{1,0:T(8,128)(2,1)S(1)}, u32[]{:S(2)}, u32[]{:S(2)}) collective-permute-start(bf16[128,512]{1,0:T(8,128)(2,1)S(1)} %constant_dynamic-slice_fusion.2), channel_id=1, source_target_pairs={{2,0},{3,1},{0,2},{1,3},{6,4},{7,5},{4,6},{5,7},{10,8},{11,9},{8,1... | collective-permute-start | bytes 393224 | tf_op jit(solution)/shard_map/ppermute | solution.py:200
  24.0 10.3 %collective-permute-start.6 = (bf16[256,512]{1,0:T(8,128)(2,1)S(1)}, bf16[256,512]{1,0:T(8,128)(2,1)}, u32[]{:S(2)}, u32[]{:S(2)}) collective-permute-start(bf16[256,512]{1,0:T(8,128)(2,1)S(1)} %shard_map.97.refs_0_), channel_id=1, source_target_pairs={{0,1},{1,0},{2,3},{3,2},{4,5},{5,4},{6,7},{7,6},{8,9},{9,8},{10,11... | collective-permute-start | bytes 786440 | tf_op jit(solution)/shard_map/ppermute | solution.py:203
  24.1 18.3 %collective-permute-start.28 = (bf16[512,512]{1,0:T(8,128)(2,1)S(1)}, bf16[512,512]{1,0:T(8,128)(2,1)}, u32[]{:S(2)}, u32[]{:S(2)}) collective-permute-start(bf16[512,512]{1,0:T(8,128)(2,1)S(1)} %shard_map.96.refs_0_), channel_id=1, source_target_pairs={{0,1},{1,0},{2,3},{3,2},{4,5},{5,4},{6,7},{7,6},{8,9},{9,8},{10,11... | collective-permute-start | bytes 1572872 | tf_op jit(solution)/shard_map/ppermute | solution.py:203
  26.1 28.9 %collective-permute-start.12 = (bf16[1024,512]{1,0:T(8,128)(2,1)}, bf16[1024,512]{1,0:T(8,128)(2,1)}, u32[]{:S(2)}, u32[]{:S(2)}) collective-permute-start(bf16[1024,512]{1,0:T(8,128)(2,1)} %shard_map.102.refs_0_), channel_id=1, source_target_pairs={{2,0},{3,1},{0,2},{1,3},{6,4},{7,5},{4,6},{5,7},{10,8},{11,9},{8,1... | collective-permute-start | bytes 3145736 | tf_op jit(solution)/shard_map/ppermute | solution.py:200
  34.3 10.9 %collective-permute-start.36 = (bf16[512,512]{1,0:T(8,128)(2,1)S(1)}, bf16[512,512]{1,0:T(8,128)(2,1)S(1)}, u32[]{:S(2)}, u32[]{:S(2)}) collective-permute-start(bf16[512,512]{1,0:T(8,128)(2,1)S(1)} %get-tuple-element.118), channel_id=1, source_target_pairs={{0,1},{1,0},{2,3},{3,2},{4,5},{5,4},{6,7},{7,6},{8,9},{9,8},{10,11... | collective-permute-start | bytes 1572872 | tf_op jit(solution)/shard_map/ppermute | solution.py:203
  34.9 10.4 %collective-permute-start.29 = (bf16[512,512]{1,0:T(8,128)(2,1)}, bf16[512,512]{1,0:T(8,128)(2,1)S(1)}, u32[]{:S(2)}, u32[]{:S(2)}) collective-permute-start(bf16[512,512]{1,0:T(8,128)(2,1)} %collective-permute-done.1.refs_2_), channel_id=1, source_target_pairs={{0,1},{1,0},{2,3},{3,2},{4,5},{5,4},{6,7},{7,6},{8,9},{9,8},{10,11... | collective-permute-start | bytes 1572872 | tf_op jit(solution)/shard_map/ppermute | solution.py:203
  36.0 20.6 %collective-permute-start.26 = (bf16[1024,512]{1,0:T(8,128)(2,1)}, bf16[1024,512]{1,0:T(8,128)(2,1)S(1)}, u32[]{:S(2)}, u32[]{:S(2)}) collective-permute-start(bf16[1024,512]{1,0:T(8,128)(2,1)} %shard_map.102.refs_0_), channel_id=1, source_target_pairs={{0,1},{1,0},{2,3},{3,2},{4,5},{5,4},{6,7},{7,6},{8,9},{9,8},{10,11... | collective-permute-start | bytes 3145736 | tf_op jit(solution)/shard_map/ppermute | solution.py:203
  42.4 34.3 %collective-permute-start.7 = (bf16[1024,512]{1,0:T(8,128)(2,1)S(1)}, bf16[1024,512]{1,0:T(8,128)(2,1)}, u32[]{:S(2)}, u32[]{:S(2)}) collective-permute-start(bf16[1024,512]{1,0:T(8,128)(2,1)S(1)} %shard_map.99.refs_0_), channel_id=1, source_target_pairs={{2,0},{3,1},{0,2},{1,3},{6,4},{7,5},{4,6},{5,7},{10,8},{11,9},{8,1... | collective-permute-start | bytes 3145736 | tf_op jit(solution)/shard_map/ppermute | solution.py:200
  45.2 36.3 %collective-permute-start.24 = (bf16[1024,512]{1,0:T(8,128)(2,1)S(1)}, bf16[1024,512]{1,0:T(8,128)(2,1)S(1)}, u32[]{:S(2)}, u32[]{:S(2)}) collective-permute-start(bf16[1024,512]{1,0:T(8,128)(2,1)S(1)} %shard_map.99.refs_0_), channel_id=1, source_target_pairs={{0,1},{1,0},{2,3},{3,2},{4,5},{5,4},{6,7},{7,6},{8,9},{9,8},{10,11... | collective-permute-start | bytes 3145736 | tf_op jit(solution)/shard_map/ppermute | solution.py:203
  46.2 36.3 %collective-permute-start.22 = (bf16[1024,512]{1,0:T(8,128)(2,1)}, bf16[1024,512]{1,0:T(8,128)(2,1)S(1)}, u32[]{:S(2)}, u32[]{:S(2)}) collective-permute-start(bf16[1024,512]{1,0:T(8,128)(2,1)} %shard_map.95.refs_0_), channel_id=1, source_target_pairs={{0,1},{1,0},{2,3},{3,2},{4,5},{5,4},{6,7},{7,6},{8,9},{9,8},{10,11... | collective-permute-start | bytes 3145736 | tf_op jit(solution)/shard_map/ppermute | solution.py:203
  55.1 29.0 %collective-permute-start.20 = (bf16[1024,512]{1,0:T(8,128)(2,1)}, bf16[1024,512]{1,0:T(8,128)(2,1)}, u32[]{:S(2)}, u32[]{:S(2)}) collective-permute-start(bf16[1024,512]{1,0:T(8,128)(2,1)} %shard_map.101.refs_0_), channel_id=1, source_target_pairs={{0,1},{1,0},{2,3},{3,2},{4,5},{5,4},{6,7},{7,6},{8,9},{9,8},{10,11... | collective-permute-start | bytes 3145736 | tf_op jit(solution)/shard_map/ppermute | solution.py:203
  56.6 27.9 %collective-permute-start.18 = (bf16[1024,512]{1,0:T(8,128)(2,1)}, bf16[1024,512]{1,0:T(8,128)(2,1)}, u32[]{:S(2)}, u32[]{:S(2)}) collective-permute-start(bf16[1024,512]{1,0:T(8,128)(2,1)} %shard_map.98.refs_0_), channel_id=1, source_target_pairs={{0,1},{1,0},{2,3},{3,2},{4,5},{5,4},{6,7},{7,6},{8,9},{9,8},{10,11... | collective-permute-start | bytes 3145736 | tf_op jit(solution)/shard_map/ppermute | solution.py:203
  76.7 26.4 %collective-permute-start.2 = (bf16[1024,512]{1,0:T(8,128)(2,1)}, bf16[1024,512]{1,0:T(8,128)(2,1)}, u32[]{:S(2)}, u32[]{:S(2)}) collective-permute-start(bf16[1024,512]{1,0:T(8,128)(2,1)} %shard_map.95.refs_0_), channel_id=1, source_target_pairs={{2,0},{3,1},{0,2},{1,3},{6,4},{7,5},{4,6},{5,7},{10,8},{11,9},{8,1... | collective-permute-start | bytes 3145736 | tf_op jit(solution)/shard_map/ppermute | solution.py:200
  82.5 20.6 %collective-permute-start.16 = (bf16[1024,512]{1,0:T(8,128)(2,1)}, bf16[1024,512]{1,0:T(8,128)(2,1)}, u32[]{:S(2)}, u32[]{:S(2)}) collective-permute-start(bf16[1024,512]{1,0:T(8,128)(2,1)} %shard_map.94.refs_0_), channel_id=1, source_target_pairs={{0,1},{1,0},{2,3},{3,2},{4,5},{5,4},{6,7},{7,6},{8,9},{9,8},{10,11... | collective-permute-start | bytes 3145736 | tf_op jit(solution)/shard_map/ppermute | solution.py:203
  83.5 20.2 %collective-permute-start.11 = (bf16[1024,512]{1,0:T(8,128)(2,1)}, bf16[1024,512]{1,0:T(8,128)(2,1)}, u32[]{:S(2)}, u32[]{:S(2)}) collective-permute-start(bf16[1024,512]{1,0:T(8,128)(2,1)} %shard_map.100.refs_0_), channel_id=1, source_target_pairs={{0,1},{1,0},{2,3},{3,2},{4,5},{5,4},{6,7},{7,6},{8,9},{9,8},{10,11... | collective-permute-start | bytes 3145736 | tf_op jit(solution)/shard_map/ppermute | solution.py:203
  84.0 370.9 %all-reduce.2.cloned.1.call-start = ((), (), s32[]{:S(2)}) async-start(), calls=%async_computation.1 | async-start | bytes 8388608 | tf_op jit(solution)/shard_map/psum | solution.py:270
  84.1 41.5 %collective-permute-start.13 = (bf16[1024,512]{1,0:T(8,128)(2,1)}, bf16[1024,512]{1,0:T(8,128)(2,1)}, u32[]{:S(2)}, u32[]{:S(2)}) collective-permute-start(bf16[1024,512]{1,0:T(8,128)(2,1)} %shard_map.101.refs_0_), channel_id=1, source_target_pairs={{2,0},{3,1},{0,2},{1,3},{6,4},{7,5},{4,6},{5,7},{10,8},{11,9},{8,1... | collective-permute-start | bytes 3145736 | tf_op jit(solution)/shard_map/ppermute | solution.py:200
  84.5 63.6 %collective-permute-start.8 = (bf16[1024,512]{1,0:T(8,128)(2,1)}, bf16[1024,512]{1,0:T(8,128)(2,1)}, u32[]{:S(2)}, u32[]{:S(2)}) collective-permute-start(bf16[1024,512]{1,0:T(8,128)(2,1)} %shard_map.98.refs_0_), channel_id=1, source_target_pairs={{2,0},{3,1},{0,2},{1,3},{6,4},{7,5},{4,6},{5,7},{10,8},{11,9},{8,1... | collective-permute-start | bytes 3145736 | tf_op jit(solution)/shard_map/ppermute | solution.py:200
  103.1 48.0 %collective-permute-start.27 = (bf16[1024,512]{1,0:T(8,128)(2,1)}, bf16[1024,512]{1,0:T(8,128)(2,1)}, u32[]{:S(2)}, u32[]{:S(2)}) collective-permute-start(bf16[1024,512]{1,0:T(8,128)(2,1)} %collective-permute-done.12.refs_2_), channel_id=1, source_target_pairs={{0,1},{1,0},{2,3},{3,2},{4,5},{5,4},{6,7},{7,6},{8,9},{9,8},{10,11... | collective-permute-start | bytes 3145736 | tf_op jit(solution)/shard_map/ppermute | solution.py:203
  103.6 66.9 %collective-permute-start.3 = (bf16[1024,512]{1,0:T(8,128)(2,1)}, bf16[1024,512]{1,0:T(8,128)(2,1)}, u32[]{:S(2)}, u32[]{:S(2)}) collective-permute-start(bf16[1024,512]{1,0:T(8,128)(2,1)} %shard_map.94.refs_0_), channel_id=1, source_target_pairs={{2,0},{3,1},{0,2},{1,3},{6,4},{7,5},{4,6},{5,7},{10,8},{11,9},{8,1... | collective-permute-start | bytes 3145736 | tf_op jit(solution)/shard_map/ppermute | solution.py:200
  106.7 76.4 %collective-permute-start.25 = (bf16[1024,512]{1,0:T(8,128)(2,1)}, bf16[1024,512]{1,0:T(8,128)(2,1)}, u32[]{:S(2)}, u32[]{:S(2)}) collective-permute-start(bf16[1024,512]{1,0:T(8,128)(2,1)} %collective-permute-done.7.refs_2_), channel_id=1, source_target_pairs={{0,1},{1,0},{2,3},{3,2},{4,5},{5,4},{6,7},{7,6},{8,9},{9,8},{10,11... | collective-permute-start | bytes 3145736 | tf_op jit(solution)/shard_map/ppermute | solution.py:203
  125.6 71.2 %collective-permute-start.23 = (bf16[1024,512]{1,0:T(8,128)(2,1)}, bf16[1024,512]{1,0:T(8,128)(2,1)}, u32[]{:S(2)}, u32[]{:S(2)}) collective-permute-start(bf16[1024,512]{1,0:T(8,128)(2,1)} %collective-permute-done.2.refs_2_), channel_id=1, source_target_pairs={{0,1},{1,0},{2,3},{3,2},{4,5},{5,4},{6,7},{7,6},{8,9},{9,8},{10,11... | collective-permute-start | bytes 3145736 | tf_op jit(solution)/shard_map/ppermute | solution.py:203
  148.1 61.4 %collective-permute-start.14 = (bf16[1024,512]{1,0:T(8,128)(2,1)}, bf16[1024,512]{1,0:T(8,128)(2,1)}, u32[]{:S(2)}, u32[]{:S(2)}) collective-permute-start(bf16[1024,512]{1,0:T(8,128)(2,1)} %shard_map.100.refs_0_), channel_id=1, source_target_pairs={{2,0},{3,1},{0,2},{1,3},{6,4},{7,5},{4,6},{5,7},{10,8},{11,9},{8,1... | collective-permute-start | bytes 3145736 | tf_op jit(solution)/shard_map/ppermute | solution.py:200
  151.1 45.7 %collective-permute-start.9 = (bf16[256,512]{1,0:T(8,128)(2,1)S(1)}, bf16[256,512]{1,0:T(8,128)(2,1)S(1)}, u32[]{:S(2)}, u32[]{:S(2)}) collective-permute-start(bf16[256,512]{1,0:T(8,128)(2,1)S(1)} %shard_map.97.refs_0_), channel_id=1, source_target_pairs={{2,0},{3,1},{0,2},{1,3},{6,4},{7,5},{4,6},{5,7},{10,8},{11,9},{8,1... | collective-permute-start | bytes 786440 | tf_op jit(solution)/shard_map/ppermute | solution.py:200
  170.5 50.9 %collective-permute-start.21 = (bf16[1024,512]{1,0:T(8,128)(2,1)}, bf16[1024,512]{1,0:T(8,128)(2,1)S(1)}, u32[]{:S(2)}, u32[]{:S(2)}) collective-permute-start(bf16[1024,512]{1,0:T(8,128)(2,1)} %collective-permute-done.13.refs_2_), channel_id=1, source_target_pairs={{0,1},{1,0},{2,3},{3,2},{4,5},{5,4},{6,7},{7,6},{8,9},{9,8},{10,11... | collective-permute-start | bytes 3145736 | tf_op jit(solution)/shard_map/ppermute | solution.py:203
  183.1 37.8 %collective-permute-start.38 = (bf16[512,512]{1,0:T(8,128)(2,1)S(1)}, bf16[512,512]{1,0:T(8,128)(2,1)S(1)}, u32[]{:S(2)}, u32[]{:S(2)}) collective-permute-start(bf16[512,512]{1,0:T(8,128)(2,1)S(1)} %get-tuple-element.120), channel_id=1, source_target_pairs={{0,1},{1,0},{2,3},{3,2},{4,5},{5,4},{6,7},{7,6},{8,9},{9,8},{10,11... | collective-permute-start | bytes 1572872 | tf_op jit(solution)/shard_map/ppermute | solution.py:203
  196.8 36.1 %collective-permute-start.19 = (bf16[1024,512]{1,0:T(8,128)(2,1)}, bf16[1024,512]{1,0:T(8,128)(2,1)S(1)}, u32[]{:S(2)}, u32[]{:S(2)}) collective-permute-start(bf16[1024,512]{1,0:T(8,128)(2,1)} %collective-permute-done.8.refs_2_), channel_id=1, source_target_pairs={{0,1},{1,0},{2,3},{3,2},{4,5},{5,4},{6,7},{7,6},{8,9},{9,8},{10,11... | collective-permute-start | bytes 3145736 | tf_op jit(solution)/shard_map/ppermute | solution.py:203
  196.8 12.4 %collective-permute-start.4 = (bf16[256,512]{1,0:T(8,128)(2,1)}, bf16[256,512]{1,0:T(8,128)(2,1)S(1)}, u32[]{:S(2)}, u32[]{:S(2)}) collective-permute-start(bf16[256,512]{1,0:T(8,128)(2,1)} %shard_map.93.refs_0_), channel_id=1, source_target_pairs={{2,0},{3,1},{0,2},{1,3},{6,4},{7,5},{4,6},{5,7},{10,8},{11,9},{8,1... | collective-permute-start | bytes 786440 | tf_op jit(solution)/shard_map/ppermute | solution.py:200
  209.2 12.0 %collective-permute-start.10 = (bf16[256,512]{1,0:T(8,128)(2,1)S(1)}, bf16[256,512]{1,0:T(8,128)(2,1)S(1)}, u32[]{:S(2)}, u32[]{:S(2)}) collective-permute-start(bf16[256,512]{1,0:T(8,128)(2,1)S(1)} %collective-permute-done.9.refs_2_), channel_id=1, source_target_pairs={{0,1},{1,0},{2,3},{3,2},{4,5},{5,4},{6,7},{7,6},{8,9},{9,8},{10,11... | collective-permute-start | bytes 786440 | tf_op jit(solution)/shard_map/ppermute | solution.py:203
  209.5 36.5 %collective-permute-start.17 = (bf16[1024,512]{1,0:T(8,128)(2,1)}, bf16[1024,512]{1,0:T(8,128)(2,1)S(1)}, u32[]{:S(2)}, u32[]{:S(2)}) collective-permute-start(bf16[1024,512]{1,0:T(8,128)(2,1)} %collective-permute-done.3.refs_2_), channel_id=1, source_target_pairs={{0,1},{1,0},{2,3},{3,2},{4,5},{5,4},{6,7},{7,6},{8,9},{9,8},{10,11... | collective-permute-start | bytes 3145736 | tf_op jit(solution)/shard_map/ppermute | solution.py:203
  220.9 37.4 %collective-permute-start.59 = (bf16[1024,512]{1,0:T(8,128)(2,1)}, bf16[1024,512]{1,0:T(8,128)(2,1)S(1)}, u32[]{:S(2)}, u32[]{:S(2)}) collective-permute-start(bf16[1024,512]{1,0:T(8,128)(2,1)} %get-tuple-element.113.refs_0_), channel_id=1, source_target_pairs={{0,1},{1,0},{2,3},{3,2},{4,5},{5,4},{6,7},{7,6},{8,9},{9,8},{10,11... | collective-permute-start | bytes 3145736 | tf_op jit(solution)/shard_map/ppermute | solution.py:203
  221.2 38.5 %collective-permute-start.57 = (bf16[1024,512]{1,0:T(8,128)(2,1)}, bf16[1024,512]{1,0:T(8,128)(2,1)S(1)}, u32[]{:S(2)}, u32[]{:S(2)}) collective-permute-start(bf16[1024,512]{1,0:T(8,128)(2,1)} %get-tuple-element.107.refs_0_), channel_id=1, source_target_pairs={{0,1},{1,0},{2,3},{3,2},{4,5},{5,4},{6,7},{7,6},{8,9},{9,8},{10,11... | collective-permute-start | bytes 3145736 | tf_op jit(solution)/shard_map/ppermute | solution.py:203
  221.5 38.8 %collective-permute-start.15 = (bf16[1024,512]{1,0:T(8,128)(2,1)}, bf16[1024,512]{1,0:T(8,128)(2,1)S(1)}, u32[]{:S(2)}, u32[]{:S(2)}) collective-permute-start(bf16[1024,512]{1,0:T(8,128)(2,1)} %collective-permute-done.14.refs_2_), channel_id=1, source_target_pairs={{0,1},{1,0},{2,3},{3,2},{4,5},{5,4},{6,7},{7,6},{8,9},{9,8},{10,11... | collective-permute-start | bytes 3145736 | tf_op jit(solution)/shard_map/ppermute | solution.py:203
  232.8 12.5 %collective-permute-start.5 = (bf16[256,512]{1,0:T(8,128)(2,1)S(1)}, bf16[256,512]{1,0:T(8,128)(2,1)S(1)}, u32[]{:S(2)}, u32[]{:S(2)}) collective-permute-start(bf16[256,512]{1,0:T(8,128)(2,1)S(1)} %collective-permute-done.4.refs_2_), channel_id=1, source_target_pairs={{0,1},{1,0},{2,3},{3,2},{4,5},{5,4},{6,7},{7,6},{8,9},{9,8},{10,11... | collective-permute-start | bytes 786440 | tf_op jit(solution)/shard_map/ppermute | solution.py:203
  245.4 38.5 %collective-permute-start.45 = (bf16[1024,512]{1,0:T(8,128)(2,1)}, bf16[1024,512]{1,0:T(8,128)(2,1)}, u32[]{:S(2)}, u32[]{:S(2)}) collective-permute-start(bf16[1024,512]{1,0:T(8,128)(2,1)} %get-tuple-element.113.refs_0_), channel_id=1, source_target_pairs={{2,0},{3,1},{0,2},{1,3},{6,4},{7,5},{4,6},{5,7},{10,8},{11,9},{8,1... | collective-permute-start | bytes 3145736 | tf_op jit(solution)/shard_map/ppermute | solution.py:200
  246.0 58.7 %collective-permute-start.55 = (bf16[1024,512]{1,0:T(8,128)(2,1)}, bf16[1024,512]{1,0:T(8,128)(2,1)}, u32[]{:S(2)}, u32[]{:S(2)}) collective-permute-start(bf16[1024,512]{1,0:T(8,128)(2,1)} %get-tuple-element.101.refs_0_), channel_id=1, source_target_pairs={{0,1},{1,0},{2,3},{3,2},{4,5},{5,4},{6,7},{7,6},{8,9},{9,8},{10,11... | collective-permute-start | bytes 3145736 | tf_op jit(solution)/shard_map/ppermute | solution.py:203
  258.3 47.0 %collective-permute-start.40 = (bf16[1024,512]{1,0:T(8,128)(2,1)}, bf16[1024,512]{1,0:T(8,128)(2,1)}, u32[]{:S(2)}, u32[]{:S(2)}) collective-permute-start(bf16[1024,512]{1,0:T(8,128)(2,1)} %get-tuple-element.107.refs_0_), channel_id=1, source_target_pairs={{2,0},{3,1},{0,2},{1,3},{6,4},{7,5},{4,6},{5,7},{10,8},{11,9},{8,1... | collective-permute-start | bytes 3145736 | tf_op jit(solution)/shard_map/ppermute | solution.py:200
  259.7 45.0 %collective-permute-start.31 = (bf16[512,512]{1,0:T(8,128)(2,1)}, bf16[512,512]{1,0:T(8,128)(2,1)}, u32[]{:S(2)}, u32[]{:S(2)}) collective-permute-start(bf16[512,512]{1,0:T(8,128)(2,1)} %get-tuple-element.100.refs_0_), channel_id=1, source_target_pairs={{2,0},{3,1},{0,2},{1,3},{6,4},{7,5},{4,6},{5,7},{10,8},{11,9},{8,1... | collective-permute-start | bytes 1572872 | tf_op jit(solution)/shard_map/ppermute | solution.py:200
  260.3 52.5 %collective-permute-start.53 = (bf16[1024,512]{1,0:T(8,128)(2,1)}, bf16[1024,512]{1,0:T(8,128)(2,1)}, u32[]{:S(2)}, u32[]{:S(2)}) collective-permute-start(bf16[1024,512]{1,0:T(8,128)(2,1)} %get-tuple-element.114.refs_0_), channel_id=1, source_target_pairs={{0,1},{1,0},{2,3},{3,2},{4,5},{5,4},{6,7},{7,6},{8,9},{9,8},{10,11... | collective-permute-start | bytes 3145736 | tf_op jit(solution)/shard_map/ppermute | solution.py:203
  283.9 31.1 %collective-permute-start.51 = (bf16[1024,512]{1,0:T(8,128)(2,1)}, bf16[1024,512]{1,0:T(8,128)(2,1)S(1)}, u32[]{:S(2)}, u32[]{:S(2)}) collective-permute-start(bf16[1024,512]{1,0:T(8,128)(2,1)} %copy-done.24), channel_id=1, source_target_pairs={{0,1},{1,0},{2,3},{3,2},{4,5},{5,4},{6,7},{7,6},{8,9},{9,8},{10,11... | collective-permute-start | bytes 3145736 | tf_op jit(solution)/shard_map/ppermute | solution.py:203
  304.7 5.7 %collective-permute-start.62 = (bf16[512,512]{1,0:T(8,128)(2,1)}, bf16[512,512]{1,0:T(8,128)(2,1)S(1)}, u32[]{:S(2)}, u32[]{:S(2)}) collective-permute-start(bf16[512,512]{1,0:T(8,128)(2,1)} %collective-permute-done.31.refs_2_), channel_id=1, source_target_pairs={{0,1},{1,0},{2,3},{3,2},{4,5},{5,4},{6,7},{7,6},{8,9},{9,8},{10,11... | collective-permute-start | bytes 1572872 | tf_op jit(solution)/shard_map/ppermute | solution.py:203
  304.7 26.3 %collective-permute-start.32 = (bf16[1024,512]{1,0:T(8,128)(2,1)}, bf16[1024,512]{1,0:T(8,128)(2,1)}, u32[]{:S(2)}, u32[]{:S(2)}) collective-permute-start(bf16[1024,512]{1,0:T(8,128)(2,1)} %get-tuple-element.101.refs_0_), channel_id=1, source_target_pairs={{2,0},{3,1},{0,2},{1,3},{6,4},{7,5},{4,6},{5,7},{10,8},{11,9},{8,1... | collective-permute-start | bytes 3145736 | tf_op jit(solution)/shard_map/ppermute | solution.py:200
  309.0 44.4 %collective-permute-start.46 = (bf16[1024,512]{1,0:T(8,128)(2,1)}, bf16[1024,512]{1,0:T(8,128)(2,1)S(1)}, u32[]{:S(2)}, u32[]{:S(2)}) collective-permute-start(bf16[1024,512]{1,0:T(8,128)(2,1)} %get-tuple-element.114.refs_0_), channel_id=1, source_target_pairs={{2,0},{3,1},{0,2},{1,3},{6,4},{7,5},{4,6},{5,7},{10,8},{11,9},{8,1... | collective-permute-start | bytes 3145736 | tf_op jit(solution)/shard_map/ppermute | solution.py:200
  312.8 41.2 %collective-permute-start.60 = (bf16[1024,512]{1,0:T(8,128)(2,1)}, bf16[1024,512]{1,0:T(8,128)(2,1)S(1)}, u32[]{:S(2)}, u32[]{:S(2)}) collective-permute-start(bf16[1024,512]{1,0:T(8,128)(2,1)} %collective-permute-done.45.refs_2_), channel_id=1, source_target_pairs={{0,1},{1,0},{2,3},{3,2},{4,5},{5,4},{6,7},{7,6},{8,9},{9,8},{10,11... | collective-permute-start | bytes 3145736 | tf_op jit(solution)/shard_map/ppermute | solution.py:203
  315.0 40.4 %collective-permute-start.49 = (bf16[1024,512]{1,0:T(8,128)(2,1)}, bf16[1024,512]{1,0:T(8,128)(2,1)S(1)}, u32[]{:S(2)}, u32[]{:S(2)}) collective-permute-start(bf16[1024,512]{1,0:T(8,128)(2,1)} %copy-done.26), channel_id=1, source_target_pairs={{0,1},{1,0},{2,3},{3,2},{4,5},{5,4},{6,7},{7,6},{8,9},{9,8},{10,11... | collective-permute-start | bytes 3145736 | tf_op jit(solution)/shard_map/ppermute | solution.py:203
  316.0 4.8 %collective-permute-start.65 = (f32[512]{0:T(512)S(1)}, f32[512]{0:T(512)S(1)}, u32[]{:S(2)}, u32[]{:S(2)}) collective-permute-start(f32[512]{0:T(512)S(1)} %add.79), channel_id=1, source_target_pairs={{0,16},{4,20},{8,24},{12,28},{16,0},{20,4},{24,8},{28,12},{1,17},{... | collective-permute-start | bytes 6152 | tf_op jit(solution)/shard_map/ppermute | solution.py:213
  320.8 34.6 %collective-permute-start.58 = (bf16[1024,512]{1,0:T(8,128)(2,1)}, bf16[1024,512]{1,0:T(8,128)(2,1)S(1)}, u32[]{:S(2)}, u32[]{:S(2)}) collective-permute-start(bf16[1024,512]{1,0:T(8,128)(2,1)} %collective-permute-done.40.refs_2_), channel_id=1, source_target_pairs={{0,1},{1,0},{2,3},{3,2},{4,5},{5,4},{6,7},{7,6},{8,9},{9,8},{10,11... | collective-permute-start | bytes 3145736 | tf_op jit(solution)/shard_map/ppermute | solution.py:203
  330.9 44.8 %collective-permute-start.41 = (bf16[1024,512]{1,0:T(8,128)(2,1)}, bf16[1024,512]{1,0:T(8,128)(2,1)S(1)}, u32[]{:S(2)}, u32[]{:S(2)}) collective-permute-start(bf16[1024,512]{1,0:T(8,128)(2,1)} %copy-done.24), channel_id=1, source_target_pairs={{2,0},{3,1},{0,2},{1,3},{6,4},{7,5},{4,6},{5,7},{10,8},{11,9},{8,1... | collective-permute-start | bytes 3145736 | tf_op jit(solution)/shard_map/ppermute | solution.py:200
  353.3 44.9 %collective-permute-start.33 = (bf16[1024,512]{1,0:T(8,128)(2,1)}, bf16[1024,512]{1,0:T(8,128)(2,1)S(1)}, u32[]{:S(2)}, u32[]{:S(2)}) collective-permute-start(bf16[1024,512]{1,0:T(8,128)(2,1)} %copy-done.26), channel_id=1, source_target_pairs={{2,0},{3,1},{0,2},{1,3},{6,4},{7,5},{4,6},{5,7},{10,8},{11,9},{8,1... | collective-permute-start | bytes 3145736 | tf_op jit(solution)/shard_map/ppermute | solution.py:200
  353.9 66.4 %collective-permute-start.47 = (bf16[1024,512]{1,0:T(8,128)(2,1)}, bf16[1024,512]{1,0:T(8,128)(2,1)S(1)}, u32[]{:S(2)}, u32[]{:S(2)}) collective-permute-start(bf16[1024,512]{1,0:T(8,128)(2,1)} %copy-done.30), channel_id=1, source_target_pairs={{2,0},{3,1},{0,2},{1,3},{6,4},{7,5},{4,6},{5,7},{10,8},{11,9},{8,1... | collective-permute-start | bytes 3145736 | tf_op jit(solution)/shard_map/ppermute | solution.py:200
  355.3 65.0 %collective-permute-start.56 = (bf16[1024,512]{1,0:T(8,128)(2,1)}, bf16[1024,512]{1,0:T(8,128)(2,1)S(1)}, u32[]{:S(2)}, u32[]{:S(2)}) collective-permute-start(bf16[1024,512]{1,0:T(8,128)(2,1)} %collective-permute-done.32.refs_2_), channel_id=1, source_target_pairs={{0,1},{1,0},{2,3},{3,2},{4,5},{5,4},{6,7},{7,6},{8,9},{9,8},{10,11... | collective-permute-start | bytes 3145736 | tf_op jit(solution)/shard_map/ppermute | solution.py:203
  355.4 76.2 %collective-permute-start.54 = (bf16[1024,512]{1,0:T(8,128)(2,1)S(1)}, bf16[1024,512]{1,0:T(8,128)(2,1)S(1)}, u32[]{:S(2)}, u32[]{:S(2)}) collective-permute-start(bf16[1024,512]{1,0:T(8,128)(2,1)S(1)} %collective-permute-done.46.refs_2_), channel_id=1, source_target_pairs={{0,1},{1,0},{2,3},{3,2},{4,5},{5,4},{6,7},{7,6},{8,9},{9,8},{10,11... | collective-permute-start | bytes 3145736 | tf_op jit(solution)/shard_map/ppermute | solution.py:203
  375.8 61.5 %collective-permute-start.52 = (bf16[1024,512]{1,0:T(8,128)(2,1)S(1)}, bf16[1024,512]{1,0:T(8,128)(2,1)S(1)}, u32[]{:S(2)}, u32[]{:S(2)}) collective-permute-start(bf16[1024,512]{1,0:T(8,128)(2,1)S(1)} %collective-permute-done.41.refs_2_), channel_id=1, source_target_pairs={{0,1},{1,0},{2,3},{3,2},{4,5},{5,4},{6,7},{7,6},{8,9},{9,8},{10,11... | collective-permute-start | bytes 3145736 | tf_op jit(solution)/shard_map/ppermute | solution.py:203
  398.3 44.5 %collective-permute-start.50 = (bf16[1024,512]{1,0:T(8,128)(2,1)S(1)}, bf16[1024,512]{1,0:T(8,128)(2,1)S(1)}, u32[]{:S(2)}, u32[]{:S(2)}) collective-permute-start(bf16[1024,512]{1,0:T(8,128)(2,1)S(1)} %collective-permute-done.33.refs_2_), channel_id=1, source_target_pairs={{0,1},{1,0},{2,3},{3,2},{4,5},{5,4},{6,7},{7,6},{8,9},{9,8},{10,11... | collective-permute-start | bytes 3145736 | tf_op jit(solution)/shard_map/ppermute | solution.py:203
  420.3 26.8 %collective-permute-start.44 = (bf16[1024,512]{1,0:T(8,128)(2,1)S(1)}, bf16[1024,512]{1,0:T(8,128)(2,1)S(1)}, u32[]{:S(2)}, u32[]{:S(2)}) collective-permute-start(bf16[1024,512]{1,0:T(8,128)(2,1)S(1)} %copy-done.31), channel_id=1, source_target_pairs={{0,1},{1,0},{2,3},{3,2},{4,5},{5,4},{6,7},{7,6},{8,9},{9,8},{10,11... | collective-permute-start | bytes 3145736 | tf_op jit(solution)/shard_map/ppermute | solution.py:203
  420.4 27.3 %collective-permute-start.48 = (bf16[1024,512]{1,0:T(8,128)(2,1)S(1)}, bf16[1024,512]{1,0:T(8,128)(2,1)S(1)}, u32[]{:S(2)}, u32[]{:S(2)}) collective-permute-start(bf16[1024,512]{1,0:T(8,128)(2,1)S(1)} %collective-permute-done.47.refs_2_), channel_id=1, source_target_pairs={{0,1},{1,0},{2,3},{3,2},{4,5},{5,4},{6,7},{7,6},{8,9},{9,8},{10,11... | collective-permute-start | bytes 3145736 | tf_op jit(solution)/shard_map/ppermute | solution.py:203
  431.6 11.1 %collective-permute-start.42 = (bf16[256,512]{1,0:T(8,128)(2,1)S(1)}, bf16[256,512]{1,0:T(8,128)(2,1)S(1)}, u32[]{:S(2)}, u32[]{:S(2)}) collective-permute-start(bf16[256,512]{1,0:T(8,128)(2,1)S(1)} %copy-done.49), channel_id=1, source_target_pairs={{2,0},{3,1},{0,2},{1,3},{6,4},{7,5},{4,6},{5,7},{10,8},{11,9},{8,1... | collective-permute-start | bytes 786440 | tf_op jit(solution)/shard_map/ppermute | solution.py:200
  437.3 9.8 %collective-permute-start.34 = (bf16[256,512]{1,0:T(8,128)(2,1)S(1)}, bf16[256,512]{1,0:T(8,128)(2,1)S(1)}, u32[]{:S(2)}, u32[]{:S(2)}) collective-permute-start(bf16[256,512]{1,0:T(8,128)(2,1)S(1)} %get-tuple-element.103.refs_0_), channel_id=1, source_target_pairs={{2,0},{3,1},{0,2},{1,3},{6,4},{7,5},{4,6},{5,7},{10,8},{11,9},{8,1... | collective-permute-start | bytes 786440 | tf_op jit(solution)/shard_map/ppermute | solution.py:200
  442.7 8.8 %collective-permute-start.39 = (bf16[256,512]{1,0:T(8,128)(2,1)S(1)}, bf16[256,512]{1,0:T(8,128)(2,1)S(1)}, u32[]{:S(2)}, u32[]{:S(2)}) collective-permute-start(bf16[256,512]{1,0:T(8,128)(2,1)S(1)} %copy-done.49), channel_id=1, source_target_pairs={{0,1},{1,0},{2,3},{3,2},{4,5},{5,4},{6,7},{7,6},{8,9},{9,8},{10,11... | collective-permute-start | bytes 786440 | tf_op jit(solution)/shard_map/ppermute | solution.py:203
  442.7 8.8 %collective-permute-start.43 = (bf16[256,512]{1,0:T(8,128)(2,1)S(1)}, bf16[256,512]{1,0:T(8,128)(2,1)S(1)}, u32[]{:S(2)}, u32[]{:S(2)}) collective-permute-start(bf16[256,512]{1,0:T(8,128)(2,1)S(1)} %collective-permute-done.42.refs_2_), channel_id=1, source_target_pairs={{0,1},{1,0},{2,3},{3,2},{4,5},{5,4},{6,7},{7,6},{8,9},{9,8},{10,11... | collective-permute-start | bytes 786440 | tf_op jit(solution)/shard_map/ppermute | solution.py:203
  447.1 6.1 %collective-permute-start.30 = (bf16[256,512]{1,0:T(8,128)(2,1)S(1)}, bf16[256,512]{1,0:T(8,128)(2,1)S(1)}, u32[]{:S(2)}, u32[]{:S(2)}) collective-permute-start(bf16[256,512]{1,0:T(8,128)(2,1)S(1)} %get-tuple-element.103.refs_0_), channel_id=1, source_target_pairs={{0,1},{1,0},{2,3},{3,2},{4,5},{5,4},{6,7},{7,6},{8,9},{9,8},{10,11... | collective-permute-start | bytes 786440 | tf_op jit(solution)/shard_map/ppermute | solution.py:203
  447.2 6.0 %collective-permute-start.35 = (bf16[256,512]{1,0:T(8,128)(2,1)S(1)}, bf16[256,512]{1,0:T(8,128)(2,1)S(1)}, u32[]{:S(2)}, u32[]{:S(2)}) collective-permute-start(bf16[256,512]{1,0:T(8,128)(2,1)S(1)} %collective-permute-done.34.refs_2_), channel_id=1, source_target_pairs={{0,1},{1,0},{2,3},{3,2},{4,5},{5,4},{6,7},{7,6},{8,9},{9,8},{10,11... | collective-permute-start | bytes 786440 | tf_op jit(solution)/shard_map/ppermute | solution.py:203
  (56 other events, 357.7 us)
Sparse Core Ops, SparseCore 0:
  84.1 40.3 all-gather.1
  284.0 157.6 all-reduce.1

commit v2 on v0

v2 whole, which is shorter than its diff:
```python
import functools

import jax
import jax.numpy as jnp
from jax import lax
from jax.experimental import pallas as pl
from jax.experimental.pallas import tpu as pltpu
from jax.sharding import PartitionSpec as P

BLOCK = 128
F32 = jnp.float32
BF16 = jnp.bfloat16
MESH = pl.DeviceIdType.MESH
SMALL = pl.CostEstimate(flops=1000, bytes_accessed=1000, transcendentals=0)
ANY = pl.BlockSpec(memory_space=pl.ANY)


def params():
    return pltpu.CompilerParams(dimension_semantics=("arbitrary",), vmem_limit_bytes=56 << 20)


def whole(shape):
    return pl.BlockSpec(shape, lambda *_: (0,) * len(shape))


def stencil_of(adjacency, segment):
    columns = jnp.broadcast_to(segment, (BLOCK, BLOCK))
    links = jnp.where(columns == columns.T, adjacency, 0).astype(F32)
    inverse = 1.0 / (jnp.sum(links, axis=1, keepdims=True) + 1.0)
    row = lax.broadcasted_iota(jnp.int32, (BLOCK, BLOCK), 0)
    column = lax.broadcasted_iota(jnp.int32, (BLOCK, BLOCK), 1)
    return (links + jnp.where(row == column, 2.0, 0.0)).astype(BF16), inverse


class cluster_sum:
    PARTS = 4
    BACK = (5, 7, 8, 9)
    rounds = 10

    def __init__(self, total, result, half_in, quarter_in, bias_in, sems, clusters):
        self.result = result
        self.total, self.half_in, self.quarter_in, self.bias_in, self.sems = total, half_in, quarter_in, bias_in, sems
        self.clusters, self.high = clusters, clusters // 2
        self.depth = total.shape[0] - 8
        self.half = self.depth // self.PARTS // 2
        self.quarter = self.half // self.high
        self.me = lax.axis_index("clu")
        self.z, self.x = self.me // 2, lax.rem(self.me, 2)
        self.others = [lax.rem(self.me + d, clusters) for d in range(1, clusters)]
        self.levels = [lax.rem(self.z + d, self.high) for d in range(1, self.high)]

    def rows_of_half(self, c, x):
        return pl.ds(pl.multiple_of(c * 2 * self.half + x * self.half, self.half), self.half)

    def rows_of_quarter(self, c, q):
        start = c * 2 * self.half + self.x * self.half + q * self.quarter
        return pl.ds(pl.multiple_of(start, self.quarter), self.quarter)

    def copy(self, source, target, kind, send, recv, device):
        return pltpu.make_async_remote_copy(
            src_ref=source, dst_ref=target, send_sem=self.sems[2 * kind].at[send],
            recv_sem=self.sems[2 * kind + 1].at[recv], device_id={"clu": device}, device_id_type=MESH,
        )

    def give_half(self, c):
        rows = self.rows_of_half(c, 1 - self.x)
        return self.copy(self.total.at[rows], self.half_in.at[c], 0, c, c, self.z * 2 + 1 - self.x)

    def give_quarter(self, c, source, target):
        rows = self.rows_of_quarter(c, target)
        return self.copy(
            self.total.at[rows], self.quarter_in.at[c, source], 1, (c, target), (c, source), target * 2 + self.x
        )

    def return_quarter(self, c, source, target):
        rows = self.rows_of_quarter(c, source)
        return self.copy(
            self.result.at[rows], self.result.at[rows], 2, (c, target), (c, source), target * 2 + self.x
        )

    def return_half(self, c, x):
        rows = self.rows_of_half(c, x)
        return self.copy(self.result.at[rows], self.result.at[rows], 3, c, c, self.z * 2 + 1 - self.x)

    def give_bias(self, source, target):
        return self.copy(
            self.total.at[pl.ds(self.depth, 8)], self.bias_in.at[source], 4, target, source, target
        )

    def start(self):
        for c in range(self.PARTS):
            self.give_half(c).start()
        for other in self.others:
            self.give_bias(self.me, other).start()

    def advance(self, k):
        total = self.total
        if k < self.PARTS:
            self.give_half(k).wait_recv()
            total[self.rows_of_half(k, self.x), :] += self.half_in[k]
            for level in self.levels:
                self.give_quarter(k, self.z, level).start()
        c = k - 2
        if 0 <= c < self.PARTS:
            rows = self.rows_of_quarter(c, self.z)
            for level in self.levels:
                self.give_quarter(c, level, self.z).wait_recv()
            value = total[rows, :]
            for level in self.levels:
                value = value + self.quarter_in[c, level]
            self.result[rows, :] = value
            for level in self.levels:
                self.return_quarter(c, self.z, level).start()
        if k in self.BACK:
            c = self.BACK.index(k)
            for level in self.levels:
                self.return_quarter(c, level, self.z).wait_recv()
            self.return_half(c, self.x).start()

    def finish(self):
        for c in range(self.PARTS):
            self.give_half(c).wait_send()
            for level in self.levels:
                self.give_quarter(c, self.z, level).wait_send()
                self.return_quarter(c, self.z, level).wait_send()
            self.return_half(c, self.x).wait_send()
            self.return_half(c, 1 - self.x).wait_recv()
        for other in self.others:
            self.give_bias(self.me, other).wait_send()
            self.give_bias(other, self.me).wait_recv()
        value = self.total[pl.ds(self.depth, 8), :]
        for other in self.others:
            value = value + self.bias_in[other]
        self.result[pl.ds(self.depth, 8), :] = value


def exchange_kernel(
    n, clusters, groups, tile, features, adjacency, cotangent, segments, weight, bias,
    out, total_out, blocks_out, *rest,
):
    grads, rest = rest[: len(groups)], rest[len(groups) :]
    landing = (None,) + rest[: n - 1]
    (pieces, feat, adj, cot, act, grad, seg, mat, vec, total, shares, load_sem, cot_sem, out_sem, grad_sem,
     fixed_sem, send_sem, recv_sem, early_send, early_recv, share_send, share_recv, spread_send, spread_recv,
     block_send, block_recv, summed_total, half_in, quarter_in, bias_in, sum_sems) = rest[n - 1 :]
    outer = n // 2
    early = groups[0]
    ends = [sum(groups[: i + 1]) for i in range(len(groups))]
    rows, width = features.shape
    depth = mat.shape[0]
    count = rows // tile
    me, cluster = lax.axis_index("col"), lax.axis_index("clu")
    chip, core = me // 2, lax.rem(me, 2)
    sibling = chip * 2 + 1 - core
    part = 2 * width // clusters

    def chip_at(shift):
        return lax.rem(chip + shift + outer, outer) * 2 + core

    def at(k):
        return pl.ds(pl.multiple_of(k * tile, tile), tile)

    def loads(k):
        slot = lax.rem(k, 2)
        return (
            pltpu.make_async_copy(features.at[at(k)], feat.at[slot], load_sem.at[0, slot]),
            pltpu.make_async_copy(adjacency.at[at(k)], adj.at[slot], load_sem.at[1, slot]),
        )

    def load_cot(k):
        slot = lax.rem(k, 2)
        return pltpu.make_async_copy(cotangent.at[at(k)], cot.at[slot], cot_sem.at[slot])

    def store_out(k):
        slot = lax.rem(k, 2)
        return pltpu.make_async_copy(act.at[slot], out.at[at(k)], out_sem.at[slot])

    def store_grad(k, act_on):
        slot = lax.rem(k, 2)
        for start, end, target in zip([0] + ends, ends, grads):

            @pl.when((k >= start) & (k < end))
            def _():
                act_on(pltpu.make_async_copy(grad.at[slot], target.at[at(k - start)], grad_sem.at[slot]))

    def remote(source, target, send, recv, device, axis="col"):
        return pltpu.make_async_remote_copy(
            src_ref=source, dst_ref=target, send_sem=send, recv_sem=recv,
            device_id={axis: device}, device_id_type=MESH,
        )

    def hop(p, k):
        source = 0 if p % 2 == 0 else p - 1
        device = chip_at(-(p // 2)) if p % 2 == 0 else sibling
        return remote(pieces.at[source, at(k)], pieces.at[p, at(k)], send_sem.at[p, k], recv_sem.at[p, k], device)

    def early_hop(p, k):
        source = grads[0] if p < 2 or p % 2 == 0 else landing[p - 1]
        device = chip_at(-(p // 2)) if p % 2 == 0 else sibling
        return remote(source.at[at(k)], landing[p].at[at(k)], early_send.at[p, k], early_recv.at[p, k], device)

    def share(shift):
        owner = lax.rem(chip - shift + outer, outer)
        rows = pl.ds(pl.multiple_of(owner * 2 * width + cluster * part, part), part)
        mine = pl.ds(pl.multiple_of(cluster * part, part), part)
        return remote(
            weight.at[rows], shares.at[shift, mine], share_send.at[shift], share_recv.at[shift], chip_at(-shift)
        )

    def spread(shift, source, peer):
        rows = pl.ds(pl.multiple_of(source * part, part), part)
        return remote(
            shares.at[shift, rows], shares.at[shift, rows],
            spread_send.at[shift, peer], spread_recv.at[shift, source], peer, "clu",
        )

    def block(p):
        half = core if p % 2 == 0 else 1 - core
        if p < 2:
            source = weight.at[pl.ds(pl.multiple_of((chip * 2 + half) * width, width), width)]
        else:
            source = shares.at[p // 2, pl.ds(pl.multiple_of(half * width, width), width)]
        if p % 2 == 0:
            return pltpu.make_async_copy(source, blocks_out.at[p], block_recv.at[p])
        return remote(source, blocks_out.at[p], block_send.at[p], block_recv.at[p], sibling)

    others = [lax.rem(cluster + d, clusters) for d in range(1, clusters)]
    for copy in loads(0):
        copy.start()
    fixed = [
        pltpu.make_async_copy(source, target, fixed_sem.at[i])
        for i, (source, target) in enumerate([(segments, seg), (weight, mat), (bias, vec)])
    ]
    for copy in fixed:
        copy.start()
    load_cot(0).start()

    barrier = pltpu.get_barrier_semaphore()
    peers = [("col", sibling)] + [("col", chip_at(shift)) for shift in range(1, outer)]
    peers += [("clu", peer) for peer in others]
    for axis, peer in peers:
        pl.semaphore_signal(barrier, inc=1, device_id={axis: peer}, device_id_type=MESH)
    pl.semaphore_wait(barrier, len(peers))
    for shift in range(1, outer):
        share(shift).start()
    block(0).start()
    block(1).start()
    fixed[0].wait()

    def aggregate_tile(k, carry):
        slot = lax.rem(k, 2)
        for copy in loads(k):
            copy.wait()

        @pl.when(k + 1 < count)
        def _():
            for copy in loads(k + 1):
                copy.start()

        for b in range(tile // BLOCK):
            part = pl.ds(b * BLOCK, BLOCK)
            stencil, inverse = stencil_of(adj[slot, part, :], seg[pl.ds(k * (tile // BLOCK) + b, 1), :])
            summed = jnp.dot(stencil, feat[slot, part, :], preferred_element_type=F32)
            target = pl.ds(pl.multiple_of(k * tile + b * BLOCK, BLOCK), BLOCK)
            pieces[0, target, :] = (summed * inverse).astype(BF16)
        for shift in range(1, outer):
            hop(2 * shift, k).start()
        hop(1, k).start()
        return carry

    lax.fori_loop(0, count, aggregate_tile, 0)
    total[...] = jnp.zeros_like(total)
    fixed[1].wait()
    fixed[2].wait()
    blocks = [lax.rem(chip + p // 2, outer) * 2 + (core if p % 2 == 0 else 1 - core) for p in range(n)]

    def forward_tile(k):
        slot = lax.rem(k, 2)
        load_cot(k).wait()

        @pl.when(k + 1 < count)
        def _():
            load_cot(k + 1).start()

        hop(1, k).wait_recv()
        for shift in range(1, outer):
            hop(2 * shift + 1, k).wait_recv()

        @pl.when(k >= 2)
        def _():
            store_out(k - 2).wait()
            store_grad(k - 2, lambda copy: copy.wait())

            @pl.when(k - 2 < early)
            def _():
                for shift in range(1, outer):
                    early_hop(2 * shift, k - 2).start()
                early_hop(1, k - 2).start()

        preact = None
        for p in range(n):
            source = pl.ds(pl.multiple_of(blocks[p] * width, width), width)
            term = jnp.dot(pieces[p, at(k), :], mat[source, :], preferred_element_type=F32)
            preact = term if preact is None else preact + term
        preact = preact + vec[...].astype(F32)
        act[slot] = jnp.maximum(preact, 0.0).astype(BF16)
        grad_preact = jnp.where(preact > 0.0, cot[slot].astype(F32), 0.0)
        total[pl.ds(depth, 8), :] += jnp.sum(grad_preact.reshape(tile // 8, 8, width), axis=0)
        grad_preact = grad_preact.astype(BF16)
        grad[slot] = grad_preact
        store_out(k).start()
        store_grad(k, lambda copy: copy.start())
        for p in range(n):
            target = pl.ds(pl.multiple_of(blocks[p] * width, width), width)
            total[target, :] += lax.dot_general(
                pieces[p, at(k), :], grad_preact, (((0,), (0,)), ((), ())), preferred_element_type=F32
            )

    def step(k, carry):
        @pl.when(k < count)
        def _():
            for shift in range(1, outer):
                hop(2 * shift, k).wait_recv()
                hop(2 * shift + 1, k).start()

        @pl.when(k == 1)
        def _():
            for shift in range(1, outer):
                share(shift).wait_recv()
                for peer in others:
                    spread(shift, cluster, peer).start()

        @pl.when(k == 4)
        def _():
            for shift in range(1, outer):
                for peer in others:
                    spread(shift, peer, cluster).wait_recv()
                block(2 * shift).start()
                block(2 * shift + 1).start()

        @pl.when(k >= 1)
        def _():
            forward_tile(k - 1)

        return carry

    lax.fori_loop(0, count + 1, step, 0)
    sums = cluster_sum(total, summed_total, half_in, quarter_in, bias_in, sum_sems, clusters)
    sums.start()
    for k in (count - 2, count - 1):
        store_out(k).wait()
        store_grad(k, lambda copy: copy.wait())

    def finish_early(k, carry):
        for p in range(1, n):
            if p == 1 or p % 2:
                early_hop(p, k).wait_recv()
            early_hop(p, k).wait_send()
        return carry

    def finish(k, carry):
        for p in range(1, n):
            hop(p, k).wait_send()
        return carry

    lax.fori_loop(0, count, finish, 0)
    for p in range(n):
        if p % 2:
            block(p).wait_send()
            block(p).wait_recv()
        else:
            block(p).wait()
    for shift in range(1, outer):
        share(shift).wait_send()
        for peer in others:
            spread(shift, cluster, peer).wait_send()
    for k in range(max(early, sums.rounds)):
        if k < early:
            for shift in range(1, outer):
                early_hop(2 * shift, k).wait_recv()
                early_hop(2 * shift + 1, k).start()
        sums.advance(k)
    sums.finish()
    result = pltpu.make_async_copy(summed_total, total_out, fixed_sem.at[3])
    result.start()
    lax.fori_loop(0, early, finish_early, 0)
    result.wait()


def exchange(features, adjacency, cotangent, segments, weight, bias, n, clusters, groups, tile):
    rows, width = features.shape
    depth = weight.shape[0]
    count, outer = rows // tile, n // 2
    early = groups[0]
    parts, high = cluster_sum.PARTS, clusters // 2
    dma = pltpu.SemaphoreType.DMA
    array = jax.ShapeDtypeStruct
    return pl.pallas_call(
        functools.partial(exchange_kernel, n, clusters, groups, tile),
        in_specs=[ANY] * 6,
        out_specs=[ANY] * (2 + n + len(groups)),
        out_shape=[array((rows, width), BF16), array((depth + 8, width), F32), array((n, width, width), BF16)]
        + [array((group * tile, width), BF16) for group in groups]
        + [array((early * tile, width), BF16)] * (n - 1),
        scratch_shapes=[
            pltpu.VMEM((n, rows, width), BF16),
            pltpu.VMEM((2, tile, width), BF16),
            pltpu.VMEM((2, tile, BLOCK), jnp.int32),
            pltpu.VMEM((2, tile, width), BF16),
            pltpu.VMEM((2, tile, width), BF16),
            pltpu.VMEM((2, tile, width), BF16),
            pltpu.VMEM(segments.shape, jnp.int32),
            pltpu.VMEM((depth, width), BF16),
            pltpu.VMEM((1, width), BF16),
            pltpu.VMEM((depth + 8, width), F32),
            pltpu.VMEM((outer, 2 * width, width), BF16),
            dma((2, 2)),
            dma((2,)),
            dma((2,)),
            dma((2,)),
            dma((4,)),
            dma((n, count)),
            dma((n, count)),
            dma((n, early)),
            dma((n, early)),
            dma((outer,)),
            dma((outer,)),
            dma((outer, clusters)),
            dma((outer, clusters)),
            dma((n,)),
            dma((n,)),
            pltpu.VMEM((depth + 8, width), F32),
            pltpu.VMEM((parts, depth // parts // 2, width), F32),
            pltpu.VMEM((parts, high, depth // parts // 2 // high, width), F32),
            pltpu.VMEM((clusters, 8, width), F32),
            [
                dma((parts,)), dma((parts,)), dma((parts, high)), dma((parts, high)), dma((parts, high)),
                dma((parts, high)), dma((parts,)), dma((parts,)), dma((clusters,)), dma((clusters,)),
            ],
        ],
        compiler_params=pltpu.CompilerParams(
            collective_id=0, has_side_effects=True, vmem_limit_bytes=62 << 20
        ),
    )(features, adjacency, cotangent, segments, weight, bias)


def backward_kernel(n, first, tile, *refs):
    grads, (weights, adjacency, segments), out = refs[:n], refs[n : n + 3], refs[-2]
    refs[-1][...] = jnp.zeros_like(refs[-1])
    step = pl.program_id(0)
    grad = None
    for p in range(n):
        term = lax.dot_general(
            grads[p][...], weights[p], (((1,), (1,)), ((), ())), preferred_element_type=F32
        )
        grad = term if grad is None else grad + term
    grad = grad.astype(BF16)
    for b in range(tile // BLOCK):
        rows = pl.ds(b * BLOCK, BLOCK)
        index = first // BLOCK + step * (tile // BLOCK) + b
        stencil, inverse = stencil_of(adjacency[rows, :], segments[pl.ds(index, 1), :])
        summed = (grad[b * BLOCK : (b + 1) * BLOCK].astype(F32) * inverse).astype(BF16)
        out[rows, :] = jnp.dot(stencil, summed, preferred_element_type=F32)


def backward(grads, weights, adjacency, segments, carried, first, size, *earlier):
    n, width = len(grads), weights.shape[1]
    rows = adjacency.shape[0]
    tile = min(size, 512)
    offset = first // tile

    def rows_from(base):
        return pl.BlockSpec((tile, width), lambda i: (base // tile + i, 0))

    in_specs = (
        [rows_from(base) for _, base in grads]
        + [whole(weights.shape)]
        + [pl.BlockSpec((tile, BLOCK), lambda i: (offset + i, 0)), whole(segments.shape)]
    )
    operands = [x for x, _ in grads] + [weights, adjacency, segments]
    aliases = {}
    if carried is not None:
        in_specs.append(ANY)
        aliases = {len(operands): 0}
        operands.append(carried)
    in_specs += [ANY] * len(earlier)
    operands += earlier
    return pl.pallas_call(
        functools.partial(backward_kernel, n, first, tile),
        grid=(size // tile,),
        in_specs=in_specs,
        out_specs=[pl.BlockSpec((tile, width), lambda i: (offset + i, 0)), whole((8, BLOCK))],
        out_shape=[jax.ShapeDtypeStruct((rows, width), F32), jax.ShapeDtypeStruct((8, BLOCK), F32)],
        input_output_aliases=aliases,
        cost_estimate=SMALL,
        compiler_params=params(),
    )(*operands)


def copy_kernel(source, earlier, target):
    target[...] = source[...]


def copied(x, earlier):
    rows, width = x.shape
    spec = pl.BlockSpec((1024, width), lambda i: (i, 0))
    return pl.pallas_call(
        copy_kernel,
        grid=(rows // 1024,),
        in_specs=[spec, ANY],
        out_specs=spec,
        out_shape=jax.ShapeDtypeStruct(x.shape, x.dtype),
        cost_estimate=SMALL,
        compiler_params=params(),
    )(x, earlier)


def tie_kernel(*refs):
    pass


def tie(x, *earlier):
    return pl.pallas_call(
        tie_kernel,
        in_specs=[ANY] * (1 + len(earlier)),
        out_specs=ANY,
        out_shape=jax.ShapeDtypeStruct(x.shape, x.dtype),
        input_output_aliases={0: 0},
        cost_estimate=SMALL,
    )(x, *earlier)


def split_kernel(total, earlier, grad_weight, grad_bias):
    depth, width = grad_weight.shape
    grad_weight[...] = total[pl.ds(0, depth), :]
    grad_bias[...] = jnp.broadcast_to(jnp.sum(total[pl.ds(depth, 8), :], axis=0, keepdims=True), (8, width))


def split(total, earlier):
    rows, width = total.shape
    return pl.pallas_call(
        split_kernel,
        grid=(1,),
        in_specs=[whole(total.shape), ANY],
        out_specs=[whole((rows - 8, width)), whole((8, width))],
        out_shape=[jax.ShapeDtypeStruct((rows - 8, width), F32), jax.ShapeDtypeStruct((8, width), F32)],
        cost_estimate=SMALL,
        compiler_params=params(),
    )(total, earlier)


def tile_groups(count):
    return [count - 5, 3, 1, 1]


def build(n, clusters):
    outer = n // 2

    def device(chip, core):
        return (chip % outer) * 2 + core

    def from_chip(x, shift):
        pairs = [(device(chip + shift, core), device(chip, core)) for chip in range(outer) for core in range(2)]
        return lax.ppermute(x, "col", pairs)

    def from_sibling(x):
        return lax.ppermute(x, "col", [(i, i ^ 1) for i in range(n)])

    def local(features, weight, bias, adjacency, segments, cotangent):
        rows, width = features.shape
        tile = 512
        groups = tile_groups(rows // tile)
        out, total, blocks, *rest = exchange(
            features, adjacency, cotangent, segments, weight, bias.reshape(1, width), n, clusters, groups, tile
        )
        grads, landing = rest[: len(groups)], rest[len(groups) :]
        own = grads[1:-1] + [grads[-1][: tile // 2], grads[-1][tile // 2 :]]
        near, far = [], []
        for k, x in enumerate(own):
            if k:
                x = own[k] = tie(x, near[-1])
            near.append(from_sibling(x))
            far.append([from_chip(x, shift) for shift in range(1, outer)])
        out = copied(out, near[-1])
        grad_weight, grad_bias = split(total, out)
        first = groups[0] * tile
        grad_features, token = backward(
            [(x, 0) for x in [grads[0]] + landing], blocks, adjacency, segments, None, 0, first, grad_bias
        )
        for k, x in enumerate(own):
            parts = [(x, 0), (near[k], 0)]
            for y in far[k]:
                y = tie(y, token)
                parts += [(y, 0), (from_sibling(y), 0)]
            size = x.shape[0]
            grad_features, token = backward(parts, blocks, adjacency, segments, grad_features, first, size)
            first += size
        return (out, grad_features, grad_weight, grad_bias[0])

    return local


def solution(mesh):
    return jax.shard_map(
        build(mesh.shape["col"], mesh.shape["clu"]),
        mesh=mesh,
        in_specs=(
            P("clu", "col"),
            P(None, "col"),
            P("col"),
            P("clu", None),
            P("clu", None),
            P("clu", "col"),
        ),
        out_specs=(P("clu", "col"), P("clu", "col"), P(None, "col"), P("col")),
        check_vma=False,
    )
```

time: 916 us -> 424 us (0.46)
  waiting for transfers between devices: 754 us -> 16.7 us
  Pallas kernels: 0 us -> 384 us
  matrix products: 98.8 us -> 0 us
  blocking collectives: 21.5 us -> 0 us
  other arithmetic: 16.2 us -> 0 us
  between operations: 13.8 us -> 0.69 us
    reduce_scatter x1 -> x0, waiting for transfers between devices: 404 us -> none  [local(): lax.psum_scatter(partials, 'col', scatter_dimension=1, tiled=True)]
    pallas_call x0 -> x15, Pallas kernels: none -> 384 us  [the longest x1 328 us: exchange(): pl.pallas_call(functools.partial(exchange_kernel, n, clusters, groups, ti...]
    all_gather x1 -> x0, waiting for transfers between devices: 204 us -> none  [local(): gathered = lax.all_gather(aggregated, 'col', axis=1, tiled=True)]
    psum x1 -> x0, waiting for transfers between devices: 146 us -> none  [local(): grad_weight, grad_bias = lax.psum((grad_weight, grad_bias), 'clu')]
    dot_general x5 -> x0, matrix products: 98.8 us -> none  [the longest x1 29.1 us: local(): lax.dot_general(grad_preact, weight, (((1,), (1,)), ((), ())), preferred_...]
    psum x1 -> x0, blocking collectives: 21.5 us -> none  [local(): grad_weight, grad_bias = lax.psum((grad_weight, grad_bias), 'clu')]
    ppermute x0 -> x12, waiting for transfers between devices: none -> 16.7 us  [the longest x8 12.1 us: from_sibling(): return lax.ppermute(x, 'col', [(i, i ^ 1) for i in range(n)])]
    convert_element_type x3 -> x0, other arithmetic: 11.5 us -> none  [the longest x1 6.74 us: local(): (grad_aggregated.astype(jnp.float32) * inverse).astype(jnp.bfloat16)]
  transfers between devices with their start and end apart: 3 -> 12, of which waited for: 3 -> 11; matrix products, arithmetic and copies ran while one was open for 4% -> 1% of each run, Pallas kernels for 0% -> 13%
where the time goes in v2:
time: 424 us; the launch traced here: 419 us
  Pallas kernels  384 us (91%)
  waiting for transfers between devices  16.7 us (4%)
  local copies, waits for them, and re-layouts  14.5 us (3%)
    pallas_call x1, Pallas kernels, exchange(): pl.pallas_call(functools.partial(exchange_kernel, n, clusters, groups, ti...  328 us
    pallas_call x5, Pallas kernels, backward(): pl.pallas_call(functools.partial(backward_kernel, n, first, tile), grid=(...  43.1 us
    ppermute x8, waiting for transfers between devices, from_sibling(): return lax.ppermute(x, 'col', [(i, i ^ 1) for i in range(n)])  12.1 us
    unnamed x30, local copies, waits for them, and re-layouts  10.1 us
    pallas_call x1, Pallas kernels, copied(): pl.pallas_call(copy_kernel, grid=(rows // 1024,), in_specs=[spec, ANY], o...  8.95 us
  transfers between devices with their start and end apart: 12, of which 11 were waited for; matrix products, arithmetic and copies ran while one was open for 1% of the time, Pallas kernels for 13%

profile of v2, /device:TPU:0, one launch (start us, length us, event | category | flops | bytes accessed | tf_op | source)
XLA Modules:
  0.0 419.5 jit_solution(13316725615862330107)
XLA Ops:
  0.6 1.3 reshape.11.bias
  1.9 327.7 %shard_map.93 = (bf16[8192,512]{1,0:T(8,128)(2,1)}, f32[2056,512]{1,0:T(8,128)}, bf16[4,512,512]{2,1,0:T(8,128)(2,1)}, bf16[5632,512]{1,0:T(8,128)(2,1)}, bf16[1...) custom-call(bf16[8192,512]{1,0:T(8,128)(2,1)} %features.1, ...), custom_call_target="tpu_custom_call" | custom-call | tf_op jit(solution)/shard_map/pallas_call | solution.py:398
  329.6 0.1 collective-permute-start
  329.7 0.6 collective-permute-start.7
  330.3 3.0 collective-permute-done.refs_1_
  333.3 0.0 copy-start
  333.3 1.1 copy-done
  334.5 0.1 collective-permute-start.1
  334.6 1.9 fusion
  336.5 0.1 collective-permute-done.1.refs_1_
  336.6 0.0 copy-start.5
  336.6 0.8 copy-done.5
  337.4 0.3 collective-permute-start.2
  337.6 1.5 collective-permute-done.2.refs_1_
  339.1 0.0 copy-start.9
  339.1 0.7 copy-done.9
  339.9 0.3 collective-permute-start.3
  340.1 1.5 collective-permute-done.3.earlier.refs_1_
  341.6 0.0 copy-start.8
  341.6 0.7 copy-done.8
  342.3 8.9 %shard_map.97.earlier = bf16[8192,512]{1,0:T(8,128)(2,1)} custom-call(bf16[8192,512]{1,0:T(8,128)(2,1)} %get-tuple-element.25.source, bf16[256,512]{1,0:T(8,128)(2,1)} %copy-done.8), custom_call_target="tpu_custom_call" | custom-call | flops 1000 | bytes 1000 | tf_op jit(solution)/shard_map/pallas_call | solution.py:507
  351.2 4.5 %shard_map.98 = (f32[2048,512]{1,0:T(8,128)}, f32[8,512]{1,0:T(8,128)}) custom-call(f32[2056,512]{1,0:T(8,128)} %get-tuple-element.34.total, bf16[8192,512]{1,0:T(8,128)(2,1)} %shard_map.97.earlier), custom_call_target="tpu_custom_call" | custom-call | flops 1000 | bytes 1000 | tf_op jit(solution)/shard_map/pallas_call | solution.py:541
  355.7 0.0 copy-start.4
  355.7 22.4 %shard_map.99 = (f32[8192,512]{1,0:T(8,128)}, f32[8,128]{1,0:T(8,128)}) custom-call(bf16[5632,512]{1,0:T(8,128)(2,1)} %get-tuple-element.29.refs_0_, bf16[5632,512]{1,0:T(8,128)(2,1)} %get-tuple-element.30.refs_1_, bf16[5632,512]{1,0:T(8,128)(2,1)} %get-tuple-element.31.refs_2_, bf16[5632,512]{1,0:T(8,128)(2,1)} %get-tuple-element.32.refs_3_, ...), custom_call_target="tpu_custom_call" | custom-call | flops 1000 | bytes 1000 | tf_op jit(solution)/shard_map/pallas_call | solution.py:488
  378.2 0.0 collective-permute-done.7.refs_0_
  378.2 0.0 copy-start.1
  378.2 1.1 copy-done.1
  379.3 0.3 collective-permute-start.8
  379.6 0.0 copy-done.4
  379.6 0.6 collective-permute-start.6
  380.1 2.8 collective-permute-done.8.refs_3_
  383.0 0.0 copy-start.7
  383.0 1.2 copy-done.7
  384.1 0.0 copy-start.3
  384.1 8.6 %shard_map.101 = (f32[8192,512]{1,0:T(8,128)}, f32[8,128]{1,0:T(8,128)}) custom-call(bf16[1536,512]{1,0:T(8,128)(2,1)} %get-tuple-element.28.refs_0_, bf16[1536,512]{1,0:T(8,128)(2,1)} %copy-done, bf16[1536,512]{1,0:T(8,128)(2,1)} %shard_map.100.refs_2_, bf16[1536,512]{1,0:T(8,128)(2,1)} %copy-done.7, ...), custom_call_target="tpu_custom_call", output_to_operand_aliasing={{0}: (7, {})} | custom-call | flops 1000 | bytes 1000 | tf_op jit(solution)/shard_map/pallas_call | solution.py:488
  392.7 1.0 collective-permute-done.6.refs_0_
  393.7 0.0 copy-start.6
  393.7 0.8 copy-done.6
  394.5 0.0 collective-permute-start.9
  394.5 0.0 copy-done.3
  394.5 0.6 collective-permute-start.5
  395.0 1.6 collective-permute-done.9.refs_3_
  396.6 0.0 copy-start.12
  396.6 0.8 copy-done.12
  397.4 0.0 copy-start.2
  397.4 4.8 %shard_map.103 = (f32[8192,512]{1,0:T(8,128)}, f32[8,128]{1,0:T(8,128)}) custom-call(bf16[512,512]{1,0:T(8,128)(2,1)} %shard_map.94.refs_0_, bf16[512,512]{1,0:T(8,128)(2,1)} %copy-done.5, bf16[512,512]{1,0:T(8,128)(2,1)} %shard_map.102.refs_2_, bf16[512,512]{1,0:T(8,128)(2,1)} %copy-done.12, ...), custom_call_target="tpu_custom_call", output_to_operand_aliasing={{0}: (7, {})} | custom-call | flops 1000 | bytes 1000 | tf_op jit(solution)/shard_map/pallas_call | solution.py:488
  402.2 1.0 collective-permute-done.5.refs_0_
  403.2 0.0 copy-start.10
  403.2 0.7 copy-done.10
  403.9 0.0 collective-permute-start.10
  403.9 0.0 copy-done.2
  403.9 0.6 collective-permute-start.4
  404.5 1.2 collective-permute-done.10.refs_3_
  405.6 0.0 copy-start.13
  405.7 0.7 copy-done.13
  406.3 3.7 shard_map.105
  410.0 2.6 collective-permute-done.4.refs_0_
  412.6 0.0 copy-start.11
  412.6 0.7 copy-done.11
  413.3 0.0 collective-permute-start.11
  413.3 1.3 slice.11
  414.6 0.4 collective-permute-done.11.refs_3_
  415.1 0.7 copy-done.14
  415.8 3.7 shard_map.107
  (8 shorter events, 0.0 us)
Async XLA Ops:
  329.6 3.7 collective-permute-start
  329.7 48.5 %collective-permute-start.7 = (bf16[1536,512]{1,0:T(8,128)(2,1)}, bf16[1536,512]{1,0:T(8,128)(2,1)S(1)}, u32[]{:S(2)}, u32[]{:S(2)}) collective-permute-start(bf16[1536,512]{1,0:T(8,128)(2,1)} %get-tuple-element.28.refs_0_), channel_id=1, source_target_pairs={{2,0},{3,1},{0,2},{1,3},{6,4},{7,5},{4,6},{5,7},{10,8},{11,9},{8,1... | collective-permute-start | bytes 4718600 | tf_op jit(solution)/shard_map/ppermute | solution.py:564
  333.3 1.1 copy-start
  334.5 2.1 collective-permute-start.1
  336.6 0.8 copy-start.5
  337.4 1.7 collective-permute-start.2
  339.1 0.7 copy-start.9
  339.9 1.7 collective-permute-start.3
  341.6 0.7 copy-start.8
  355.7 23.9 %copy-start.4 = (bf16[512,512]{1,0:T(8,128)(2,1)S(1)}, bf16[512,512]{1,0:T(8,128)(2,1)}, u32[]{:S(2)}) copy-start(bf16[512,512]{1,0:T(8,128)(2,1)} %shard_map.94.refs_0_) | copy-start | bytes 1572868
  378.2 1.2 copy-start.1
  379.3 3.6 collective-permute-start.8
  379.6 14.1 %collective-permute-start.6 = (bf16[512,512]{1,0:T(8,128)(2,1)S(1)}, bf16[512,512]{1,0:T(8,128)(2,1)S(1)}, u32[]{:S(2)}, u32[]{:S(2)}) collective-permute-start(bf16[512,512]{1,0:T(8,128)(2,1)S(1)} %copy-done.4), channel_id=1, source_target_pairs={{2,0},{3,1},{0,2},{1,3},{6,4},{7,5},{4,6},{5,7},{10,8},{11,9},{8,1... | collective-permute-start | bytes 1572872 | tf_op jit(solution)/shard_map/ppermute | solution.py:564
  383.0 1.2 copy-start.7
  384.1 10.3 %copy-start.3 = (bf16[256,512]{1,0:T(8,128)(2,1)S(1)}, bf16[256,512]{1,0:T(8,128)(2,1)}, u32[]{:S(2)}) copy-start(bf16[256,512]{1,0:T(8,128)(2,1)} %shard_map.95.refs_0_) | copy-start | bytes 786436
  393.7 0.8 copy-start.6
  394.5 2.1 collective-permute-start.9
  394.5 8.7 %collective-permute-start.5 = (bf16[256,512]{1,0:T(8,128)(2,1)S(1)}, bf16[256,512]{1,0:T(8,128)(2,1)S(1)}, u32[]{:S(2)}, u32[]{:S(2)}) collective-permute-start(bf16[256,512]{1,0:T(8,128)(2,1)S(1)} %copy-done.3), channel_id=1, source_target_pairs={{2,0},{3,1},{0,2},{1,3},{6,4},{7,5},{4,6},{5,7},{10,8},{11,9},{8,1... | collective-permute-start | bytes 786440 | tf_op jit(solution)/shard_map/ppermute | solution.py:564
  396.6 0.8 copy-start.12
  397.4 6.5 %copy-start.2 = (bf16[256,512]{1,0:T(8,128)(2,1)S(1)}, bf16[256,512]{1,0:T(8,128)(2,1)}, u32[]{:S(2)}) copy-start(bf16[256,512]{1,0:T(8,128)(2,1)} %shard_map.96.refs_0_) | copy-start | bytes 786436
  403.2 0.7 copy-start.10
  403.9 1.7 collective-permute-start.10
  403.9 8.7 %collective-permute-start.4 = (bf16[256,512]{1,0:T(8,128)(2,1)S(1)}, bf16[256,512]{1,0:T(8,128)(2,1)S(1)}, u32[]{:S(2)}, u32[]{:S(2)}) collective-permute-start(bf16[256,512]{1,0:T(8,128)(2,1)S(1)} %copy-done.2), channel_id=1, source_target_pairs={{2,0},{3,1},{0,2},{1,3},{6,4},{7,5},{4,6},{5,7},{10,8},{11,9},{8,1... | collective-permute-start | bytes 786440 | tf_op jit(solution)/shard_map/ppermute | solution.py:564
  405.6 0.7 copy-start.13
  412.6 0.7 copy-start.11
  413.3 1.7 collective-permute-start.11
  415.1 0.7 copy-start.14

commit v3 on v2

--- a/solution.py
+++ b/solution.py
@@ -36,6 +36,7 @@
     PARTS = 4
     BACK = (5, 7, 8, 9)
     rounds = 10
+    last = 12
 
     def __init__(self, total, result, half_in, quarter_in, bias_in, sems, clusters):
         self.result = result
@@ -135,17 +136,14 @@
 
 
 def exchange_kernel(
-    n, clusters, groups, tile, features, adjacency, cotangent, segments, weight, bias,
-    out, total_out, blocks_out, *rest,
+    n, clusters, early, tile, features, adjacency, cotangent, segments, weight, bias,
+    out, total_out, blocks_out, stencil_out, back_out, grads, late_grads, late_near, *rest,
 ):
-    grads, rest = rest[: len(groups)], rest[len(groups) :]
     landing = (None,) + rest[: n - 1]
-    (pieces, feat, adj, cot, act, grad, seg, mat, vec, total, shares, load_sem, cot_sem, out_sem, grad_sem,
-     fixed_sem, send_sem, recv_sem, early_send, early_recv, share_send, share_recv, spread_send, spread_recv,
+    (pieces, feat, adj, cot, act, grad, seg, sten, mat, vec, total, shares, back, load_sem, cot_sem, out_sem, grad_sem,
+     fixed_sem, send_sem, recv_sem, early_send, early_recv, back_sem, share_send, share_recv, spread_send, spread_recv,
      block_send, block_recv, summed_total, half_in, quarter_in, bias_in, sum_sems) = rest[n - 1 :]
     outer = n // 2
-    early = groups[0]
-    ends = [sum(groups[: i + 1]) for i in range(len(groups))]
     rows, width = features.shape
     depth = mat.shape[0]
     count = rows // tile
@@ -175,13 +173,18 @@
         slot = lax.rem(k, 2)
         return pltpu.make_async_copy(act.at[slot], out.at[at(k)], out_sem.at[slot])
 
-    def store_grad(k, act_on):
-        slot = lax.rem(k, 2)
-        for start, end, target in zip([0] + ends, ends, grads):
-
-            @pl.when((k >= start) & (k < end))
+    def store_grad(k, then):
+        slot = lax.rem(k, 2)
+
+        @pl.when(k < early)
+        def _():
+            then(pltpu.make_async_copy(grad.at[slot], grads.at[at(k)], grad_sem.at[slot]))
+
+        if early < count:
+
+            @pl.when(k >= early)
             def _():
-                act_on(pltpu.make_async_copy(grad.at[slot], target.at[at(k - start)], grad_sem.at[slot]))
+                then(pltpu.make_async_copy(grad.at[slot], late_grads.at[at(k - early)], grad_sem.at[slot]))
 
     def remote(source, target, send, recv, device, axis="col"):
         return pltpu.make_async_remote_copy(
@@ -195,9 +198,36 @@
         return remote(pieces.at[source, at(k)], pieces.at[p, at(k)], send_sem.at[p, k], recv_sem.at[p, k], device)
 
     def early_hop(p, k):
-        source = grads[0] if p < 2 or p % 2 == 0 else landing[p - 1]
+        source = grads if p < 2 or p % 2 == 0 else landing[p - 1]
         device = chip_at(-(p // 2)) if p % 2 == 0 else sibling
         return remote(source.at[at(k)], landing[p].at[at(k)], early_send.at[p, k], early_recv.at[p, k], device)
+
+    def late_hop(k):
+        return remote(
+            late_grads.at[at(k - early)], late_near.at[at(k - early)], early_send.at[1, k], early_recv.at[1, k], sibling
+        )
+
+    def send_grad(k):
+        @pl.when(k < early)
+        def _():
+            for shift in range(1, outer):
+                early_hop(2 * shift, k).start()
+            early_hop(1, k).start()
+
+        if early < count:
+
+            @pl.when(k >= early)
+            def _():
+                late_hop(k).start()
+
+    def load_piece(p, k):
+        slot = lax.rem(k, 2)
+        source = landing[p] if p else grads
+        return pltpu.make_async_copy(source.at[at(k)], back.at[slot, p], back_sem.at[slot, p])
+
+    def store_back(k):
+        slot = lax.rem(k, 2)
+        return pltpu.make_async_copy(act.at[slot], back_out.at[at(k)], out_sem.at[slot])
 
     def share(shift):
         owner = lax.rem(chip - shift + outer, outer)
@@ -262,6 +292,7 @@
             stencil, inverse = stencil_of(adj[slot, part, :], seg[pl.ds(k * (tile // BLOCK) + b, 1), :])
             summed = jnp.dot(stencil, feat[slot, part, :], preferred_element_type=F32)
             target = pl.ds(pl.multiple_of(k * tile + b * BLOCK, BLOCK), BLOCK)
+            sten[target, :] = stencil
             pieces[0, target, :] = (summed * inverse).astype(BF16)
         for shift in range(1, outer):
             hop(2 * shift, k).start()
@@ -269,6 +300,8 @@
         return carry
 
     lax.fori_loop(0, count, aggregate_tile, 0)
+    stencil_copy = pltpu.make_async_copy(sten, stencil_out, fixed_sem.at[4])
+    stencil_copy.start()
     total[...] = jnp.zeros_like(total)
     fixed[1].wait()
     fixed[2].wait()
@@ -290,12 +323,7 @@
         def _():
             store_out(k - 2).wait()
             store_grad(k - 2, lambda copy: copy.wait())
-
-            @pl.when(k - 2 < early)
-            def _():
-                for shift in range(1, outer):
-                    early_hop(2 * shift, k - 2).start()
-                early_hop(1, k - 2).start()
+            send_grad(k - 2)
 
         preact = None
         for p in range(n):
@@ -350,57 +378,134 @@
     for k in (count - 2, count - 1):
         store_out(k).wait()
         store_grad(k, lambda copy: copy.wait())
-
-    def finish_early(k, carry):
-        for p in range(1, n):
-            if p == 1 or p % 2:
-                early_hop(p, k).wait_recv()
-            early_hop(p, k).wait_send()
+        send_grad(k)
+    for p in range(n):
+        if p % 2:
+            block(p).wait_recv()
+        else:
+            block(p).wait()
+    copies = [
+        pltpu.make_async_copy(blocks_out.at[p], mat.at[pl.ds(p * width, width)], block_send.at[p - p % 2])
+        for p in range(0, n, 2)
+    ] + [
+        pltpu.make_async_copy(blocks_out.at[p], mat.at[pl.ds(p * width, width)], block_recv.at[p])
+        for p in range(1, n, 2)
+    ]
+    for copy in copies:
+        copy.start()
+    for copy in copies:
+        copy.wait()
+
+    def backward_tile(k):
+        slot = lax.rem(k, 2)
+        for p in range(n):
+            load_piece(p, k).wait()
+
+        @pl.when(k >= 2)
+        def _():
+            store_back(k - 2).wait()
+
+        value = None
+        for p in range(n):
+            term = lax.dot_general(
+                back[slot, p], mat[pl.ds(p * width, width), :], (((1,), (1,)), ((), ())), preferred_element_type=F32
+            )
+            value = term if value is None else value + term
+        inverse = 1.0 / (jnp.sum(sten[at(k), :].astype(F32), axis=1, keepdims=True) - 1.0)
+        act[slot] = (value.astype(BF16).astype(F32) * inverse).astype(BF16)
+        store_back(k).start()
+
+    result = pltpu.make_async_copy(summed_total, total_out, fixed_sem.at[3])
+
+    def finish_sums():
+        sums.finish()
+        result.start()
+
+    def moment(r):
+        return max(r * 512 // tile, 0)
+
+    def back_step(k, carry):
+        @pl.when(k >= 1)
+        def _():
+            backward_tile(k - 1)
+
+        @pl.when(k < early)
+        def _():
+            for shift in range(1, outer):
+                early_hop(2 * shift, k).wait_recv()
+                early_hop(2 * shift + 1, k).start()
+            early_hop(1, k).wait_recv()
+            for shift in range(1, outer):
+                early_hop(2 * shift + 1, k).wait_recv()
+            for p in range(n):
+                load_piece(p, k).start()
+
+        for r in range(sums.rounds):
+            if moment(r) <= early:
+                pl.when(k == moment(r))(functools.partial(sums.advance, r))
+        if moment(sums.last) <= early:
+            pl.when(k == moment(sums.last))(finish_sums)
         return carry
+
+    lax.fori_loop(0, early + 1, back_step, 0)
+    for r in range(sums.rounds):
+        if moment(r) > early:
+            sums.advance(r)
+    if moment(sums.last) > early:
+        finish_sums()
+    for k in (early - 2, early - 1):
+        store_back(k).wait()
 
     def finish(k, carry):
         for p in range(1, n):
             hop(p, k).wait_send()
+
+        @pl.when(k < early)
+        def _():
+            for p in range(1, n):
+                early_hop(p, k).wait_send()
+
+        if early < count:
+
+            @pl.when(k >= early)
+            def _():
+                late_hop(k).wait()
+
         return carry
 
     lax.fori_loop(0, count, finish, 0)
-    for p in range(n):
-        if p % 2:
-            block(p).wait_send()
-            block(p).wait_recv()
-        else:
-            block(p).wait()
+    for p in range(1, n, 2):
+        block(p).wait_send()
     for shift in range(1, outer):
         share(shift).wait_send()
         for peer in others:
             spread(shift, cluster, peer).wait_send()
-    for k in range(max(early, sums.rounds)):
-        if k < early:
-            for shift in range(1, outer):
-                early_hop(2 * shift, k).wait_recv()
-                early_hop(2 * shift + 1, k).start()
-        sums.advance(k)
-    sums.finish()
-    result = pltpu.make_async_copy(summed_total, total_out, fixed_sem.at[3])
-    result.start()
-    lax.fori_loop(0, early, finish_early, 0)
+    stencil_copy.wait()
     result.wait()
 
 
-def exchange(features, adjacency, cotangent, segments, weight, bias, n, clusters, groups, tile):
+def exchange(features, adjacency, cotangent, segments, weight, bias, n, clusters, early, tile):
     rows, width = features.shape
     depth = weight.shape[0]
     count, outer = rows // tile, n // 2
-    early = groups[0]
+    late = max(count - early, 1)
     parts, high = cluster_sum.PARTS, clusters // 2
     dma = pltpu.SemaphoreType.DMA
     array = jax.ShapeDtypeStruct
     return pl.pallas_call(
-        functools.partial(exchange_kernel, n, clusters, groups, tile),
+        functools.partial(exchange_kernel, n, clusters, early, tile),
         in_specs=[ANY] * 6,
-        out_specs=[ANY] * (2 + n + len(groups)),
-        out_shape=[array((rows, width), BF16), array((depth + 8, width), F32), array((n, width, width), BF16)]
-        + [array((group * tile, width), BF16) for group in groups]
+        out_specs=[ANY] * (7 + n),
+        out_shape=[
+            array((rows, width), BF16),
+            array((depth + 8, width), F32),
+            array((n, width, width), BF16),
+            array((rows, BLOCK), BF16),
+            array((early * tile, width), BF16),
+            array((early * tile, width), BF16),
+            array((late * tile, width), BF16),
+            array((late * tile, width), BF16),
+        ]
         + [array((early * tile, width), BF16)] * (n - 1),
         scratch_shapes=[
             pltpu.VMEM((n, rows, width), BF16),
@@ -410,19 +515,22 @@
             pltpu.VMEM((2, tile, width), BF16),
             pltpu.VMEM((2, tile, width), BF16),
             pltpu.VMEM(segments.shape, jnp.int32),
+            pltpu.VMEM((rows, BLOCK), BF16),
             pltpu.VMEM((depth, width), BF16),
             pltpu.VMEM((1, width), BF16),
             pltpu.VMEM((depth + 8, width), F32),
             pltpu.VMEM((outer, 2 * width, width), BF16),
+            pltpu.VMEM((2, n, tile, width), BF16),
             dma((2, 2)),
             dma((2,)),
             dma((2,)),
             dma((2,)),
-            dma((4,)),
+            dma((5,)),
             dma((n, count)),
             dma((n, count)),
-            dma((n, early)),
-            dma((n, early)),
+            dma((n, count)),
+            dma((n, count)),
+            dma((2, n)),
             dma((outer,)),
             dma((outer,)),
             dma((outer, clusters)),
@@ -439,118 +547,48 @@
             ],
         ],
         compiler_params=pltpu.CompilerParams(
-            collective_id=0, has_side_effects=True, vmem_limit_bytes=62 << 20
+            collective_id=0, has_side_effects=True, vmem_limit_bytes=63 << 20
         ),
     )(features, adjacency, cotangent, segments, weight, bias)
 
 
-def backward_kernel(n, first, tile, *refs):
-    grads, (weights, adjacency, segments), out = refs[:n], refs[n : n + 3], refs[-2]
-    refs[-1][...] = jnp.zeros_like(refs[-1])
-    step = pl.program_id(0)
-    grad = None
-    for p in range(n):
-        term = lax.dot_general(
-            grads[p][...], weights[p], (((1,), (1,)), ((), ())), preferred_element_type=F32
-        )
-        grad = term if grad is None else grad + term
-    grad = grad.astype(BF16)
-    for b in range(tile // BLOCK):
-        rows = pl.ds(b * BLOCK, BLOCK)
-        index = first // BLOCK + step * (tile // BLOCK) + b
-        stencil, inverse = stencil_of(adjacency[rows, :], segments[pl.ds(index, 1), :])
-        summed = (grad[b * BLOCK : (b + 1) * BLOCK].astype(F32) * inverse).astype(BF16)
-        out[rows, :] = jnp.dot(stencil, summed, preferred_element_type=F32)
-
-
-def backward(grads, weights, adjacency, segments, carried, first, size, *earlier):
-    n, width = len(grads), weights.shape[1]
-    rows = adjacency.shape[0]
-    tile = min(size, 512)
-    offset = first // tile
-
-    def rows_from(base):
-        return pl.BlockSpec((tile, width), lambda i: (base // tile + i, 0))
-
-    in_specs = (
-        [rows_from(base) for _, base in grads]
-        + [whole(weights.shape)]
-        + [pl.BlockSpec((tile, BLOCK), lambda i: (offset + i, 0)), whole(segments.shape)]
-    )
-    operands = [x for x, _ in grads] + [weights, adjacency, segments]
-    aliases = {}
-    if carried is not None:
-        in_specs.append(ANY)
-        aliases = {len(operands): 0}
-        operands.append(carried)
-    in_specs += [ANY] * len(earlier)
-    operands += earlier
+def finish_kernel(steps, stencil, back, out_in, total, bias, grad_features, out, grad_weight, grad_bias):
+    @pl.when(pl.program_id(0) < steps)
+    def _():
+        for b in range(back.shape[0] // BLOCK):
+            rows = pl.ds(b * BLOCK, BLOCK)
+            grad_features[rows, :] = jnp.dot(stencil[rows, :], back[rows, :], preferred_element_type=F32)
+
+    out[...] = out_in[...]
+    grad_weight[...] = total[...]
+    grad_bias[...] = jnp.broadcast_to(jnp.sum(bias[...], axis=0, keepdims=True), bias.shape)
+
+
+def finish(stencil, back, out, total):
+    rows, width = out.shape
+    depth = total.shape[0] - 8
+    tile = 1024
+    steps, grid = back.shape[0] // tile, rows // tile
+    part = depth // grid
+    every = lambda size: pl.BlockSpec((size, width), lambda i: (i, 0))
+    first = lambda size: pl.BlockSpec((tile, size), lambda i: (jnp.minimum(i, steps - 1), 0))
+    fixed = lambda index: pl.BlockSpec((8, width), lambda i: (index, 0))
     return pl.pallas_call(
-        functools.partial(backward_kernel, n, first, tile),
-        grid=(size // tile,),
-        in_specs=in_specs,
-        out_specs=[pl.BlockSpec((tile, width), lambda i: (offset + i, 0)), whole((8, BLOCK))],
-        out_shape=[jax.ShapeDtypeStruct((rows, width), F32), jax.ShapeDtypeStruct((8, BLOCK), F32)],
-        input_output_aliases=aliases,
-        cost_estimate=SMALL,
+        functools.partial(finish_kernel, steps),
+        grid=(grid,),
+        in_specs=[first(BLOCK), first(width), every(tile), every(part), fixed(depth // 8)],
+        out_specs=[first(width), every(tile), every(part), fixed(0)],
+        out_shape=[
+            jax.ShapeDtypeStruct((rows, width), F32),
+            jax.ShapeDtypeStruct((rows, width), BF16),
+            jax.ShapeDtypeStruct((depth, width), F32),
+            jax.ShapeDtypeStruct((8, width), F32),
+        ],
+        cost_estimate=pl.CostEstimate(
+            flops=2 * rows * BLOCK * width, bytes_accessed=10 * rows * width + 8 * depth * width, transcendentals=0
+        ),
         compiler_params=params(),
-    )(*operands)
-
-
-def copy_kernel(source, earlier, target):
-    target[...] = source[...]
-
-
-def copied(x, earlier):
-    rows, width = x.shape
-    spec = pl.BlockSpec((1024, width), lambda i: (i, 0))
-    return pl.pallas_call(
-        copy_kernel,
-        grid=(rows // 1024,),
-        in_specs=[spec, ANY],
-        out_specs=spec,
-        out_shape=jax.ShapeDtypeStruct(x.shape, x.dtype),
-        cost_estimate=SMALL,
-        compiler_params=params(),
-    )(x, earlier)
-
-
-def tie_kernel(*refs):
-    pass
-
-
-def tie(x, *earlier):
-    return pl.pallas_call(
-        tie_kernel,
-        in_specs=[ANY] * (1 + len(earlier)),
-        out_specs=ANY,
-        out_shape=jax.ShapeDtypeStruct(x.shape, x.dtype),
-        input_output_aliases={0: 0},
-        cost_estimate=SMALL,
-    )(x, *earlier)
-
-
-def split_kernel(total, earlier, grad_weight, grad_bias):
-    depth, width = grad_weight.shape
-    grad_weight[...] = total[pl.ds(0, depth), :]
-    grad_bias[...] = jnp.broadcast_to(jnp.sum(total[pl.ds(depth, 8), :], axis=0, keepdims=True), (8, width))
-
-
-def split(total, earlier):
-    rows, width = total.shape
-    return pl.pallas_call(
-        split_kernel,
-        grid=(1,),
-        in_specs=[whole(total.shape), ANY],
-        out_specs=[whole((rows - 8, width)), whole((8, width))],
-        out_shape=[jax.ShapeDtypeStruct((rows - 8, width), F32), jax.ShapeDtypeStruct((8, width), F32)],
-        cost_estimate=SMALL,
-        compiler_params=params(),
-    )(total, earlier)
-
-
-def tile_groups(count):
-    return [count - 5, 3, 1, 1]
+    )(stencil, back, out, total, total)
 
 
 def build(n, clusters):
@@ -568,33 +606,12 @@
 
     def local(features, weight, bias, adjacency, segments, cotangent):
         rows, width = features.shape
-        tile = 512
-        groups = tile_groups(rows // tile)
-        out, total, blocks, *rest = exchange(
-            features, adjacency, cotangent, segments, weight, bias.reshape(1, width), n, clusters, groups, tile
-        )
-        grads, landing = rest[: len(groups)], rest[len(groups) :]
-        own = grads[1:-1] + [grads[-1][: tile // 2], grads[-1][tile // 2 :]]
-        near, far = [], []
-        for k, x in enumerate(own):
-            if k:
-                x = own[k] = tie(x, near[-1])
-            near.append(from_sibling(x))
-            far.append([from_chip(x, shift) for shift in range(1, outer)])
-        out = copied(out, near[-1])
-        grad_weight, grad_bias = split(total, out)
-        first = groups[0] * tile
-        grad_features, token = backward(
-            [(x, 0) for x in [grads[0]] + landing], blocks, adjacency, segments, None, 0, first, grad_bias
-        )
-        for k, x in enumerate(own):
-            parts = [(x, 0), (near[k], 0)]
-            for y in far[k]:
-                y = tie(y, token)
-                parts += [(y, 0), (from_sibling(y), 0)]
-            size = x.shape[0]
-            grad_features, token = backward(parts, blocks, adjacency, segments, grad_features, first, size)
-            first += size
+        tile = 256 if n <= 4 else 512
+        early = rows // tile
+        out, total, blocks, stencil, back, *rest = exchange(
+            features, adjacency, cotangent, segments, weight, bias.reshape(1, width), n, clusters, early, tile
+        )
+        grad_features, out, grad_weight, grad_bias = finish(stencil, back, out, total)
         return (out, grad_features, grad_weight, grad_bias[0])
 
     return local

time: 424 us -> 405 us (0.955)
  waiting for transfers between devices: 16.7 us -> 0 us
  Pallas kernels: 384 us -> 399 us
  local copies, waits for them, and re-layouts: 14.5 us -> 2.56 us
    ppermute x12 -> x0, waiting for transfers between devices: 16.7 us -> none  [the longest x8 12.1 us: from_sibling(): return lax.ppermute(x, 'col', [(i, i ^ 1) for i in range(n)])]
    pallas_call x15 -> x2, Pallas kernels: 384 us -> 399 us  [the longest x1 380 us: exchange(): pl.pallas_call(functools.partial(exchange_kernel, n, clusters, early, til...]
    unnamed x30 -> x0, local copies, waits for them, and re-layouts: 10.1 us -> none
  transfers between devices with their start and end apart: 12 -> 0, of which waited for: 11 -> 0; matrix products, arithmetic and copies ran while one was open for 1% -> 0% of each run, Pallas kernels for 13% -> 0%
where the time goes in v3:
time: 405 us; the launch traced here: 403 us
  Pallas kernels  399 us (99%)
    pallas_call x1, Pallas kernels, exchange(): pl.pallas_call(functools.partial(exchange_kernel, n, clusters, early, til...  380 us
    pallas_call x1, Pallas kernels, finish(): pl.pallas_call(functools.partial(finish_kernel, steps), grid=(grid,), in_...  19 us

profile of v3, /device:TPU:0, one launch (start us, length us, event | category | flops | bytes accessed | tf_op | source)
XLA Modules:
  0.0 402.6 jit_solution(10391433281005134885)
XLA Ops:
  0.6 1.3 reshape.11.bias
  1.9 380.4 %shard_map.93 = (bf16[8192,512]{1,0:T(8,128)(2,1)}, f32[2056,512]{1,0:T(8,128)}, bf16[4,512,512]{2,1,0:T(8,128)(2,1)}, bf16[8192,128]{1,0:T(8,128)(2,1)}, bf16[8...) custom-call(bf16[8192,512]{1,0:T(8,128)(2,1)} %features.1, ...), custom_call_target="tpu_custom_call" | custom-call | tf_op jit(solution)/shard_map/pallas_call | solution.py:495
  382.3 19.0 %shard_map.94 = (f32[8192,512]{1,0:T(8,128)}, bf16[8192,512]{1,0:T(8,128)(2,1)}, f32[2048,512]{1,0:T(8,128)}, f32[8,512]{1,0:T(8,128)}) custom-call(bf16[8192,128]{1,0:T(8,128)(2,1)} %get-tuple-element.12.stencil, bf16[8192,512]{1,0:T(8,128)(2,1)} %get-tuple-element.13.back, bf16[8192,512]{1,0:T(8,128)(2,1)} %get-tuple-element.14.out_in, ...), custom_call_target="tpu_custom_call" | custom-call | flops 1073741824 | bytes 50331648 | tf_op jit(solution)/shard_map/pallas_call | solution.py:576
  401.3 1.3 slice.3

commit v4 on v3

--- a/solution.py
+++ b/solution.py
@@ -8,19 +8,12 @@
 from jax.sharding import PartitionSpec as P
 
 BLOCK = 128
+SLOTS = 4
 F32 = jnp.float32
 BF16 = jnp.bfloat16
 MESH = pl.DeviceIdType.MESH
-SMALL = pl.CostEstimate(flops=1000, bytes_accessed=1000, transcendentals=0)
-ANY = pl.BlockSpec(memory_space=pl.ANY)
-
-
-def params():
-    return pltpu.CompilerParams(dimension_semantics=("arbitrary",), vmem_limit_bytes=56 << 20)
-
-
-def whole(shape):
-    return pl.BlockSpec(shape, lambda *_: (0,) * len(shape))
+HBM = pl.BlockSpec(memory_space=pltpu.HBM)
+VMEM = pl.BlockSpec(memory_space=pltpu.VMEM)
 
 
 def stencil_of(adjacency, segment):
@@ -136,13 +129,15 @@
 
 
 def exchange_kernel(
-    n, clusters, early, tile, features, adjacency, cotangent, segments, weight, bias,
-    out, total_out, blocks_out, stencil_out, back_out, grads, late_grads, late_near, *rest,
+    n, clusters, tile, features, adjacency, cotangent, segments, weight, bias,
+    activations, scaled, summed_total, sten, blocks_out, grads, *rest,
 ):
     landing = (None,) + rest[: n - 1]
-    (pieces, feat, adj, cot, act, grad, seg, sten, mat, vec, total, shares, back, load_sem, cot_sem, out_sem, grad_sem,
-     fixed_sem, send_sem, recv_sem, early_send, early_recv, back_sem, share_send, share_recv, spread_send, spread_recv,
-     block_send, block_recv, summed_total, half_in, quarter_in, bias_in, sum_sems) = rest[n - 1 :]
+    pieces = list(rest[n - 1 : 2 * n - 3])
+    pieces = pieces[:1] + [activations] + pieces[1:] + [scaled]
+    (feat, adj, cot, grad, seg, mat, vec, total, shares, back, load_sem, cot_sem, grad_sem,
+     fixed_sem, send_sem, recv_sem, grad_out, grad_in, back_sem, share_send, share_recv, spread_send, spread_recv,
+     block_send, block_recv, half_in, quarter_in, bias_in, sum_sems) = rest[2 * n - 3 :]
     outer = n // 2
     rows, width = features.shape
     depth = mat.shape[0]
@@ -169,22 +164,9 @@
         slot = lax.rem(k, 2)
         return pltpu.make_async_copy(cotangent.at[at(k)], cot.at[slot], cot_sem.at[slot])
 
-    def store_out(k):
-        slot = lax.rem(k, 2)
-        return pltpu.make_async_copy(act.at[slot], out.at[at(k)], out_sem.at[slot])
-
-    def store_grad(k, then):
-        slot = lax.rem(k, 2)
-
-        @pl.when(k < early)
-        def _():
-            then(pltpu.make_async_copy(grad.at[slot], grads.at[at(k)], grad_sem.at[slot]))
-
-        if early < count:
-
-            @pl.when(k >= early)
-            def _():
-                then(pltpu.make_async_copy(grad.at[slot], late_grads.at[at(k - early)], grad_sem.at[slot]))
+    def store_grad(k):
+        slot = lax.rem(k, 2)
+        return pltpu.make_async_copy(grad.at[slot], grads.at[at(k)], grad_sem.at[slot])
 
     def remote(source, target, send, recv, device, axis="col"):
         return pltpu.make_async_remote_copy(
@@ -195,39 +177,22 @@
     def hop(p, k):
         source = 0 if p % 2 == 0 else p - 1
         device = chip_at(-(p // 2)) if p % 2 == 0 else sibling
-        return remote(pieces.at[source, at(k)], pieces.at[p, at(k)], send_sem.at[p, k], recv_sem.at[p, k], device)
-
-    def early_hop(p, k):
+        return remote(pieces[source].at[at(k)], pieces[p].at[at(k)], send_sem.at[p, k], recv_sem.at[p, k], device)
+
+    def grad_hop(p, k):
         source = grads if p < 2 or p % 2 == 0 else landing[p - 1]
         device = chip_at(-(p // 2)) if p % 2 == 0 else sibling
-        return remote(source.at[at(k)], landing[p].at[at(k)], early_send.at[p, k], early_recv.at[p, k], device)
-
-    def late_hop(k):
-        return remote(
-            late_grads.at[at(k - early)], late_near.at[at(k - early)], early_send.at[1, k], early_recv.at[1, k], sibling
-        )
+        return remote(source.at[at(k)], landing[p].at[at(k)], grad_out.at[p, k], grad_in.at[p, k], device)
 
     def send_grad(k):
-        @pl.when(k < early)
-        def _():
-            for shift in range(1, outer):
-                early_hop(2 * shift, k).start()
-            early_hop(1, k).start()
-
-        if early < count:
-
-            @pl.when(k >= early)
-            def _():
-                late_hop(k).start()
+        for shift in range(1, outer):
+            grad_hop(2 * shift, k).start()
+        grad_hop(1, k).start()
 
     def load_piece(p, k):
         slot = lax.rem(k, 2)
         source = landing[p] if p else grads
         return pltpu.make_async_copy(source.at[at(k)], back.at[slot, p], back_sem.at[slot, p])
-
-    def store_back(k):
-        slot = lax.rem(k, 2)
-        return pltpu.make_async_copy(act.at[slot], back_out.at[at(k)], out_sem.at[slot])
 
     def share(shift):
         owner = lax.rem(chip - shift + outer, outer)
@@ -293,15 +258,13 @@
             summed = jnp.dot(stencil, feat[slot, part, :], preferred_element_type=F32)
             target = pl.ds(pl.multiple_of(k * tile + b * BLOCK, BLOCK), BLOCK)
             sten[target, :] = stencil
-            pieces[0, target, :] = (summed * inverse).astype(BF16)
+            pieces[0][target, :] = (summed * inverse).astype(BF16)
         for shift in range(1, outer):
             hop(2 * shift, k).start()
         hop(1, k).start()
         return carry
 
     lax.fori_loop(0, count, aggregate_tile, 0)
-    stencil_copy = pltpu.make_async_copy(sten, stencil_out, fixed_sem.at[4])
-    stencil_copy.start()
     total[...] = jnp.zeros_like(total)
     fixed[1].wait()
     fixed[2].wait()
@@ -321,28 +284,26 @@
 
         @pl.when(k >= 2)
         def _():
-            store_out(k - 2).wait()
-            store_grad(k - 2, lambda copy: copy.wait())
+            store_grad(k - 2).wait()
             send_grad(k - 2)
 
         preact = None
         for p in range(n):
             source = pl.ds(pl.multiple_of(blocks[p] * width, width), width)
-            term = jnp.dot(pieces[p, at(k), :], mat[source, :], preferred_element_type=F32)
+            term = jnp.dot(pieces[p][at(k), :], mat[source, :], preferred_element_type=F32)
             preact = term if preact is None else preact + term
-        preact = preact + vec[...].astype(F32)
-        act[slot] = jnp.maximum(preact, 0.0).astype(BF16)
+        preact = preact + vec[...].astype(F32).reshape(1, width)
         grad_preact = jnp.where(preact > 0.0, cot[slot].astype(F32), 0.0)
         total[pl.ds(depth, 8), :] += jnp.sum(grad_preact.reshape(tile // 8, 8, width), axis=0)
         grad_preact = grad_preact.astype(BF16)
         grad[slot] = grad_preact
-        store_out(k).start()
-        store_grad(k, lambda copy: copy.start())
+        store_grad(k).start()
         for p in range(n):
             target = pl.ds(pl.multiple_of(blocks[p] * width, width), width)
             total[target, :] += lax.dot_general(
-                pieces[p, at(k), :], grad_preact, (((0,), (0,)), ((), ())), preferred_element_type=F32
+                pieces[p][at(k), :], grad_preact, (((0,), (0,)), ((), ())), preferred_element_type=F32
             )
+        activations[at(k), :] = jnp.maximum(preact, 0.0).astype(BF16)
 
     def step(k, carry):
         @pl.when(k < count)
@@ -376,8 +337,7 @@
     sums = cluster_sum(total, summed_total, half_in, quarter_in, bias_in, sum_sems, clusters)
     sums.start()
     for k in (count - 2, count - 1):
-        store_out(k).wait()
-        store_grad(k, lambda copy: copy.wait())
+        store_grad(k).wait()
         send_grad(k)
     for p in range(n):
         if p % 2:
@@ -401,10 +361,6 @@
         for p in range(n):
             load_piece(p, k).wait()
 
-        @pl.when(k >= 2)
-        def _():
-            store_back(k - 2).wait()
-
         value = None
         for p in range(n):
             term = lax.dot_general(
@@ -412,14 +368,7 @@
             )
             value = term if value is None else value + term
         inverse = 1.0 / (jnp.sum(sten[at(k), :].astype(F32), axis=1, keepdims=True) - 1.0)
-        act[slot] = (value.astype(BF16).astype(F32) * inverse).astype(BF16)
-        store_back(k).start()
-
-    result = pltpu.make_async_copy(summed_total, total_out, fixed_sem.at[3])
-
-    def finish_sums():
-        sums.finish()
-        result.start()
+        scaled[at(k), :] = (value.astype(BF16).astype(F32) * inverse).astype(BF16)
 
     def moment(r):
         return max(r * 512 // tile, 0)
@@ -429,48 +378,35 @@
         def _():
             backward_tile(k - 1)
 
-        @pl.when(k < early)
+        @pl.when(k < count)
         def _():
             for shift in range(1, outer):
-                early_hop(2 * shift, k).wait_recv()
-                early_hop(2 * shift + 1, k).start()
-            early_hop(1, k).wait_recv()
+                grad_hop(2 * shift, k).wait_recv()
+                grad_hop(2 * shift + 1, k).start()
+            grad_hop(1, k).wait_recv()
             for shift in range(1, outer):
-                early_hop(2 * shift + 1, k).wait_recv()
+                grad_hop(2 * shift + 1, k).wait_recv()
             for p in range(n):
                 load_piece(p, k).start()
 
         for r in range(sums.rounds):
-            if moment(r) <= early:
+            if moment(r) <= count:
                 pl.when(k == moment(r))(functools.partial(sums.advance, r))
-        if moment(sums.last) <= early:
-            pl.when(k == moment(sums.last))(finish_sums)
+        if moment(sums.last) <= count:
+            pl.when(k == moment(sums.last))(sums.finish)
         return carry
 
-    lax.fori_loop(0, early + 1, back_step, 0)
+    lax.fori_loop(0, count + 1, back_step, 0)
     for r in range(sums.rounds):
-        if moment(r) > early:
+        if moment(r) > count:
             sums.advance(r)
-    if moment(sums.last) > early:
-        finish_sums()
-    for k in (early - 2, early - 1):
-        store_back(k).wait()
+    if moment(sums.last) > count:
+        sums.finish()
 
     def finish(k, carry):
         for p in range(1, n):
             hop(p, k).wait_send()
-
-        @pl.when(k < early)
-        def _():
-            for p in range(1, n):
-                early_hop(p, k).wait_send()
-
-        if early < count:
-
-            @pl.when(k >= early)
-            def _():
-                late_hop(k).wait()
-
+            grad_hop(p, k).wait_send()
         return carry
 
     lax.fori_loop(0, count, finish, 0)
@@ -480,52 +416,43 @@
         share(shift).wait_send()
         for peer in others:
             spread(shift, cluster, peer).wait_send()
-    stencil_copy.wait()
-    result.wait()
-
-
-def exchange(features, adjacency, cotangent, segments, weight, bias, n, clusters, early, tile):
+
+
+def exchange(features, adjacency, cotangent, segments, weight, bias, n, clusters, tile):
     rows, width = features.shape
     depth = weight.shape[0]
     count, outer = rows // tile, n // 2
-    late = max(count - early, 1)
     parts, high = cluster_sum.PARTS, clusters // 2
     dma = pltpu.SemaphoreType.DMA
     array = jax.ShapeDtypeStruct
     return pl.pallas_call(
-        functools.partial(exchange_kernel, n, clusters, early, tile),
-        in_specs=[ANY] * 6,
-        out_specs=[ANY] * (7 + n),
+        functools.partial(exchange_kernel, n, clusters, tile),
+        in_specs=[HBM] * 6,
+        out_specs=[VMEM] * 4 + [HBM] * (n + 1),
         out_shape=[
-            array((rows, width), BF16),
-            array((depth + 8, width), F32),
+            pltpu.VMEM((rows, width), BF16),
+            pltpu.VMEM((rows, width), BF16),
+            pltpu.VMEM((depth + 8, width), F32),
+            pltpu.VMEM((rows, BLOCK), BF16),
             array((n, width, width), BF16),
-            array((rows, BLOCK), BF16),
-            array((early * tile, width), BF16),
-            array((early * tile, width), BF16),
-            array((late * tile, width), BF16),
-            array((late * tile, width), BF16),
         ]
-        + [array((early * tile, width), BF16)] * (n - 1),
-        scratch_shapes=[
-            pltpu.VMEM((n, rows, width), BF16),
+        + [array((rows, width), BF16)] * n,
+        scratch_shapes=[pltpu.VMEM((rows, width), BF16)] * (n - 2)
+        + [
             pltpu.VMEM((2, tile, width), BF16),
             pltpu.VMEM((2, tile, BLOCK), jnp.int32),
             pltpu.VMEM((2, tile, width), BF16),
             pltpu.VMEM((2, tile, width), BF16),
-            pltpu.VMEM((2, tile, width), BF16),
             pltpu.VMEM(segments.shape, jnp.int32),
-            pltpu.VMEM((rows, BLOCK), BF16),
             pltpu.VMEM((depth, width), BF16),
-            pltpu.VMEM((1, width), BF16),
+            pltpu.VMEM((width,), BF16),
             pltpu.VMEM((depth + 8, width), F32),
             pltpu.VMEM((outer, 2 * width, width), BF16),
             pltpu.VMEM((2, n, tile, width), BF16),
             dma((2, 2)),
             dma((2,)),
             dma((2,)),
-            dma((2,)),
-            dma((5,)),
+            dma((3,)),
             dma((n, count)),
             dma((n, count)),
             dma((n, count)),
@@ -537,7 +464,6 @@
             dma((outer, clusters)),
             dma((n,)),
             dma((n,)),
-            pltpu.VMEM((depth + 8, width), F32),
             pltpu.VMEM((parts, depth // parts // 2, width), F32),
             pltpu.VMEM((parts, high, depth // parts // 2 // high, width), F32),
             pltpu.VMEM((clusters, 8, width), F32),
@@ -547,72 +473,85 @@
             ],
         ],
         compiler_params=pltpu.CompilerParams(
-            collective_id=0, has_side_effects=True, vmem_limit_bytes=63 << 20
+            collective_id=0, has_side_effects=True, vmem_limit_bytes=40 << 20
         ),
-    )(features, adjacency, cotangent, segments, weight, bias)
-
-
-def finish_kernel(steps, stencil, back, out_in, total, bias, grad_features, out, grad_weight, grad_bias):
-    @pl.when(pl.program_id(0) < steps)
-    def _():
-        for b in range(back.shape[0] // BLOCK):
-            rows = pl.ds(b * BLOCK, BLOCK)
-            grad_features[rows, :] = jnp.dot(stencil[rows, :], back[rows, :], preferred_element_type=F32)
-
-    out[...] = out_in[...]
-    grad_weight[...] = total[...]
-    grad_bias[...] = jnp.broadcast_to(jnp.sum(bias[...], axis=0, keepdims=True), bias.shape)
-
-
-def finish(stencil, back, out, total):
-    rows, width = out.shape
+    )(*[pltpu.with_memory_space_constraint(x, pltpu.HBM) for x in (features, adjacency, cotangent, segments, weight, bias)])
+
+
+def finish_kernel(tile, activations, scaled, total, stencil, grad_features, out, grad_weight, grad_bias, slots, row, slot_sem, fixed_sem):
+    rows, width = scaled.shape
     depth = total.shape[0] - 8
-    tile = 1024
-    steps, grid = back.shape[0] // tile, rows // tile
-    part = depth // grid
-    every = lambda size: pl.BlockSpec((size, width), lambda i: (i, 0))
-    first = lambda size: pl.BlockSpec((tile, size), lambda i: (jnp.minimum(i, steps - 1), 0))
-    fixed = lambda index: pl.BlockSpec((8, width), lambda i: (index, 0))
+    count = rows // tile
+    row[...] = jnp.sum(total[pl.ds(depth, 8), :], axis=0, keepdims=True)
+    fixed = [
+        pltpu.make_async_copy(activations, out, fixed_sem.at[0]),
+        pltpu.make_async_copy(total.at[pl.ds(0, depth)], grad_weight, fixed_sem.at[1]),
+        pltpu.make_async_copy(row, grad_bias, fixed_sem.at[2]),
+    ]
+    for copy in fixed:
+        copy.start()
+
+    def store(k):
+        slot = lax.rem(k, SLOTS)
+        target = pl.ds(pl.multiple_of(k * tile, tile), tile)
+        return pltpu.make_async_copy(slots.at[slot], grad_features.at[target], slot_sem.at[slot])
+
+    def step(k, carry):
+        slot = lax.rem(k, SLOTS)
+
+        @pl.when(k >= SLOTS)
+        def _():
+            store(k - SLOTS).wait()
+
+        for b in range(tile // BLOCK):
+            source = pl.ds(pl.multiple_of(k * tile + b * BLOCK, BLOCK), BLOCK)
+            slots[slot, pl.ds(b * BLOCK, BLOCK), :] = jnp.dot(
+                stencil[source, :], scaled[source, :], preferred_element_type=F32
+            )
+        store(k).start()
+        return carry
+
+    lax.fori_loop(0, count, step, 0)
+    for k in range(max(count - SLOTS, 0), count):
+        store(k).wait()
+    for copy in fixed:
+        copy.wait()
+
+
+def finish(activations, scaled, total, stencil):
+    rows, width = scaled.shape
+    depth = total.shape[0] - 8
+    tile = 512
+    dma = pltpu.SemaphoreType.DMA
     return pl.pallas_call(
-        functools.partial(finish_kernel, steps),
-        grid=(grid,),
-        in_specs=[first(BLOCK), first(width), every(tile), every(part), fixed(depth // 8)],
-        out_specs=[first(width), every(tile), every(part), fixed(0)],
+        functools.partial(finish_kernel, tile),
+        in_specs=[VMEM] * 4,
+        out_specs=[HBM] * 4,
         out_shape=[
             jax.ShapeDtypeStruct((rows, width), F32),
             jax.ShapeDtypeStruct((rows, width), BF16),
             jax.ShapeDtypeStruct((depth, width), F32),
-            jax.ShapeDtypeStruct((8, width), F32),
+            jax.ShapeDtypeStruct((1, width), F32),
+        ],
+        scratch_shapes=[
+            pltpu.VMEM((SLOTS, tile, width), F32),
+            pltpu.VMEM((1, width), F32),
+            dma((SLOTS,)),
+            dma((3,)),
         ],
         cost_estimate=pl.CostEstimate(
-            flops=2 * rows * BLOCK * width, bytes_accessed=10 * rows * width + 8 * depth * width, transcendentals=0
+            flops=2 * rows * BLOCK * width, bytes_accessed=6 * rows * width + 4 * depth * width, transcendentals=0
         ),
-        compiler_params=params(),
-    )(stencil, back, out, total, total)
+        compiler_params=pltpu.CompilerParams(vmem_limit_bytes=12 << 20),
+    )(activations, scaled, total, stencil)
 
 
 def build(n, clusters):
-    outer = n // 2
-
-    def device(chip, core):
-        return (chip % outer) * 2 + core
-
-    def from_chip(x, shift):
-        pairs = [(device(chip + shift, core), device(chip, core)) for chip in range(outer) for core in range(2)]
-        return lax.ppermute(x, "col", pairs)
-
-    def from_sibling(x):
-        return lax.ppermute(x, "col", [(i, i ^ 1) for i in range(n)])
-
     def local(features, weight, bias, adjacency, segments, cotangent):
-        rows, width = features.shape
         tile = 256 if n <= 4 else 512
-        early = rows // tile
-        out, total, blocks, stencil, back, *rest = exchange(
-            features, adjacency, cotangent, segments, weight, bias.reshape(1, width), n, clusters, early, tile
-        )
-        grad_features, out, grad_weight, grad_bias = finish(stencil, back, out, total)
-        return (out, grad_features, grad_weight, grad_bias[0])
+        held = exchange(features, adjacency, cotangent, segments, weight, bias, n, clusters, tile)[:4]
+        grad_features, out, grad_weight, grad_bias = finish(*held)
+        return (out, grad_features, grad_weight, grad_bias.reshape(-1))
 
     return local
 

time: 405 us -> 392 us (0.968)
  Pallas kernels: 399 us -> 390 us
    pallas_call x2, Pallas kernels: 399 us -> 390 us  [the longest x1 380 us: exchange(): pl.pallas_call(functools.partial(exchange_kernel, n, clusters, tile), in_...]
where the time goes in v4:
time: 392 us; the launch traced here: 390 us
  Pallas kernels  390 us (99%)
    pallas_call x1, Pallas kernels, exchange(): pl.pallas_call(functools.partial(exchange_kernel, n, clusters, tile), in_...  380 us
    pallas_call x1, Pallas kernels, finish(): pl.pallas_call(functools.partial(finish_kernel, tile), in_specs=[VMEM] *...  9.79 us

profile of v4, /device:TPU:0, one launch (start us, length us, event | category | flops | bytes accessed | tf_op | source)
XLA Modules:
  0.0 390.2 jit_solution(8268264273468990233)
XLA Ops:
  0.6 379.8 %shard_map.93 = (bf16[8192,512]{1,0:T(8,128)(2,1)S(1)}, bf16[8192,512]{1,0:T(8,128)(2,1)S(1)}, f32[2056,512]{1,0:T(8,128)S(1)}, bf16[8192,128]{1,0:T(8,128)(2,1)...) custom-call(bf16[8192,512]{1,0:T(8,128)(2,1)} %features.1, ...), custom_call_target="tpu_custom_call" | custom-call | tf_op jit(solution)/shard_map/pallas_call | solution.py:428
  380.4 9.8 %shard_map.94 = (f32[8192,512]{1,0:T(8,128)}, bf16[8192,512]{1,0:T(8,128)(2,1)}, f32[2048,512]{1,0:T(8,128)}, f32[1,512]{1,0:T(1,128)}) custom-call(bf16[8192,512]{1,0:T(8,128)(2,1)S(1)} %get-tuple-element.12.activations, bf16[8192,512]{1,0:T(8,128)(2,1)S(1)} %get-tuple-element.13.scaled, f32[2056,512]{1,0:T(8,128)S(1)} %get-tuple-element.14.total, ...), custom_call_target="tpu_custom_call" | custom-call | flops 1073741824 | bytes 29360128 | tf_op jit(solution)/shard_map/pallas_call | solution.py:526

commit v5 on v4

--- a/solution.py
+++ b/solution.py
@@ -23,6 +23,18 @@
     row = lax.broadcasted_iota(jnp.int32, (BLOCK, BLOCK), 0)
     column = lax.broadcasted_iota(jnp.int32, (BLOCK, BLOCK), 1)
     return (links + jnp.where(row == column, 2.0, 0.0)).astype(BF16), inverse
+
+
+def back_through(piece, n, blocks, stencil):
+    width = blocks.shape[1]
+    value = None
+    for p in range(n):
+        term = lax.dot_general(
+            piece(p), blocks[pl.ds(p * width, width), :], (((1,), (1,)), ((), ())), preferred_element_type=F32
+        )
+        value = term if value is None else value + term
+    inverse = 1.0 / (jnp.sum(stencil.astype(F32), axis=1, keepdims=True) - 1.0)
+    return (value.astype(BF16).astype(F32) * inverse).astype(BF16)
 
 
 class cluster_sum:
@@ -130,12 +142,12 @@
 
 def exchange_kernel(
     n, clusters, tile, features, adjacency, cotangent, segments, weight, bias,
-    activations, scaled, summed_total, sten, blocks_out, grads, *rest,
+    activations, scaled, summed_total, sten, mat, last, blocks_out, grads, *rest,
 ):
     landing = (None,) + rest[: n - 1]
     pieces = list(rest[n - 1 : 2 * n - 3])
     pieces = pieces[:1] + [activations] + pieces[1:] + [scaled]
-    (feat, adj, cot, grad, seg, mat, vec, total, shares, back, load_sem, cot_sem, grad_sem,
+    (feat, adj, cot, grad, seg, vec, total, shares, back, load_sem, cot_sem, grad_sem,
      fixed_sem, send_sem, recv_sem, grad_out, grad_in, back_sem, share_send, share_recv, spread_send, spread_recv,
      block_send, block_recv, half_in, quarter_in, bias_in, sum_sems) = rest[2 * n - 3 :]
     outer = n // 2
@@ -183,6 +195,11 @@
         source = grads if p < 2 or p % 2 == 0 else landing[p - 1]
         device = chip_at(-(p // 2)) if p % 2 == 0 else sibling
         return remote(source.at[at(k)], landing[p].at[at(k)], grad_out.at[p, k], grad_in.at[p, k], device)
+
+    def last_hop(p):
+        device = chip_at(-(p // 2)) if p % 2 == 0 else sibling
+        source = last.at[0 if p % 2 == 0 else p - 1]
+        return remote(source, last.at[p], grad_out.at[p, count - 1], grad_in.at[p, count - 1], device)
 
     def send_grad(k):
         for shift in range(1, outer):
@@ -297,7 +314,15 @@
         total[pl.ds(depth, 8), :] += jnp.sum(grad_preact.reshape(tile // 8, 8, width), axis=0)
         grad_preact = grad_preact.astype(BF16)
         grad[slot] = grad_preact
-        store_grad(k).start()
+
+        @pl.when(k < count - 1)
+        def _():
+            store_grad(k).start()
+
+        @pl.when(k == count - 1)
+        def _():
+            last[0] = grad_preact
+
         for p in range(n):
             target = pl.ds(pl.multiple_of(blocks[p] * width, width), width)
             total[target, :] += lax.dot_general(
@@ -336,9 +361,17 @@
     lax.fori_loop(0, count + 1, step, 0)
     sums = cluster_sum(total, summed_total, half_in, quarter_in, bias_in, sum_sems, clusters)
     sums.start()
-    for k in (count - 2, count - 1):
-        store_grad(k).wait()
-        send_grad(k)
+    store_grad(count - 2).wait()
+    send_grad(count - 2)
+    for p in range(1, n):
+        if p == 1 or p % 2 == 0:
+            last_hop(p).start()
+    for p in range(1, n, 2):
+        block(p).wait_send()
+    for shift in range(1, outer):
+        share(shift).wait_send()
+        for peer in others:
+            spread(shift, cluster, peer).wait_send()
     for p in range(n):
         if p % 2:
             block(p).wait_recv()
@@ -360,15 +393,7 @@
         slot = lax.rem(k, 2)
         for p in range(n):
             load_piece(p, k).wait()
-
-        value = None
-        for p in range(n):
-            term = lax.dot_general(
-                back[slot, p], mat[pl.ds(p * width, width), :], (((1,), (1,)), ((), ())), preferred_element_type=F32
-            )
-            value = term if value is None else value + term
-        inverse = 1.0 / (jnp.sum(sten[at(k), :].astype(F32), axis=1, keepdims=True) - 1.0)
-        scaled[at(k), :] = (value.astype(BF16).astype(F32) * inverse).astype(BF16)
+        scaled[at(k), :] = back_through(lambda p: back[slot, p], n, mat, sten[at(k), :])
 
     def moment(r):
         return max(r * 512 // tile, 0)
@@ -377,8 +402,13 @@
         @pl.when(k >= 1)
         def _():
             backward_tile(k - 1)
-
-        @pl.when(k < count)
+            for p in range(1, n):
+                grad_hop(p, k - 1).wait_send()
+
+        for p in range(1, n):
+            hop(p, k).wait_send()
+
+        @pl.when(k < count - 1)
         def _():
             for shift in range(1, outer):
                 grad_hop(2 * shift, k).wait_recv()
@@ -390,32 +420,25 @@
                 load_piece(p, k).start()
 
         for r in range(sums.rounds):
-            if moment(r) <= count:
+            if moment(r) < count:
                 pl.when(k == moment(r))(functools.partial(sums.advance, r))
-        if moment(sums.last) <= count:
+        if moment(sums.last) < count:
             pl.when(k == moment(sums.last))(sums.finish)
         return carry
 
-    lax.fori_loop(0, count + 1, back_step, 0)
+    lax.fori_loop(0, count, back_step, 0)
     for r in range(sums.rounds):
-        if moment(r) > count:
+        if moment(r) >= count:
             sums.advance(r)
-    if moment(sums.last) > count:
+    if moment(sums.last) >= count:
         sums.finish()
-
-    def finish(k, carry):
-        for p in range(1, n):
-            hop(p, k).wait_send()
-            grad_hop(p, k).wait_send()
-        return carry
-
-    lax.fori_loop(0, count, finish, 0)
-    for p in range(1, n, 2):
-        block(p).wait_send()
-    for shift in range(1, outer):
-        share(shift).wait_send()
-        for peer in others:
-            spread(shift, cluster, peer).wait_send()
+    for p in range(2, n, 2):
+        last_hop(p).wait_recv()
+        last_hop(p + 1).start()
+    for p in range(1, n):
+        if p % 2:
+            last_hop(p).wait_recv()
+        last_hop(p).wait_send()
 
 
 def exchange(features, adjacency, cotangent, segments, weight, bias, n, clusters, tile):
@@ -428,12 +451,14 @@
     return pl.pallas_call(
         functools.partial(exchange_kernel, n, clusters, tile),
         in_specs=[HBM] * 6,
-        out_specs=[VMEM] * 4 + [HBM] * (n + 1),
+        out_specs=[VMEM] * 6 + [HBM] * (n + 1),
         out_shape=[
             pltpu.VMEM((rows, width), BF16),
             pltpu.VMEM((rows, width), BF16),
             pltpu.VMEM((depth + 8, width), F32),
             pltpu.VMEM((rows, BLOCK), BF16),
+            pltpu.VMEM((depth, width), BF16),
+            pltpu.VMEM((n, tile, width), BF16),
             array((n, width, width), BF16),
         ]
         + [array((rows, width), BF16)] * n,
@@ -444,7 +469,6 @@
             pltpu.VMEM((2, tile, width), BF16),
             pltpu.VMEM((2, tile, width), BF16),
             pltpu.VMEM(segments.shape, jnp.int32),
-            pltpu.VMEM((depth, width), BF16),
             pltpu.VMEM((width,), BF16),
             pltpu.VMEM((depth + 8, width), F32),
             pltpu.VMEM((outer, 2 * width, width), BF16),
@@ -473,15 +497,20 @@
             ],
         ],
         compiler_params=pltpu.CompilerParams(
-            collective_id=0, has_side_effects=True, vmem_limit_bytes=40 << 20
+            collective_id=0, has_side_effects=True, vmem_limit_bytes=38 << 20
         ),
     )(*[pltpu.with_memory_space_constraint(x, pltpu.HBM) for x in (features, adjacency, cotangent, segments, weight, bias)])
 
 
-def finish_kernel(tile, activations, scaled, total, stencil, grad_features, out, grad_weight, grad_bias, slots, row, slot_sem, fixed_sem):
+def finish_kernel(
+    activations, scaled, total, stencil, blocks, last,
+    grad_features, out, grad_weight, grad_bias, slots, row, rest, slot_sem, fixed_sem,
+):
     rows, width = scaled.shape
+    n, tile, _ = last.shape
     depth = total.shape[0] - 8
-    count = rows // tile
+    span = 2 * tile
+    count = rows // span
     row[...] = jnp.sum(total[pl.ds(depth, 8), :], axis=0, keepdims=True)
     fixed = [
         pltpu.make_async_copy(activations, out, fixed_sem.at[0]),
@@ -490,42 +519,52 @@
     ]
     for copy in fixed:
         copy.start()
+    rest[...] = back_through(lambda p: last[p], n, blocks, stencil[pl.ds(rows - tile, tile), :])
 
     def store(k):
         slot = lax.rem(k, SLOTS)
-        target = pl.ds(pl.multiple_of(k * tile, tile), tile)
+        target = pl.ds(pl.multiple_of(k * span, span), span)
         return pltpu.make_async_copy(slots.at[slot], grad_features.at[target], slot_sem.at[slot])
 
-    def step(k, carry):
+    def step(k, own):
         slot = lax.rem(k, SLOTS)
-
-        @pl.when(k >= SLOTS)
-        def _():
-            store(k - SLOTS).wait()
-
-        for b in range(tile // BLOCK):
-            source = pl.ds(pl.multiple_of(k * tile + b * BLOCK, BLOCK), BLOCK)
+        for b in range(span // BLOCK):
+            source = pl.ds(pl.multiple_of(k * span + b * BLOCK, BLOCK), BLOCK)
+            if b * BLOCK < own:
+                value = scaled[source, :]
+            else:
+                value = rest[pl.ds(b * BLOCK - own, BLOCK), :]
             slots[slot, pl.ds(b * BLOCK, BLOCK), :] = jnp.dot(
-                stencil[source, :], scaled[source, :], preferred_element_type=F32
+                stencil[source, :], value, preferred_element_type=F32
             )
         store(k).start()
+
+    def full(k, carry):
+        @pl.when(k >= SLOTS)
+        def _():
+            store(k - SLOTS).wait()
+
+        step(k, span)
         return carry
 
-    lax.fori_loop(0, count, step, 0)
+    lax.fori_loop(0, count - 1, full, 0)
+    if count > SLOTS:
+        store(count - 1 - SLOTS).wait()
+    step(count - 1, tile)
     for k in range(max(count - SLOTS, 0), count):
         store(k).wait()
     for copy in fixed:
         copy.wait()
 
 
-def finish(activations, scaled, total, stencil):
+def finish(activations, scaled, total, stencil, blocks, last):
     rows, width = scaled.shape
+    tile = last.shape[1]
     depth = total.shape[0] - 8
-    tile = 512
     dma = pltpu.SemaphoreType.DMA
     return pl.pallas_call(
-        functools.partial(finish_kernel, tile),
-        in_specs=[VMEM] * 4,
+        finish_kernel,
+        in_specs=[VMEM] * 6,
         out_specs=[HBM] * 4,
         out_shape=[
             jax.ShapeDtypeStruct((rows, width), F32),
@@ -534,8 +573,9 @@
             jax.ShapeDtypeStruct((1, width), F32),
         ],
         scratch_shapes=[
-            pltpu.VMEM((SLOTS, tile, width), F32),
+            pltpu.VMEM((SLOTS, 2 * tile, width), F32),
             pltpu.VMEM((1, width), F32),
+            pltpu.VMEM((tile, width), BF16),
             dma((SLOTS,)),
             dma((3,)),
         ],
@@ -543,13 +583,13 @@
             flops=2 * rows * BLOCK * width, bytes_accessed=6 * rows * width + 4 * depth * width, transcendentals=0
         ),
         compiler_params=pltpu.CompilerParams(vmem_limit_bytes=12 << 20),
-    )(activations, scaled, total, stencil)
+    )(activations, scaled, total, stencil, blocks, last)
 
 
 def build(n, clusters):
     def local(features, weight, bias, adjacency, segments, cotangent):
         tile = 256 if n <= 4 else 512
-        held = exchange(features, adjacency, cotangent, segments, weight, bias, n, clusters, tile)[:4]
+        held = exchange(features, adjacency, cotangent, segments, weight, bias, n, clusters, tile)[:6]
         grad_features, out, grad_weight, grad_bias = finish(*held)
         return (out, grad_features, grad_weight, grad_bias.reshape(-1))
 

time: 392 us -> 389 us (level)
  no operation moved by 1% of the time
where the time goes in v5:
time: 389 us; the launch traced here: 388 us
  Pallas kernels  387 us (99%)
    pallas_call x1, Pallas kernels, exchange(): pl.pallas_call(functools.partial(exchange_kernel, n, clusters, tile), in_...  378 us
    pallas_call x1, Pallas kernels, finish(): pl.pallas_call(finish_kernel, in_specs=[VMEM] * 6, out_specs=[HBM] * 4, o...  9.79 us

profile of v5, /device:TPU:0, one launch (start us, length us, event | category | flops | bytes accessed | tf_op | source)
XLA Modules:
  0.0 388.1 jit_solution(12465338401443974041)
XLA Ops:
  0.6 377.7 %shard_map.93 = (bf16[8192,512]{1,0:T(8,128)(2,1)S(1)}, bf16[8192,512]{1,0:T(8,128)(2,1)S(1)}, f32[2056,512]{1,0:T(8,128)S(1)}, bf16[8192,128]{1,0:T(8,128)(2,1)...) custom-call(bf16[8192,512]{1,0:T(8,128)(2,1)} %features.1, ...), custom_call_target="tpu_custom_call" | custom-call | tf_op jit(solution)/shard_map/pallas_call | solution.py:451
  378.3 9.8 %shard_map.94 = (f32[8192,512]{1,0:T(8,128)}, bf16[8192,512]{1,0:T(8,128)(2,1)}, f32[2048,512]{1,0:T(8,128)}, f32[1,512]{1,0:T(1,128)}) custom-call(bf16[8192,512]{1,0:T(8,128)(2,1)S(1)} %get-tuple-element.14.activations, bf16[8192,512]{1,0:T(8,128)(2,1)S(1)} %get-tuple-element.15.scaled, f32[2056,512]{1,0:T(8,128)S(1)} %get-tuple-element.16.total, ...), custom_call_target="tpu_custom_call" | custom-call | flops 1073741824 | bytes 29360128 | tf_op jit(solution)/shard_map/pallas_call | solution.py:565

commit v6 on v5

--- a/solution.py
+++ b/solution.py
@@ -62,35 +62,38 @@
         start = c * 2 * self.half + self.x * self.half + q * self.quarter
         return pl.ds(pl.multiple_of(start, self.quarter), self.quarter)
 
-    def copy(self, source, target, kind, send, recv, device):
+    def copy(self, source, target, kind, recv, device):
         return pltpu.make_async_remote_copy(
-            src_ref=source, dst_ref=target, send_sem=self.sems[2 * kind].at[send],
-            recv_sem=self.sems[2 * kind + 1].at[recv], device_id={"clu": device}, device_id_type=MESH,
-        )
+            src_ref=source, dst_ref=target, send_sem=self.sems[0].at[kind],
+            recv_sem=self.sems[1 + kind].at[recv], device_id={"clu": device}, device_id_type=MESH,
+        )
+
+    def several(self, rows, kind, recv=0):
+        return self.copy(self.total.at[pl.ds(0, rows)], self.result.at[pl.ds(0, rows)], kind, recv, self.others[0])
 
     def give_half(self, c):
         rows = self.rows_of_half(c, 1 - self.x)
-        return self.copy(self.total.at[rows], self.half_in.at[c], 0, c, c, self.z * 2 + 1 - self.x)
+        return self.copy(self.total.at[rows], self.half_in.at[c], 0, c, self.z * 2 + 1 - self.x)
 
     def give_quarter(self, c, source, target):
         rows = self.rows_of_quarter(c, target)
         return self.copy(
-            self.total.at[rows], self.quarter_in.at[c, source], 1, (c, target), (c, source), target * 2 + self.x
+            self.total.at[rows], self.quarter_in.at[c, source], 1, c, target * 2 + self.x
         )
 
     def return_quarter(self, c, source, target):
         rows = self.rows_of_quarter(c, source)
         return self.copy(
-            self.result.at[rows], self.result.at[rows], 2, (c, target), (c, source), target * 2 + self.x
+            self.result.at[rows], self.result.at[rows], 2, c, target * 2 + self.x
         )
 
     def return_half(self, c, x):
         rows = self.rows_of_half(c, x)
-        return self.copy(self.result.at[rows], self.result.at[rows], 3, c, c, self.z * 2 + 1 - self.x)
+        return self.copy(self.result.at[rows], self.result.at[rows], 3, 0, self.z * 2 + 1 - self.x)
 
     def give_bias(self, source, target):
         return self.copy(
-            self.total.at[pl.ds(self.depth, 8)], self.bias_in.at[source], 4, target, source, target
+            self.total.at[pl.ds(self.depth, 8)], self.bias_in.at[source], 4, 0, target
         )
 
     def start(self):
@@ -109,8 +112,7 @@
         c = k - 2
         if 0 <= c < self.PARTS:
             rows = self.rows_of_quarter(c, self.z)
-            for level in self.levels:
-                self.give_quarter(c, level, self.z).wait_recv()
+            self.several(len(self.levels) * self.quarter, 1, c).wait_recv()
             value = total[rows, :]
             for level in self.levels:
                 value = value + self.quarter_in[c, level]
@@ -119,21 +121,16 @@
                 self.return_quarter(c, self.z, level).start()
         if k in self.BACK:
             c = self.BACK.index(k)
-            for level in self.levels:
-                self.return_quarter(c, level, self.z).wait_recv()
+            self.several(len(self.levels) * self.quarter, 2, c).wait_recv()
             self.return_half(c, self.x).start()
 
     def finish(self):
-        for c in range(self.PARTS):
-            self.give_half(c).wait_send()
-            for level in self.levels:
-                self.give_quarter(c, self.z, level).wait_send()
-                self.return_quarter(c, self.z, level).wait_send()
-            self.return_half(c, self.x).wait_send()
-            self.return_half(c, 1 - self.x).wait_recv()
-        for other in self.others:
-            self.give_bias(self.me, other).wait_send()
-            self.give_bias(other, self.me).wait_recv()
+        halves = self.PARTS * self.half
+        quarters = self.PARTS * len(self.levels) * self.quarter
+        for kind, rows in enumerate((halves, quarters, quarters, halves, 8 * len(self.others))):
+            self.several(rows, kind).wait_send()
+        self.several(halves, 3).wait_recv()
+        self.several(8 * len(self.others), 4).wait_recv()
         value = self.total[pl.ds(self.depth, 8), :]
         for other in self.others:
             value = value + self.bias_in[other]
@@ -148,7 +145,7 @@
     pieces = list(rest[n - 1 : 2 * n - 3])
     pieces = pieces[:1] + [activations] + pieces[1:] + [scaled]
     (feat, adj, cot, grad, seg, vec, total, shares, back, load_sem, cot_sem, grad_sem,
-     fixed_sem, send_sem, recv_sem, grad_out, grad_in, back_sem, share_send, share_recv, spread_send, spread_recv,
+     fixed_sem, send_sem, far_in, near_in, grad_out, grad_far, grad_near, last_out, back_sem, share_send, share_recv, spread_send, spread_recv,
      block_send, block_recv, half_in, quarter_in, bias_in, sum_sems) = rest[2 * n - 3 :]
     outer = n // 2
     rows, width = features.shape
@@ -158,6 +155,7 @@
     chip, core = me // 2, lax.rem(me, 2)
     sibling = chip * 2 + 1 - core
     part = 2 * width // clusters
+    others = [lax.rem(cluster + d, clusters) for d in range(1, clusters)]
 
     def chip_at(shift):
         return lax.rem(chip + shift + outer, outer) * 2 + core
@@ -189,17 +187,24 @@
     def hop(p, k):
         source = 0 if p % 2 == 0 else p - 1
         device = chip_at(-(p // 2)) if p % 2 == 0 else sibling
-        return remote(pieces[source].at[at(k)], pieces[p].at[at(k)], send_sem.at[p, k], recv_sem.at[p, k], device)
+        arrival = far_in.at[p // 2 - 1, k] if p % 2 == 0 else near_in.at[k]
+        return remote(pieces[source].at[at(k)], pieces[p].at[at(k)], send_sem.at[p], arrival, device)
 
     def grad_hop(p, k):
         source = grads if p < 2 or p % 2 == 0 else landing[p - 1]
         device = chip_at(-(p // 2)) if p % 2 == 0 else sibling
-        return remote(source.at[at(k)], landing[p].at[at(k)], grad_out.at[p, k], grad_in.at[p, k], device)
+        arrival = grad_far.at[p // 2 - 1, k] if p % 2 == 0 else grad_near.at[k]
+        return remote(source.at[at(k)], landing[p].at[at(k)], grad_out.at[p], arrival, device)
+
+    def several(tiles, send, arrival):
+        span = pl.ds(0, tiles * tile)
+        return remote(grads.at[span], landing[1].at[span], send, arrival, sibling)
 
     def last_hop(p):
         device = chip_at(-(p // 2)) if p % 2 == 0 else sibling
         source = last.at[0 if p % 2 == 0 else p - 1]
-        return remote(source, last.at[p], grad_out.at[p, count - 1], grad_in.at[p, count - 1], device)
+        arrival = grad_far.at[p // 2 - 1, count - 1] if p % 2 == 0 else grad_near.at[count - 1]
+        return remote(source, last.at[p], last_out.at[p], arrival, device)
 
     def send_grad(k):
         for shift in range(1, outer):
@@ -223,7 +228,13 @@
         rows = pl.ds(pl.multiple_of(source * part, part), part)
         return remote(
             shares.at[shift, rows], shares.at[shift, rows],
-            spread_send.at[shift, peer], spread_recv.at[shift, source], peer, "clu",
+            spread_send.at[shift], spread_recv.at[shift], peer, "clu",
+        )
+
+    def all_shares(shift):
+        rows = pl.ds(0, len(others) * part)
+        return remote(
+            shares.at[shift, rows], shares.at[shift, rows], spread_send.at[shift], spread_recv.at[shift], others[0], "clu"
         )
 
     def block(p):
@@ -236,7 +247,6 @@
             return pltpu.make_async_copy(source, blocks_out.at[p], block_recv.at[p])
         return remote(source, blocks_out.at[p], block_send.at[p], block_recv.at[p], sibling)
 
-    others = [lax.rem(cluster + d, clusters) for d in range(1, clusters)]
     for copy in loads(0):
         copy.start()
     fixed = [
@@ -295,9 +305,7 @@
         def _():
             load_cot(k + 1).start()
 
-        hop(1, k).wait_recv()
-        for shift in range(1, outer):
-            hop(2 * shift + 1, k).wait_recv()
+        several(outer, send_sem.at[0], near_in.at[k]).wait_recv()
 
         @pl.when(k >= 2)
         def _():
@@ -347,8 +355,7 @@
         @pl.when(k == 4)
         def _():
             for shift in range(1, outer):
-                for peer in others:
-                    spread(shift, peer, cluster).wait_recv()
+                all_shares(shift).wait_recv()
                 block(2 * shift).start()
                 block(2 * shift + 1).start()
 
@@ -366,12 +373,13 @@
     for p in range(1, n):
         if p == 1 or p % 2 == 0:
             last_hop(p).start()
+    for p in range(1, n):
+        several(count, send_sem.at[p], near_in.at[0]).wait_send()
     for p in range(1, n, 2):
         block(p).wait_send()
     for shift in range(1, outer):
         share(shift).wait_send()
-        for peer in others:
-            spread(shift, cluster, peer).wait_send()
+        all_shares(shift).wait_send()
     for p in range(n):
         if p % 2:
             block(p).wait_recv()
@@ -402,20 +410,13 @@
         @pl.when(k >= 1)
         def _():
             backward_tile(k - 1)
-            for p in range(1, n):
-                grad_hop(p, k - 1).wait_send()
-
-        for p in range(1, n):
-            hop(p, k).wait_send()
 
         @pl.when(k < count - 1)
         def _():
             for shift in range(1, outer):
                 grad_hop(2 * shift, k).wait_recv()
                 grad_hop(2 * shift + 1, k).start()
-            grad_hop(1, k).wait_recv()
-            for shift in range(1, outer):
-                grad_hop(2 * shift + 1, k).wait_recv()
+            several(outer, grad_out.at[0], grad_near.at[k]).wait_recv()
             for p in range(n):
                 load_piece(p, k).start()
 
@@ -436,9 +437,9 @@
         last_hop(p).wait_recv()
         last_hop(p + 1).start()
     for p in range(1, n):
-        if p % 2:
-            last_hop(p).wait_recv()
+        several(count - 1, grad_out.at[p], grad_near.at[0]).wait_send()
         last_hop(p).wait_send()
+    several(outer, last_out.at[0], grad_near.at[count - 1]).wait_recv()
 
 
 def exchange(features, adjacency, cotangent, segments, weight, bias, n, clusters, tile):
@@ -477,24 +478,24 @@
             dma((2,)),
             dma((2,)),
             dma((3,)),
-            dma((n, count)),
-            dma((n, count)),
-            dma((n, count)),
-            dma((n, count)),
+            dma((n,)),
+            dma((outer - 1, count)),
+            dma((count,)),
+            dma((n,)),
+            dma((outer - 1, count)),
+            dma((count,)),
+            dma((n,)),
             dma((2, n)),
             dma((outer,)),
             dma((outer,)),
-            dma((outer, clusters)),
-            dma((outer, clusters)),
+            dma((outer,)),
+            dma((outer,)),
             dma((n,)),
             dma((n,)),
             pltpu.VMEM((parts, depth // parts // 2, width), F32),
             pltpu.VMEM((parts, high, depth // parts // 2 // high, width), F32),
             pltpu.VMEM((clusters, 8, width), F32),
-            [
-                dma((parts,)), dma((parts,)), dma((parts, high)), dma((parts, high)), dma((parts, high)),
-                dma((parts, high)), dma((parts,)), dma((parts,)), dma((clusters,)), dma((clusters,)),
-            ],
+            [dma((5,)), dma((parts,)), dma((parts,)), dma((parts,)), dma((1,)), dma((1,))],
         ],
         compiler_params=pltpu.CompilerParams(
             collective_id=0, has_side_effects=True, vmem_limit_bytes=38 << 20

time: 389 us -> 385 us (0.990)
  Pallas kernels: 387 us -> 383 us
    pallas_call x1, Pallas kernels: 378 us -> 373 us  [exchange(): pl.pallas_call(functools.partial(exchange_kernel, n, clusters, tile), in_...]
where the time goes in v6:
time: 385 us; the launch traced here: 384 us
  Pallas kernels  383 us (99%)
    pallas_call x1, Pallas kernels, exchange(): pl.pallas_call(functools.partial(exchange_kernel, n, clusters, tile), in_...  373 us
    pallas_call x1, Pallas kernels, finish(): pl.pallas_call(finish_kernel, in_specs=[VMEM] * 6, out_specs=[HBM] * 4, o...  9.79 us

profile of v6, /device:TPU:0, one launch (start us, length us, event | category | flops | bytes accessed | tf_op | source)
XLA Modules:
  0.0 383.9 jit_solution(11408842921414138105)
XLA Ops:
  0.6 373.4 %shard_map.93 = (bf16[8192,512]{1,0:T(8,128)(2,1)S(1)}, bf16[8192,512]{1,0:T(8,128)(2,1)S(1)}, f32[2056,512]{1,0:T(8,128)S(1)}, bf16[8192,128]{1,0:T(8,128)(2,1)...) custom-call(bf16[8192,512]{1,0:T(8,128)(2,1)} %features.1, ...), custom_call_target="tpu_custom_call" | custom-call | tf_op jit(solution)/shard_map/pallas_call | solution.py:452
  374.1 9.8 %shard_map.94 = (f32[8192,512]{1,0:T(8,128)}, bf16[8192,512]{1,0:T(8,128)(2,1)}, f32[2048,512]{1,0:T(8,128)}, f32[1,512]{1,0:T(1,128)}) custom-call(bf16[8192,512]{1,0:T(8,128)(2,1)S(1)} %get-tuple-element.14.activations, bf16[8192,512]{1,0:T(8,128)(2,1)S(1)} %get-tuple-element.15.scaled, f32[2056,512]{1,0:T(8,128)S(1)} %get-tuple-element.16.total, ...), custom_call_target="tpu_custom_call" | custom-call | flops 1073741824 | bytes 29360128 | tf_op jit(solution)/shard_map/pallas_call | solution.py:566

commit v7 on v6

--- a/solution.py
+++ b/solution.py
@@ -258,11 +258,26 @@
     load_cot(0).start()
 
     barrier = pltpu.get_barrier_semaphore()
-    peers = [("col", sibling)] + [("col", chip_at(shift)) for shift in range(1, outer)]
-    peers += [("clu", peer) for peer in others]
-    for axis, peer in peers:
+    centre = core * (clusters - 1)
+    neighbours = [sibling] + [chip_at(shift) for shift in range(1, outer)]
+
+    def greet(axis, peer):
         pl.semaphore_signal(barrier, inc=1, device_id={axis: peer}, device_id_type=MESH)
-    pl.semaphore_wait(barrier, len(peers))
+
+    for peer in neighbours:
+        greet("col", peer)
+
+    @pl.when(cluster == centre)
+    def _():
+        pl.semaphore_wait(barrier, len(neighbours) + len(others))
+        for peer in others:
+            greet("clu", peer)
+
+    @pl.when(cluster != centre)
+    def _():
+        pl.semaphore_wait(barrier, len(neighbours))
+        greet("clu", centre)
+
     for shift in range(1, outer):
         share(shift).start()
     block(0).start()
@@ -345,14 +360,18 @@
                 hop(2 * shift, k).wait_recv()
                 hop(2 * shift + 1, k).start()
 
-        @pl.when(k == 1)
+        @pl.when((k == 2) & (cluster != centre))
+        def _():
+            pl.semaphore_wait(barrier, 1)
+
+        @pl.when(k == 2)
         def _():
             for shift in range(1, outer):
                 share(shift).wait_recv()
                 for peer in others:
                     spread(shift, cluster, peer).start()
 
-        @pl.when(k == 4)
+        @pl.when(k == 6)
         def _():
             for shift in range(1, outer):
                 all_shares(shift).wait_recv()

time: 385 us -> 383 us (level)
  no operation moved by 1% of the time
where the time goes in v7:
time: 383 us; the launch traced here: 382 us
  Pallas kernels  381 us (99%)
    pallas_call x1, Pallas kernels, exchange(): pl.pallas_call(functools.partial(exchange_kernel, n, clusters, tile), in_...  371 us
    pallas_call x1, Pallas kernels, finish(): pl.pallas_call(finish_kernel, in_specs=[VMEM] * 6, out_specs=[HBM] * 4, o...  9.79 us

profile of v7, /device:TPU:0, one launch (start us, length us, event | category | flops | bytes accessed | tf_op | source)
XLA Modules:
  0.0 381.7 jit_solution(279771253453291572)
XLA Ops:
  0.6 371.2 %shard_map.93 = (bf16[8192,512]{1,0:T(8,128)(2,1)S(1)}, bf16[8192,512]{1,0:T(8,128)(2,1)S(1)}, f32[2056,512]{1,0:T(8,128)S(1)}, bf16[8192,128]{1,0:T(8,128)(2,1)...) custom-call(bf16[8192,512]{1,0:T(8,128)(2,1)} %features.1, ...), custom_call_target="tpu_custom_call" | custom-call | tf_op jit(solution)/shard_map/pallas_call | solution.py:471
  371.9 9.8 %shard_map.94 = (f32[8192,512]{1,0:T(8,128)}, bf16[8192,512]{1,0:T(8,128)(2,1)}, f32[2048,512]{1,0:T(8,128)}, f32[1,512]{1,0:T(1,128)}) custom-call(bf16[8192,512]{1,0:T(8,128)(2,1)S(1)} %get-tuple-element.14.activations, bf16[8192,512]{1,0:T(8,128)(2,1)S(1)} %get-tuple-element.15.scaled, f32[2056,512]{1,0:T(8,128)S(1)} %get-tuple-element.16.total, ...), custom_call_target="tpu_custom_call" | custom-call | flops 1073741824 | bytes 29360128 | tf_op jit(solution)/shard_map/pallas_call | solution.py:585

commit v8 on v7

--- a/solution.py
+++ b/solution.py
@@ -163,6 +163,9 @@
     def at(k):
         return pl.ds(pl.multiple_of(k * tile, tile), tile)
 
+    def pair(c):
+        return pl.ds(pl.multiple_of(c * 2 * tile, 2 * tile), 2 * tile)
+
     def loads(k):
         slot = lax.rem(k, 2)
         return (
@@ -184,17 +187,17 @@
             device_id={axis: device}, device_id_type=MESH,
         )
 
-    def hop(p, k):
+    def hop(p, c):
         source = 0 if p % 2 == 0 else p - 1
         device = chip_at(-(p // 2)) if p % 2 == 0 else sibling
-        arrival = far_in.at[p // 2 - 1, k] if p % 2 == 0 else near_in.at[k]
-        return remote(pieces[source].at[at(k)], pieces[p].at[at(k)], send_sem.at[p], arrival, device)
-
-    def grad_hop(p, k):
+        arrival = far_in.at[p // 2 - 1, c] if p % 2 == 0 else near_in.at[c]
+        return remote(pieces[source].at[pair(c)], pieces[p].at[pair(c)], send_sem.at[p], arrival, device)
+
+    def grad_hop(p, c, rows):
         source = grads if p < 2 or p % 2 == 0 else landing[p - 1]
         device = chip_at(-(p // 2)) if p % 2 == 0 else sibling
-        arrival = grad_far.at[p // 2 - 1, k] if p % 2 == 0 else grad_near.at[k]
-        return remote(source.at[at(k)], landing[p].at[at(k)], grad_out.at[p], arrival, device)
+        arrival = grad_far.at[p // 2 - 1, c] if p % 2 == 0 else grad_near.at[c]
+        return remote(source.at[rows], landing[p].at[rows], grad_out.at[p], arrival, device)
 
     def several(tiles, send, arrival):
         span = pl.ds(0, tiles * tile)
@@ -203,13 +206,19 @@
     def last_hop(p):
         device = chip_at(-(p // 2)) if p % 2 == 0 else sibling
         source = last.at[0 if p % 2 == 0 else p - 1]
-        arrival = grad_far.at[p // 2 - 1, count - 1] if p % 2 == 0 else grad_near.at[count - 1]
+        arrival = grad_far.at[p // 2 - 1, count // 2] if p % 2 == 0 else grad_near.at[count // 2]
         return remote(source, last.at[p], last_out.at[p], arrival, device)
 
-    def send_grad(k):
+    def send_grad(c, rows):
         for shift in range(1, outer):
-            grad_hop(2 * shift, k).start()
-        grad_hop(1, k).start()
+            grad_hop(2 * shift, c, rows).start()
+        grad_hop(1, c, rows).start()
+
+    def pass_grad(c, rows, tiles):
+        for shift in range(1, outer):
+            grad_hop(2 * shift, c, rows).wait_recv()
+            grad_hop(2 * shift + 1, c, rows).start()
+        several(tiles * outer, grad_out.at[0], grad_near.at[c]).wait_recv()
 
     def load_piece(p, k):
         slot = lax.rem(k, 2)
@@ -258,7 +267,7 @@
     load_cot(0).start()
 
     barrier = pltpu.get_barrier_semaphore()
-    centre = core * (clusters - 1)
+    centre = clusters - 2 + core
     neighbours = [sibling] + [chip_at(shift) for shift in range(1, outer)]
 
     def greet(axis, peer):
@@ -301,9 +310,13 @@
             target = pl.ds(pl.multiple_of(k * tile + b * BLOCK, BLOCK), BLOCK)
             sten[target, :] = stencil
             pieces[0][target, :] = (summed * inverse).astype(BF16)
-        for shift in range(1, outer):
-            hop(2 * shift, k).start()
-        hop(1, k).start()
+
+        @pl.when(lax.rem(k, 2) == 1)
+        def _():
+            for shift in range(1, outer):
+                hop(2 * shift, k // 2).start()
+            hop(1, k // 2).start()
+
         return carry
 
     lax.fori_loop(0, count, aggregate_tile, 0)
@@ -320,12 +333,18 @@
         def _():
             load_cot(k + 1).start()
 
-        several(outer, send_sem.at[0], near_in.at[k]).wait_recv()
+        @pl.when(lax.rem(k, 2) == 0)
+        def _():
+            several(2 * outer, send_sem.at[0], near_in.at[k // 2]).wait_recv()
+
 
         @pl.when(k >= 2)
         def _():
             store_grad(k - 2).wait()
-            send_grad(k - 2)
+
+        @pl.when((k >= 3) & (lax.rem(k, 2) == 1))
+        def _():
+            send_grad((k - 3) // 2, pair((k - 3) // 2))
 
         preact = None
         for p in range(n):
@@ -354,11 +373,11 @@
         activations[at(k), :] = jnp.maximum(preact, 0.0).astype(BF16)
 
     def step(k, carry):
-        @pl.when(k < count)
+        @pl.when((k < count) & (lax.rem(k, 2) == 0))
         def _():
             for shift in range(1, outer):
-                hop(2 * shift, k).wait_recv()
-                hop(2 * shift + 1, k).start()
+                hop(2 * shift, k // 2).wait_recv()
+                hop(2 * shift + 1, k // 2).start()
 
         @pl.when((k == 2) & (cluster != centre))
         def _():
@@ -388,7 +407,7 @@
     sums = cluster_sum(total, summed_total, half_in, quarter_in, bias_in, sum_sems, clusters)
     sums.start()
     store_grad(count - 2).wait()
-    send_grad(count - 2)
+    send_grad(count // 2 - 1, at(count - 2))
     for p in range(1, n):
         if p == 1 or p % 2 == 0:
             last_hop(p).start()
@@ -430,14 +449,18 @@
         def _():
             backward_tile(k - 1)
 
-        @pl.when(k < count - 1)
-        def _():
-            for shift in range(1, outer):
-                grad_hop(2 * shift, k).wait_recv()
-                grad_hop(2 * shift + 1, k).start()
-            several(outer, grad_out.at[0], grad_near.at[k]).wait_recv()
+        @pl.when((k < count - 2) & (lax.rem(k, 2) == 0))
+        def _():
+            pass_grad(k // 2, pair(k // 2), 2)
             for p in range(n):
                 load_piece(p, k).start()
+                load_piece(p, k + 1).start()
+
+        @pl.when(k == count - 2)
+        def _():
+            pass_grad(count // 2 - 1, at(count - 2), 1)
+            for p in range(n):
+                load_piece(p, count - 2).start()
 
         for r in range(sums.rounds):
             if moment(r) < count:
@@ -458,7 +481,7 @@
     for p in range(1, n):
         several(count - 1, grad_out.at[p], grad_near.at[0]).wait_send()
         last_hop(p).wait_send()
-    several(outer, last_out.at[0], grad_near.at[count - 1]).wait_recv()
+    several(outer, last_out.at[0], grad_near.at[count // 2]).wait_recv()
 
 
 def exchange(features, adjacency, cotangent, segments, weight, bias, n, clusters, tile):
@@ -498,11 +521,11 @@
             dma((2,)),
             dma((3,)),
             dma((n,)),
-            dma((outer - 1, count)),
-            dma((count,)),
+            dma((outer - 1, count // 2)),
+            dma((count // 2,)),
             dma((n,)),
-            dma((outer - 1, count)),
-            dma((count,)),
+            dma((outer - 1, count // 2 + 1)),
+            dma((count // 2 + 1,)),
             dma((n,)),
             dma((2, n)),
             dma((outer,)),

time: 383 us -> 381 us (level)
  no operation moved by 1% of the time
where the time goes in v8:
time: 381 us; the launch traced here: 380 us
  Pallas kernels  379 us (99%)
    pallas_call x1, Pallas kernels, exchange(): pl.pallas_call(functools.partial(exchange_kernel, n, clusters, tile), in_...  369 us
    pallas_call x1, Pallas kernels, finish(): pl.pallas_call(finish_kernel, in_specs=[VMEM] * 6, out_specs=[HBM] * 4, o...  9.79 us

profile of v8, /device:TPU:0, one launch (start us, length us, event | category | flops | bytes accessed | tf_op | source)
XLA Modules:
  0.0 379.7 jit_solution(15907636042211183132)
XLA Ops:
  0.6 369.3 %shard_map.93 = (bf16[8192,512]{1,0:T(8,128)(2,1)S(1)}, bf16[8192,512]{1,0:T(8,128)(2,1)S(1)}, f32[2056,512]{1,0:T(8,128)S(1)}, bf16[8192,128]{1,0:T(8,128)(2,1)...) custom-call(bf16[8192,512]{1,0:T(8,128)(2,1)} %features.1, ...), custom_call_target="tpu_custom_call" | custom-call | tf_op jit(solution)/shard_map/pallas_call | solution.py:494
  369.9 9.8 %shard_map.94 = (f32[8192,512]{1,0:T(8,128)}, bf16[8192,512]{1,0:T(8,128)(2,1)}, f32[2048,512]{1,0:T(8,128)}, f32[1,512]{1,0:T(1,128)}) custom-call(bf16[8192,512]{1,0:T(8,128)(2,1)S(1)} %get-tuple-element.14.activations, bf16[8192,512]{1,0:T(8,128)(2,1)S(1)} %get-tuple-element.15.scaled, f32[2056,512]{1,0:T(8,128)S(1)} %get-tuple-element.16.total, ...), custom_call_target="tpu_custom_call" | custom-call | flops 1073741824 | bytes 29360128 | tf_op jit(solution)/shard_map/pallas_call | solution.py:608

commit v9 on v8

--- a/solution.py
+++ b/solution.py
@@ -9,6 +9,7 @@
 
 BLOCK = 128
 SLOTS = 4
+TAIL = 6
 F32 = jnp.float32
 BF16 = jnp.bfloat16
 MESH = pl.DeviceIdType.MESH
@@ -138,14 +139,14 @@
 
 
 def exchange_kernel(
-    n, clusters, tile, features, adjacency, cotangent, segments, weight, bias,
-    activations, scaled, summed_total, sten, mat, last, blocks_out, grads, *rest,
+    n, clusters, early, tile, features, adjacency, cotangent, segments, weight, bias,
+    activations, scaled, summed_total, sten, mat, blocks_out, grads, *rest,
 ):
     landing = (None,) + rest[: n - 1]
     pieces = list(rest[n - 1 : 2 * n - 3])
     pieces = pieces[:1] + [activations] + pieces[1:] + [scaled]
     (feat, adj, cot, grad, seg, vec, total, shares, back, load_sem, cot_sem, grad_sem,
-     fixed_sem, send_sem, far_in, near_in, grad_out, grad_far, grad_near, last_out, back_sem, share_send, share_recv, spread_send, spread_recv,
+     fixed_sem, send_sem, far_in, near_in, grad_out, grad_far, grad_near, back_sem, share_send, share_recv, spread_send, spread_recv,
      block_send, block_recv, half_in, quarter_in, bias_in, sum_sems) = rest[2 * n - 3 :]
     outer = n // 2
     rows, width = features.shape
@@ -193,7 +194,8 @@
         arrival = far_in.at[p // 2 - 1, c] if p % 2 == 0 else near_in.at[c]
         return remote(pieces[source].at[pair(c)], pieces[p].at[pair(c)], send_sem.at[p], arrival, device)
 
-    def grad_hop(p, c, rows):
+    def grad_hop(p, c):
+        rows = pair(c)
         source = grads if p < 2 or p % 2 == 0 else landing[p - 1]
         device = chip_at(-(p // 2)) if p % 2 == 0 else sibling
         arrival = grad_far.at[p // 2 - 1, c] if p % 2 == 0 else grad_near.at[c]
@@ -203,22 +205,13 @@
         span = pl.ds(0, tiles * tile)
         return remote(grads.at[span], landing[1].at[span], send, arrival, sibling)
 
-    def last_hop(p):
-        device = chip_at(-(p // 2)) if p % 2 == 0 else sibling
-        source = last.at[0 if p % 2 == 0 else p - 1]
-        arrival = grad_far.at[p // 2 - 1, count // 2] if p % 2 == 0 else grad_near.at[count // 2]
-        return remote(source, last.at[p], last_out.at[p], arrival, device)
-
-    def send_grad(c, rows):
-        for shift in range(1, outer):
-            grad_hop(2 * shift, c, rows).start()
-        grad_hop(1, c, rows).start()
-
-    def pass_grad(c, rows, tiles):
-        for shift in range(1, outer):
-            grad_hop(2 * shift, c, rows).wait_recv()
-            grad_hop(2 * shift + 1, c, rows).start()
-        several(tiles * outer, grad_out.at[0], grad_near.at[c]).wait_recv()
+    def send_grad(c):
+        @pl.when((c < early // 2) | (core == 1))
+        def _():
+            for shift in range(1, outer):
+                grad_hop(2 * shift, c).start()
+
+        grad_hop(1, c).start()
 
     def load_piece(p, k):
         slot = lax.rem(k, 2)
@@ -344,7 +337,7 @@
 
         @pl.when((k >= 3) & (lax.rem(k, 2) == 1))
         def _():
-            send_grad((k - 3) // 2, pair((k - 3) // 2))
+            send_grad((k - 3) // 2)
 
         preact = None
         for p in range(n):
@@ -357,14 +350,7 @@
         grad_preact = grad_preact.astype(BF16)
         grad[slot] = grad_preact
 
-        @pl.when(k < count - 1)
-        def _():
-            store_grad(k).start()
-
-        @pl.when(k == count - 1)
-        def _():
-            last[0] = grad_preact
-
+        store_grad(k).start()
         for p in range(n):
             target = pl.ds(pl.multiple_of(blocks[p] * width, width), width)
             total[target, :] += lax.dot_general(
@@ -406,11 +392,9 @@
     lax.fori_loop(0, count + 1, step, 0)
     sums = cluster_sum(total, summed_total, half_in, quarter_in, bias_in, sum_sems, clusters)
     sums.start()
-    store_grad(count - 2).wait()
-    send_grad(count // 2 - 1, at(count - 2))
-    for p in range(1, n):
-        if p == 1 or p % 2 == 0:
-            last_hop(p).start()
+    for k in (count - 2, count - 1):
+        store_grad(k).wait()
+    send_grad(count // 2 - 1)
     for p in range(1, n):
         several(count, send_sem.at[p], near_in.at[0]).wait_send()
     for p in range(1, n, 2):
@@ -449,42 +433,56 @@
         def _():
             backward_tile(k - 1)
 
-        @pl.when((k < count - 2) & (lax.rem(k, 2) == 0))
-        def _():
-            pass_grad(k // 2, pair(k // 2), 2)
+        @pl.when((k < early) & (lax.rem(k, 2) == 0))
+        def _():
+            for shift in range(1, outer):
+                grad_hop(2 * shift, k // 2).wait_recv()
+                grad_hop(2 * shift + 1, k // 2).start()
+            several(2 * outer, grad_out.at[0], grad_near.at[k // 2]).wait_recv()
             for p in range(n):
                 load_piece(p, k).start()
                 load_piece(p, k + 1).start()
 
-        @pl.when(k == count - 2)
-        def _():
-            pass_grad(count // 2 - 1, at(count - 2), 1)
-            for p in range(n):
-                load_piece(p, count - 2).start()
-
         for r in range(sums.rounds):
-            if moment(r) < count:
+            if moment(r) <= early:
                 pl.when(k == moment(r))(functools.partial(sums.advance, r))
-        if moment(sums.last) < count:
+        if moment(sums.last) <= early:
             pl.when(k == moment(sums.last))(sums.finish)
         return carry
 
-    lax.fori_loop(0, count, back_step, 0)
+    lax.fori_loop(0, early + 1, back_step, 0)
     for r in range(sums.rounds):
-        if moment(r) >= count:
+        if moment(r) > early:
             sums.advance(r)
-    if moment(sums.last) >= count:
+    if moment(sums.last) > early:
         sums.finish()
-    for p in range(2, n, 2):
-        last_hop(p).wait_recv()
-        last_hop(p + 1).start()
-    for p in range(1, n):
-        several(count - 1, grad_out.at[p], grad_near.at[0]).wait_send()
-        last_hop(p).wait_send()
-    several(outer, last_out.at[0], grad_near.at[count // 2]).wait_recv()
-
-
-def exchange(features, adjacency, cotangent, segments, weight, bias, n, clusters, tile):
+    def late_step(c, carry):
+        several(2, grad_out.at[0], grad_near.at[c]).wait_recv()
+
+        @pl.when(core == 1)
+        def _():
+            for shift in range(1, outer):
+                grad_hop(2 * shift, c).wait_recv()
+
+        return carry
+
+    for p in range(3, n, 2):
+        several(early, grad_out.at[p], grad_near.at[0]).wait_send()
+    several(count, grad_out.at[1], grad_near.at[0]).wait_send()
+    lax.fori_loop(early // 2, count // 2, late_step, 0)
+
+    @pl.when(core == 0)
+    def _():
+        for p in range(2, n, 2):
+            several(early, grad_out.at[p], grad_near.at[0]).wait_send()
+
+    @pl.when(core == 1)
+    def _():
+        for p in range(2, n, 2):
+            several(count, grad_out.at[p], grad_near.at[0]).wait_send()
+
+
+def exchange(features, adjacency, cotangent, segments, weight, bias, n, clusters, early, tile):
     rows, width = features.shape
     depth = weight.shape[0]
     count, outer = rows // tile, n // 2
@@ -492,16 +490,15 @@
     dma = pltpu.SemaphoreType.DMA
     array = jax.ShapeDtypeStruct
     return pl.pallas_call(
-        functools.partial(exchange_kernel, n, clusters, tile),
+        functools.partial(exchange_kernel, n, clusters, early, tile),
         in_specs=[HBM] * 6,
-        out_specs=[VMEM] * 6 + [HBM] * (n + 1),
+        out_specs=[VMEM] * 5 + [HBM] * (n + 1),
         out_shape=[
             pltpu.VMEM((rows, width), BF16),
             pltpu.VMEM((rows, width), BF16),
             pltpu.VMEM((depth + 8, width), F32),
             pltpu.VMEM((rows, BLOCK), BF16),
             pltpu.VMEM((depth, width), BF16),
-            pltpu.VMEM((n, tile, width), BF16),
             array((n, width, width), BF16),
         ]
         + [array((rows, width), BF16)] * n,
@@ -524,9 +521,8 @@
             dma((outer - 1, count // 2)),
             dma((count // 2,)),
             dma((n,)),
-            dma((outer - 1, count // 2 + 1)),
-            dma((count // 2 + 1,)),
-            dma((n,)),
+            dma((outer - 1, count // 2)),
+            dma((count // 2,)),
             dma((2, n)),
             dma((outer,)),
             dma((outer,)),
@@ -545,15 +541,20 @@
     )(*[pltpu.with_memory_space_constraint(x, pltpu.HBM) for x in (features, adjacency, cotangent, segments, weight, bias)])
 
 
+def stencil_rows(stencil, scaled, slots, slot, first, start, span):
+    for b in range(span // BLOCK):
+        source = pl.multiple_of(start + b * BLOCK, BLOCK)
+        slots[slot, pl.ds(b * BLOCK, BLOCK), :] = jnp.dot(
+            stencil[pl.ds(first + source, BLOCK), :], scaled[pl.ds(source, BLOCK), :], preferred_element_type=F32
+        )
+
+
 def finish_kernel(
-    activations, scaled, total, stencil, blocks, last,
-    grad_features, out, grad_weight, grad_bias, slots, row, rest, slot_sem, fixed_sem,
+    early, span, activations, scaled, total, stencil,
+    grad_features, out, grad_weight, grad_bias, slots, row, slot_sem, fixed_sem,
 ):
-    rows, width = scaled.shape
-    n, tile, _ = last.shape
     depth = total.shape[0] - 8
-    span = 2 * tile
-    count = rows // span
+    count = early // span
     row[...] = jnp.sum(total[pl.ds(depth, 8), :], axis=0, keepdims=True)
     fixed = [
         pltpu.make_async_copy(activations, out, fixed_sem.at[0]),
@@ -562,52 +563,35 @@
     ]
     for copy in fixed:
         copy.start()
-    rest[...] = back_through(lambda p: last[p], n, blocks, stencil[pl.ds(rows - tile, tile), :])
 
     def store(k):
         slot = lax.rem(k, SLOTS)
         target = pl.ds(pl.multiple_of(k * span, span), span)
         return pltpu.make_async_copy(slots.at[slot], grad_features.at[target], slot_sem.at[slot])
 
-    def step(k, own):
-        slot = lax.rem(k, SLOTS)
-        for b in range(span // BLOCK):
-            source = pl.ds(pl.multiple_of(k * span + b * BLOCK, BLOCK), BLOCK)
-            if b * BLOCK < own:
-                value = scaled[source, :]
-            else:
-                value = rest[pl.ds(b * BLOCK - own, BLOCK), :]
-            slots[slot, pl.ds(b * BLOCK, BLOCK), :] = jnp.dot(
-                stencil[source, :], value, preferred_element_type=F32
-            )
+    def step(k, carry):
+        @pl.when(k >= SLOTS)
+        def _():
+            store(k - SLOTS).wait()
+
+        stencil_rows(stencil, scaled, slots, lax.rem(k, SLOTS), 0, k * span, span)
         store(k).start()
-
-    def full(k, carry):
-        @pl.when(k >= SLOTS)
-        def _():
-            store(k - SLOTS).wait()
-
-        step(k, span)
         return carry
 
-    lax.fori_loop(0, count - 1, full, 0)
-    if count > SLOTS:
-        store(count - 1 - SLOTS).wait()
-    step(count - 1, tile)
+    lax.fori_loop(0, count, step, 0)
     for k in range(max(count - SLOTS, 0), count):
         store(k).wait()
     for copy in fixed:
         copy.wait()
 
 
-def finish(activations, scaled, total, stencil, blocks, last):
+def finish(activations, scaled, total, stencil, early, tile):
     rows, width = scaled.shape
-    tile = last.shape[1]
     depth = total.shape[0] - 8
     dma = pltpu.SemaphoreType.DMA
     return pl.pallas_call(
-        finish_kernel,
-        in_specs=[VMEM] * 6,
+        functools.partial(finish_kernel, early * tile, 2 * tile),
+        in_specs=[VMEM] * 4,
         out_specs=[HBM] * 4,
         out_shape=[
             jax.ShapeDtypeStruct((rows, width), F32),
@@ -618,7 +602,6 @@
         scratch_shapes=[
             pltpu.VMEM((SLOTS, 2 * tile, width), F32),
             pltpu.VMEM((1, width), F32),
-            pltpu.VMEM((tile, width), BF16),
             dma((SLOTS,)),
             dma((3,)),
         ],
@@ -626,14 +609,161 @@
             flops=2 * rows * BLOCK * width, bytes_accessed=6 * rows * width + 4 * depth * width, transcendentals=0
         ),
         compiler_params=pltpu.CompilerParams(vmem_limit_bytes=12 << 20),
-    )(activations, scaled, total, stencil, blocks, last)
+    )(activations, scaled, total, stencil)
+
+
+def late_kernel(n, early, tile, *refs):
+    grads, landing = refs[0], (None,) + refs[1:n]
+    sten, mat, scaled, pieces, load_sem, far_out, far_in, near_out, near_in = refs[n + 1 :]
+    outer = n // 2
+    rows, width = grads.shape
+    late = rows // tile - early
+    kept = pl.ds(early * tile, late * tile)
+    me = lax.axis_index("col")
+    chip, core = me // 2, lax.rem(me, 2)
+    sibling = chip * 2 + 1 - core
+
+    def chip_at(shift):
+        return lax.rem(chip + shift + outer, outer) * 2 + core
+
+    def at(j):
+        return pl.ds(pl.multiple_of(j * tile, tile), tile)
+
+    def remote(source, target, send, recv, device):
+        return pltpu.make_async_remote_copy(
+            src_ref=source, dst_ref=target, send_sem=send, recv_sem=recv,
+            device_id={"col": device}, device_id_type=MESH,
+        )
+
+    def load(p):
+        source = landing[p] if p else grads
+        return pltpu.make_async_copy(source.at[kept], pieces.at[p], load_sem.at[p])
+
+    def far(p, j):
+        source = grads.at[pl.ds(pl.multiple_of((early + j) * tile, tile), tile)]
+        return remote(source, pieces.at[p, at(j)], far_out.at[p], far_in.at[p // 2 - 1, j], chip_at(-(p // 2)))
+
+    def near(p, j):
+        return remote(pieces.at[p - 1, at(j)], pieces.at[p, at(j)], near_out.at[p], near_in.at[p // 2 - 1, j], sibling)
+
+    barrier = pltpu.get_barrier_semaphore()
+    load(0).start()
+    load(1).start()
+
+    @pl.when(core == 0)
+    def _():
+        for shift in range(1, outer):
+            pl.semaphore_signal(barrier, inc=1, device_id={"col": chip_at(shift)}, device_id_type=MESH)
+        pl.semaphore_wait(barrier, outer - 1)
+        for j in range(late):
+            for p in range(2, n, 2):
+                far(p, j).start()
+        pl.semaphore_signal(barrier, inc=1, device_id={"col": sibling}, device_id_type=MESH)
+        pl.semaphore_wait(barrier, 1)
+
+    @pl.when(core == 1)
+    def _():
+        for p in range(2, n, 2):
+            load(p).start()
+        pl.semaphore_wait(barrier, 1)
+        pl.semaphore_signal(barrier, inc=1, device_id={"col": sibling}, device_id_type=MESH)
+        for p in range(2, n, 2):
+            load(p).wait()
+        for j in range(late):
+            for p in range(3, n, 2):
+                near(p, j).start()
+
+    load(0).wait()
+    load(1).wait()
+
+    def step(j, carry):
+        @pl.when(core == 0)
+        def _():
+            for p in range(2, n, 2):
+                far(p, j).wait_recv()
+                near(p + 1, j).start()
+
+        for p in range(3, n, 2):
+            near(p, j).wait_recv()
+        stencil = sten[pl.ds(pl.multiple_of((early + j) * tile, tile), tile), :]
+        scaled[at(j), :] = back_through(lambda p: pieces[p, at(j), :], n, mat, stencil)
+        return carry
+
+    lax.fori_loop(0, late, step, 0)
+
+    @pl.when(core == 0)
+    def _():
+        for p in range(2, n, 2):
+            remote(grads.at[kept], pieces.at[p], far_out.at[p], far_in.at[p // 2 - 1, 0], chip_at(-(p // 2))).wait_send()
+
+    for p in range(3, n, 2):
+        remote(pieces.at[p - 1], pieces.at[p], near_out.at[p], near_in.at[p // 2 - 1, 0], sibling).wait_send()
+
+
+def exchange_late(grads, landing, earlier, stencil, blocks, n, early, tile):
+    rows, width = grads.shape
+    late, outer = rows // tile - early, n // 2
+    dma = pltpu.SemaphoreType.DMA
+    far = [pltpu.with_memory_space_constraint(x, pltpu.HBM) for x in (grads, *landing, earlier)]
+    return pl.pallas_call(
+        functools.partial(late_kernel, n, early, tile),
+        in_specs=[HBM] * (n + 1) + [VMEM] * 2,
+        out_specs=VMEM,
+        out_shape=pltpu.VMEM((late * tile, width), BF16),
+        scratch_shapes=[
+            pltpu.VMEM((n, late * tile, width), BF16),
+            dma((n,)),
+            dma((n,)),
+            dma((outer - 1, late)),
+            dma((n,)),
+            dma((outer - 1, late)),
+        ],
+        compiler_params=pltpu.CompilerParams(
+            collective_id=1, has_side_effects=True, vmem_limit_bytes=12 << 20
+        ),
+    )(*far, stencil, blocks)
+
+
+def finish_late_kernel(first, span, scaled, stencil, _, grad_features, slots, sem):
+    count = scaled.shape[0] // span
+
+    def store(k):
+        return pltpu.make_async_copy(slots.at[k], grad_features.at[pl.ds(first + k * span, span)], sem.at[k])
+
+    for k in range(count):
+        stencil_rows(stencil, scaled, slots, k, first, k * span, span)
+        store(k).start()
+    for k in range(count):
+        store(k).wait()
+
+
+def finish_late(scaled, stencil, grad_features, early, tile):
+    late, width = scaled.shape
+    span = tile
+    return pl.pallas_call(
+        functools.partial(finish_late_kernel, early * tile, span),
+        in_specs=[VMEM] * 2 + [HBM],
+        out_specs=HBM,
+        out_shape=jax.ShapeDtypeStruct(grad_features.shape, F32),
+        input_output_aliases={2: 0},
+        scratch_shapes=[pltpu.VMEM((late // span, span, width), F32), pltpu.SemaphoreType.DMA((late // span,))],
+        cost_estimate=pl.CostEstimate(
+            flops=2 * late * BLOCK * width, bytes_accessed=4 * late * width, transcendentals=0
+        ),
+        compiler_params=pltpu.CompilerParams(vmem_limit_bytes=12 << 20),
+    )(scaled, stencil, grad_features)
 
 
 def build(n, clusters):
     def local(features, weight, bias, adjacency, segments, cotangent):
         tile = 256 if n <= 4 else 512
-        held = exchange(features, adjacency, cotangent, segments, weight, bias, n, clusters, tile)[:6]
-        grad_features, out, grad_weight, grad_bias = finish(*held)
+        early = features.shape[0] // tile - TAIL
+        activations, scaled, total, stencil, blocks, _, grads, *landing = exchange(
+            features, adjacency, cotangent, segments, weight, bias, n, clusters, early, tile
+        )
+        grad_features, out, grad_weight, grad_bias = finish(activations, scaled, total, stencil, early, tile)
+        scaled = exchange_late(grads, landing, grad_bias, stencil, blocks, n, early, tile)
+        grad_features = finish_late(scaled, stencil, grad_features, early, tile)
         return (out, grad_features, grad_weight, grad_bias.reshape(-1))
 
     return local

time: 381 us -> 374 us (0.982)
  Pallas kernels: 379 us -> 372 us
    pallas_call x2 -> x4, Pallas kernels: 379 us -> 372 us  [the longest x1 339 us: exchange(): pl.pallas_call(functools.partial(exchange_kernel, n, clusters, early, til...]
where the time goes in v9:
time: 374 us; the launch traced here: 373 us
  Pallas kernels  372 us (99%)
    pallas_call x1, Pallas kernels, exchange(): pl.pallas_call(functools.partial(exchange_kernel, n, clusters, early, til...  339 us
    pallas_call x1, Pallas kernels, exchange_late(): pl.pallas_call(functools.partial(late_kernel, n, early, tile), in_specs=[...  22.1 us
    pallas_call x1, Pallas kernels, finish(): pl.pallas_call(functools.partial(finish_kernel, early * tile, 2 * tile),...  8.85 us

profile of v9, /device:TPU:0, one launch (start us, length us, event | category | flops | bytes accessed | tf_op | source)
XLA Modules:
  0.0 372.8 jit_solution(5643955509388688171)
XLA Ops:
  0.6 339.3 %shard_map.93 = (bf16[8192,512]{1,0:T(8,128)(2,1)S(1)}, bf16[8192,512]{1,0:T(8,128)(2,1)S(1)}, f32[2056,512]{1,0:T(8,128)S(1)}, bf16[8192,128]{1,0:T(8,128)(2,1)...) custom-call(bf16[8192,512]{1,0:T(8,128)(2,1)} %features.1, ...), custom_call_target="tpu_custom_call" | custom-call | tf_op jit(solution)/shard_map/pallas_call | solution.py:492
  339.9 8.8 %shard_map.94 = (f32[8192,512]{1,0:T(8,128)}, bf16[8192,512]{1,0:T(8,128)(2,1)}, f32[2048,512]{1,0:T(8,128)}, f32[1,512]{1,0:T(1,128)}) custom-call(bf16[8192,512]{1,0:T(8,128)(2,1)S(1)} %get-tuple-element.17.activations, bf16[8192,512]{1,0:T(8,128)(2,1)S(1)} %get-tuple-element.18.scaled, f32[2056,512]{1,0:T(8,128)S(1)} %get-tuple-element.19.total, ...), custom_call_target="tpu_custom_call" | custom-call | flops 1073741824 | bytes 29360128 | tf_op jit(solution)/shard_map/pallas_call | solution.py:592
  348.8 22.1 %shard_map.95.scaled = bf16[1536,512]{1,0:T(8,128)(2,1)S(1)} custom-call(bf16[8192,512]{1,0:T(8,128)(2,1)} %get-tuple-element.22.refs_0_, bf16[8192,512]{1,0:T(8,128)(2,1)} %get-tuple-element.23.refs_1_, bf16[8192,512]{1,0:T(8,128)(2,1)} %get-tuple-element.24.refs_2_, bf16[8192,512]{1,0:T(8,128)(2,1)} %get-tuple-element.25.refs_3_, ...), custom_call_target="tpu_custom_call" | custom-call | tf_op jit(solution)/shard_map/pallas_call | solution.py:708
  370.8 1.9 shard_map.96

commit v10 on v9

--- a/solution.py
+++ b/solution.py
@@ -9,7 +9,8 @@
 
 BLOCK = 128
 SLOTS = 4
-TAIL = 6
+TAIL = 8
+GROUP = 2
 F32 = jnp.float32
 BF16 = jnp.bfloat16
 MESH = pl.DeviceIdType.MESH
@@ -26,14 +27,17 @@
     return (links + jnp.where(row == column, 2.0, 0.0)).astype(BF16), inverse
 
 
-def back_through(piece, n, blocks, stencil):
+def back_through(piece, numbers, blocks):
     width = blocks.shape[1]
     value = None
-    for p in range(n):
-        term = lax.dot_general(
-            piece(p), blocks[pl.ds(p * width, width), :], (((1,), (1,)), ((), ())), preferred_element_type=F32
-        )
+    for p in numbers:
+        block = blocks[pl.ds(pl.multiple_of(p * width, width), width), :]
+        term = lax.dot_general(piece(p), block, (((1,), (1,)), ((), ())), preferred_element_type=F32)
         value = term if value is None else value + term
+    return value
+
+
+def scale(value, stencil):
     inverse = 1.0 / (jnp.sum(stencil.astype(F32), axis=1, keepdims=True) - 1.0)
     return (value.astype(BF16).astype(F32) * inverse).astype(BF16)
 
@@ -423,7 +427,7 @@
         slot = lax.rem(k, 2)
         for p in range(n):
             load_piece(p, k).wait()
-        scaled[at(k), :] = back_through(lambda p: back[slot, p], n, mat, sten[at(k), :])
+        scaled[at(k), :] = scale(back_through(lambda p: back[slot, p], range(n), mat), sten[at(k), :])
 
     def moment(r):
         return max(r * 512 // tile, 0)
@@ -635,9 +639,11 @@
             device_id={"col": device}, device_id_type=MESH,
         )
 
-    def load(p):
+    def load(p, part):
         source = landing[p] if p else grads
-        return pltpu.make_async_copy(source.at[kept], pieces.at[p], load_sem.at[p])
+        first, size = ((0, 2 * tile), (2 * tile, (late - 2) * tile))[part]
+        here = source.at[pl.ds(early * tile + first, size)]
+        return pltpu.make_async_copy(here, pieces.at[p, pl.ds(first, size)], load_sem.at[part, p])
 
     def far(p, j):
         source = grads.at[pl.ds(pl.multiple_of((early + j) * tile, tile), tile)]
@@ -647,8 +653,9 @@
         return remote(pieces.at[p - 1, at(j)], pieces.at[p, at(j)], near_out.at[p], near_in.at[p // 2 - 1, j], sibling)
 
     barrier = pltpu.get_barrier_semaphore()
-    load(0).start()
-    load(1).start()
+    for part in range(2):
+        for p in range(2):
+            load(p, part).start()
 
     @pl.when(core == 0)
     def _():
@@ -663,33 +670,71 @@
 
     @pl.when(core == 1)
     def _():
-        for p in range(2, n, 2):
-            load(p).start()
+        for part in range(2):
+            for p in range(2, n, 2):
+                load(p, part).start()
         pl.semaphore_wait(barrier, 1)
         pl.semaphore_signal(barrier, inc=1, device_id={"col": sibling}, device_id_type=MESH)
-        for p in range(2, n, 2):
-            load(p).wait()
-        for j in range(late):
-            for p in range(3, n, 2):
-                near(p, j).start()
-
-    load(0).wait()
-    load(1).wait()
-
-    def step(j, carry):
+        for part in range(2):
+            for p in range(2, n, 2):
+                load(p, part).wait()
+            for j in ((0, 1), range(2, late))[part]:
+                for p in range(3, n, 2):
+                    near(p, j).start()
+
+    def loaded(part):
+        for p in range(2):
+            load(p, part).wait()
+
+    def take(j):
         @pl.when(core == 0)
         def _():
             for p in range(2, n, 2):
                 far(p, j).wait_recv()
                 near(p + 1, j).start()
 
+    def wait_near(j):
         for p in range(3, n, 2):
             near(p, j).wait_recv()
-        stencil = sten[pl.ds(pl.multiple_of((early + j) * tile, tile), tile), :]
-        scaled[at(j), :] = back_through(lambda p: pieces[p, at(j), :], n, mat, stencil)
+
+    def products(j, size, numbers):
+        rows = pl.ds(pl.multiple_of(j * tile, tile), size * tile)
+        return back_through(lambda p: pieces[p, rows, :], numbers, mat)
+
+    def store(j, size, value):
+        rows = pl.ds(pl.multiple_of((early + j) * tile, tile), size * tile)
+        scaled[pl.ds(pl.multiple_of(j * tile, tile), size * tile), :] = scale(value, sten[rows, :])
+
+    def step(g, carry):
+        for j in range(GROUP):
+            take(GROUP * g + j)
+        for j in range(GROUP):
+            wait_near(GROUP * g + j)
+        store(GROUP * g, GROUP, products(GROUP * g, GROUP, range(n)))
         return carry
 
-    lax.fori_loop(0, late, step, 0)
+    loaded(0)
+    lax.fori_loop(0, 2 // GROUP, step, 0)
+    loaded(1)
+    lax.fori_loop(2 // GROUP, (late - 2) // GROUP, step, 0)
+    last = late - 1
+    take(last - 1)
+    wait_near(last - 1)
+    store(last - 1, 1, products(last - 1, 1, range(n)))
+    first = [0, 1] + [2 * shift + 1 - core for shift in range(1, outer)]
+
+    @pl.when(core == 0)
+    def _():
+        wait_near(last)
+
+    value = products(last, 1, first)
+    take(last)
+
+    @pl.when(core == 1)
+    def _():
+        wait_near(last)
+
+    store(last, 1, value + products(last, 1, [2 * shift + core for shift in range(1, outer)]))
 
     @pl.when(core == 0)
     def _():
@@ -712,14 +757,14 @@
         out_shape=pltpu.VMEM((late * tile, width), BF16),
         scratch_shapes=[
             pltpu.VMEM((n, late * tile, width), BF16),
-            dma((n,)),
+            dma((2, n)),
             dma((n,)),
             dma((outer - 1, late)),
             dma((n,)),
             dma((outer - 1, late)),
         ],
         compiler_params=pltpu.CompilerParams(
-            collective_id=1, has_side_effects=True, vmem_limit_bytes=12 << 20
+            collective_id=1, has_side_effects=True, vmem_limit_bytes=20 << 20
         ),
     )(*far, stencil, blocks)
 

time: 374 us -> 373 us (level)
    pallas_call x1, Pallas kernels: 339 us -> 328 us  [exchange(): pl.pallas_call(functools.partial(exchange_kernel, n, clusters, early, til...]
    pallas_call x1, Pallas kernels: 22.1 us -> 31.9 us  [exchange_late(): pl.pallas_call(functools.partial(late_kernel, n, early, tile), in_specs=[...]
where the time goes in v10:
time: 373 us; the launch traced here: 371 us
  Pallas kernels  371 us (99%)
    pallas_call x1, Pallas kernels, exchange(): pl.pallas_call(functools.partial(exchange_kernel, n, clusters, early, til...  328 us
    pallas_call x1, Pallas kernels, exchange_late(): pl.pallas_call(functools.partial(late_kernel, n, early, tile), in_specs=[...  31.9 us
    pallas_call x1, Pallas kernels, finish(): pl.pallas_call(functools.partial(finish_kernel, early * tile, 2 * tile),...  8.53 us

profile of v10, /device:TPU:0, one launch (start us, length us, event | category | flops | bytes accessed | tf_op | source)
XLA Modules:
  0.0 371.4 jit_solution(122237349585273562)
XLA Ops:
  0.6 328.1 %shard_map.93 = (bf16[8192,512]{1,0:T(8,128)(2,1)S(1)}, bf16[8192,512]{1,0:T(8,128)(2,1)S(1)}, f32[2056,512]{1,0:T(8,128)S(1)}, bf16[8192,128]{1,0:T(8,128)(2,1)...) custom-call(bf16[8192,512]{1,0:T(8,128)(2,1)} %features.1, ...), custom_call_target="tpu_custom_call" | custom-call | tf_op jit(solution)/shard_map/pallas_call | solution.py:496
  328.7 8.5 %shard_map.94 = (f32[8192,512]{1,0:T(8,128)}, bf16[8192,512]{1,0:T(8,128)(2,1)}, f32[2048,512]{1,0:T(8,128)}, f32[1,512]{1,0:T(1,128)}) custom-call(bf16[8192,512]{1,0:T(8,128)(2,1)S(1)} %get-tuple-element.17.activations, bf16[8192,512]{1,0:T(8,128)(2,1)S(1)} %get-tuple-element.18.scaled, f32[2056,512]{1,0:T(8,128)S(1)} %get-tuple-element.19.total, ...), custom_call_target="tpu_custom_call" | custom-call | flops 1073741824 | bytes 29360128 | tf_op jit(solution)/shard_map/pallas_call | solution.py:596
  337.3 31.9 %shard_map.95.scaled = bf16[2048,512]{1,0:T(8,128)(2,1)S(1)} custom-call(bf16[8192,512]{1,0:T(8,128)(2,1)} %get-tuple-element.22.refs_0_, bf16[8192,512]{1,0:T(8,128)(2,1)} %get-tuple-element.23.refs_1_, bf16[8192,512]{1,0:T(8,128)(2,1)} %get-tuple-element.24.refs_2_, bf16[8192,512]{1,0:T(8,128)(2,1)} %get-tuple-element.25.refs_3_, ...), custom_call_target="tpu_custom_call" | custom-call | tf_op jit(solution)/shard_map/pallas_call | solution.py:753
  369.2 2.3 shard_map.96

commit v11 on v10

--- a/solution.py
+++ b/solution.py
@@ -9,7 +9,7 @@
 
 BLOCK = 128
 SLOTS = 4
-TAIL = 8
+TAIL = 6
 GROUP = 2
 F32 = jnp.float32
 BF16 = jnp.bfloat16
@@ -209,8 +209,31 @@
         span = pl.ds(0, tiles * tile)
         return remote(grads.at[span], landing[1].at[span], send, arrival, sibling)
 
+    border = early // 2 - 1
+
+    def border_hop(p, i):
+        rows, c = at(early - 2 + i), (border, count // 2)[i]
+        source = landing[p - 1] if p % 2 else grads
+        device = sibling if p % 2 else chip_at(-(p // 2))
+        arrival = grad_near.at[c] if p % 2 else grad_far.at[p // 2 - 1, c]
+        return remote(source.at[rows], landing[p].at[rows], grad_out.at[p], arrival, device)
+
+    def pass_border(i):
+        for p in range(2, n, 2):
+            border_hop(p, i).wait_recv()
+            border_hop(p + 1, i).start()
+        several(outer - 1 + 2 * (1 - i), grad_out.at[0], grad_near.at[(border, count // 2)[i]]).wait_recv()
+        for p in range(n):
+            load_piece(p, early - 2 + i).start()
+
     def send_grad(c):
-        @pl.when((c < early // 2) | (core == 1))
+        @pl.when(c == border)
+        def _():
+            for i in range(2):
+                for p in range(2, n, 2):
+                    border_hop(p, i).start()
+
+        @pl.when((c < border) | ((core == 1) & (c > border)))
         def _():
             for shift in range(1, outer):
                 grad_hop(2 * shift, c).start()
@@ -253,6 +276,16 @@
             return pltpu.make_async_copy(source, blocks_out.at[p], block_recv.at[p])
         return remote(source, blocks_out.at[p], block_send.at[p], block_recv.at[p], sibling)
 
+    barrier = pltpu.get_barrier_semaphore()
+    centre = clusters - 2 + core
+    neighbours = [sibling] + [chip_at(shift) for shift in range(1, outer)]
+
+    def greet(axis, peer):
+        pl.semaphore_signal(barrier, inc=1, device_id={axis: peer}, device_id_type=MESH)
+
+    for peer in neighbours:
+        greet("col", peer)
+
     for copy in loads(0):
         copy.start()
     fixed = [
@@ -263,16 +296,6 @@
         copy.start()
     load_cot(0).start()
 
-    barrier = pltpu.get_barrier_semaphore()
-    centre = clusters - 2 + core
-    neighbours = [sibling] + [chip_at(shift) for shift in range(1, outer)]
-
-    def greet(axis, peer):
-        pl.semaphore_signal(barrier, inc=1, device_id={axis: peer}, device_id_type=MESH)
-
-    for peer in neighbours:
-        greet("col", peer)
-
     @pl.when(cluster == centre)
     def _():
         pl.semaphore_wait(barrier, len(neighbours) + len(others))
@@ -282,10 +305,10 @@
     @pl.when(cluster != centre)
     def _():
         pl.semaphore_wait(barrier, len(neighbours))
-        greet("clu", centre)
 
     for shift in range(1, outer):
         share(shift).start()
+    pl.when(cluster != centre)(functools.partial(greet, "clu", centre))
     block(0).start()
     block(1).start()
     fixed[0].wait()
@@ -437,7 +460,10 @@
         def _():
             backward_tile(k - 1)
 
-        @pl.when((k < early) & (lax.rem(k, 2) == 0))
+        for i in range(2):
+            pl.when(k == early - 2 + i)(functools.partial(pass_border, i))
+
+        @pl.when((k < early - 2) & (lax.rem(k, 2) == 0))
         def _():
             for shift in range(1, outer):
                 grad_hop(2 * shift, k // 2).wait_recv()
@@ -525,8 +551,8 @@
             dma((outer - 1, count // 2)),
             dma((count // 2,)),
             dma((n,)),
-            dma((outer - 1, count // 2)),
-            dma((count // 2,)),
+            dma((outer - 1, count // 2 + 1)),
+            dma((count // 2 + 1,)),
             dma((2, n)),
             dma((outer,)),
             dma((outer,)),
@@ -653,9 +679,6 @@
         return remote(pieces.at[p - 1, at(j)], pieces.at[p, at(j)], near_out.at[p], near_in.at[p // 2 - 1, j], sibling)
 
     barrier = pltpu.get_barrier_semaphore()
-    for part in range(2):
-        for p in range(2):
-            load(p, part).start()
 
     @pl.when(core == 0)
     def _():
@@ -666,13 +689,17 @@
             for p in range(2, n, 2):
                 far(p, j).start()
         pl.semaphore_signal(barrier, inc=1, device_id={"col": sibling}, device_id_type=MESH)
+        for part in range(2):
+            for p in range(2):
+                load(p, part).start()
         pl.semaphore_wait(barrier, 1)
 
     @pl.when(core == 1)
     def _():
         for part in range(2):
-            for p in range(2, n, 2):
-                load(p, part).start()
+            for p in range(n):
+                if p < 2 or p % 2 == 0:
+                    load(p, part).start()
         pl.semaphore_wait(barrier, 1)
         pl.semaphore_signal(barrier, inc=1, device_id={"col": sibling}, device_id_type=MESH)
         for part in range(2):

time: 373 us -> 373 us (level)
    pallas_call x1, Pallas kernels: 31.9 us -> 22.1 us  [exchange_late(): pl.pallas_call(functools.partial(late_kernel, n, early, tile), in_specs=[...]
    pallas_call x1, Pallas kernels: 328 us -> 338 us  [exchange(): pl.pallas_call(functools.partial(exchange_kernel, n, clusters, early, til...]
where the time goes in v11:
time: 373 us; the launch traced here: 371 us
  Pallas kernels  371 us (99%)
    pallas_call x1, Pallas kernels, exchange(): pl.pallas_call(functools.partial(exchange_kernel, n, clusters, early, til...  338 us
    pallas_call x1, Pallas kernels, exchange_late(): pl.pallas_call(functools.partial(late_kernel, n, early, tile), in_specs=[...  22.1 us
    pallas_call x1, Pallas kernels, finish(): pl.pallas_call(functools.partial(finish_kernel, early * tile, 2 * tile),...  8.85 us

profile of v11, /device:TPU:0, one launch (start us, length us, event | category | flops | bytes accessed | tf_op | source)
XLA Modules:
  0.0 371.4 jit_solution(10152068388339768666)
XLA Ops:
  0.6 337.8 %shard_map.93 = (bf16[8192,512]{1,0:T(8,128)(2,1)S(1)}, bf16[8192,512]{1,0:T(8,128)(2,1)S(1)}, f32[2056,512]{1,0:T(8,128)S(1)}, bf16[8192,128]{1,0:T(8,128)(2,1)...) custom-call(bf16[8192,512]{1,0:T(8,128)(2,1)} %features.1, ...), custom_call_target="tpu_custom_call" | custom-call | tf_op jit(solution)/shard_map/pallas_call | solution.py:522
  338.5 8.8 %shard_map.94 = (f32[8192,512]{1,0:T(8,128)}, bf16[8192,512]{1,0:T(8,128)(2,1)}, f32[2048,512]{1,0:T(8,128)}, f32[1,512]{1,0:T(1,128)}) custom-call(bf16[8192,512]{1,0:T(8,128)(2,1)S(1)} %get-tuple-element.17.activations, bf16[8192,512]{1,0:T(8,128)(2,1)S(1)} %get-tuple-element.18.scaled, f32[2056,512]{1,0:T(8,128)S(1)} %get-tuple-element.19.total, ...), custom_call_target="tpu_custom_call" | custom-call | flops 1073741824 | bytes 29360128 | tf_op jit(solution)/shard_map/pallas_call | solution.py:622
  347.3 22.1 %shard_map.95.scaled = bf16[1536,512]{1,0:T(8,128)(2,1)S(1)} custom-call(bf16[8192,512]{1,0:T(8,128)(2,1)} %get-tuple-element.22.refs_0_, bf16[8192,512]{1,0:T(8,128)(2,1)} %get-tuple-element.23.refs_1_, bf16[8192,512]{1,0:T(8,128)(2,1)} %get-tuple-element.24.refs_2_, bf16[8192,512]{1,0:T(8,128)(2,1)} %get-tuple-element.25.refs_3_, ...), custom_call_target="tpu_custom_call" | custom-call | tf_op jit(solution)/shard_map/pallas_call | solution.py:780
  369.4 1.9 shard_map.96

commit v12 on v11

--- a/solution.py
+++ b/solution.py
@@ -243,27 +243,27 @@
     def load_piece(p, k):
         slot = lax.rem(k, 2)
         source = landing[p] if p else grads
-        return pltpu.make_async_copy(source.at[at(k)], back.at[slot, p], back_sem.at[slot, p])
+        return pltpu.make_async_copy(source.at[at(k)], back.at[slot, pl.ds(p * tile, tile)], back_sem.at[slot])
 
     def share(shift):
         owner = lax.rem(chip - shift + outer, outer)
         rows = pl.ds(pl.multiple_of(owner * 2 * width + cluster * part, part), part)
         mine = pl.ds(pl.multiple_of(cluster * part, part), part)
         return remote(
-            weight.at[rows], shares.at[shift, mine], share_send.at[shift], share_recv.at[shift], chip_at(-shift)
+            weight.at[rows], shares.at[shift, mine], share_send.at[shift - 1], share_recv.at[shift - 1], chip_at(-shift)
         )
 
     def spread(shift, source, peer):
         rows = pl.ds(pl.multiple_of(source * part, part), part)
         return remote(
             shares.at[shift, rows], shares.at[shift, rows],
-            spread_send.at[shift], spread_recv.at[shift], peer, "clu",
+            spread_send.at[shift - 1], spread_recv.at[shift - 1], peer, "clu",
         )
 
     def all_shares(shift):
         rows = pl.ds(0, len(others) * part)
         return remote(
-            shares.at[shift, rows], shares.at[shift, rows], spread_send.at[shift], spread_recv.at[shift], others[0], "clu"
+            shares.at[shift, rows], shares.at[shift, rows], spread_send.at[shift - 1], spread_recv.at[shift - 1], others[0], "clu"
         )
 
     def block(p):
@@ -448,9 +448,8 @@
 
     def backward_tile(k):
         slot = lax.rem(k, 2)
-        for p in range(n):
-            load_piece(p, k).wait()
-        scaled[at(k), :] = scale(back_through(lambda p: back[slot, p], range(n), mat), sten[at(k), :])
+        pltpu.make_async_copy(grads.at[pl.ds(0, n * tile)], back.at[slot], back_sem.at[slot]).wait()
+        scaled[at(k), :] = scale(back_through(lambda p: back[slot, pl.ds(p * tile, tile), :], range(n), mat), sten[at(k), :])
 
     def moment(r):
         return max(r * 512 // tile, 0)
@@ -542,7 +541,7 @@
             pltpu.VMEM((width,), BF16),
             pltpu.VMEM((depth + 8, width), F32),
             pltpu.VMEM((outer, 2 * width, width), BF16),
-            pltpu.VMEM((2, n, tile, width), BF16),
+            pltpu.VMEM((2, n * tile, width), BF16),
             dma((2, 2)),
             dma((2,)),
             dma((2,)),
@@ -553,11 +552,11 @@
             dma((n,)),
             dma((outer - 1, count // 2 + 1)),
             dma((count // 2 + 1,)),
-            dma((2, n)),
-            dma((outer,)),
-            dma((outer,)),
-            dma((outer,)),
-            dma((outer,)),
+            dma((2,)),
+            dma((outer - 1,)),
+            dma((outer - 1,)),
+            dma((outer - 1,)),
+            dma((outer - 1,)),
             dma((n,)),
             dma((n,)),
             pltpu.VMEM((parts, depth // parts // 2, width), F32),

time: 373 us -> 373 us (level)
  no operation moved by 1% of the time
where the time goes in v12:
time: 373 us; the launch traced here: 371 us
  Pallas kernels  371 us (99%)
    pallas_call x1, Pallas kernels, exchange(): pl.pallas_call(functools.partial(exchange_kernel, n, clusters, early, til...  338 us
    pallas_call x1, Pallas kernels, exchange_late(): pl.pallas_call(functools.partial(late_kernel, n, early, tile), in_specs=[...  22.1 us
    pallas_call x1, Pallas kernels, finish(): pl.pallas_call(functools.partial(finish_kernel, early * tile, 2 * tile),...  8.85 us

profile of v12, /device:TPU:0, one launch (start us, length us, event | category | flops | bytes accessed | tf_op | source)
XLA Modules:
  0.0 371.3 jit_solution(9719637373202731235)
XLA Ops:
  0.6 337.7 %shard_map.93 = (bf16[8192,512]{1,0:T(8,128)(2,1)S(1)}, bf16[8192,512]{1,0:T(8,128)(2,1)S(1)}, f32[2056,512]{1,0:T(8,128)S(1)}, bf16[8192,128]{1,0:T(8,128)(2,1)...) custom-call(bf16[8192,512]{1,0:T(8,128)(2,1)} %features.1, ...), custom_call_target="tpu_custom_call" | custom-call | tf_op jit(solution)/shard_map/pallas_call | solution.py:521
  338.4 8.8 %shard_map.94 = (f32[8192,512]{1,0:T(8,128)}, bf16[8192,512]{1,0:T(8,128)(2,1)}, f32[2048,512]{1,0:T(8,128)}, f32[1,512]{1,0:T(1,128)}) custom-call(bf16[8192,512]{1,0:T(8,128)(2,1)S(1)} %get-tuple-element.17.activations, bf16[8192,512]{1,0:T(8,128)(2,1)S(1)} %get-tuple-element.18.scaled, f32[2056,512]{1,0:T(8,128)S(1)} %get-tuple-element.19.total, ...), custom_call_target="tpu_custom_call" | custom-call | flops 1073741824 | bytes 29360128 | tf_op jit(solution)/shard_map/pallas_call | solution.py:621
  347.2 22.1 %shard_map.95.scaled = bf16[1536,512]{1,0:T(8,128)(2,1)S(1)} custom-call(bf16[8192,512]{1,0:T(8,128)(2,1)} %get-tuple-element.22.refs_0_, bf16[8192,512]{1,0:T(8,128)(2,1)} %get-tuple-element.23.refs_1_, bf16[8192,512]{1,0:T(8,128)(2,1)} %get-tuple-element.24.refs_2_, bf16[8192,512]{1,0:T(8,128)(2,1)} %get-tuple-element.25.refs_3_, ...), custom_call_target="tpu_custom_call" | custom-call | tf_op jit(solution)/shard_map/pallas_call | solution.py:779
  369.3 1.9 shard_map.96

commit v13 on v11

--- a/solution.py
+++ b/solution.py
@@ -10,7 +10,7 @@
 BLOCK = 128
 SLOTS = 4
 TAIL = 6
-GROUP = 2
+GROUP = 1
 F32 = jnp.float32
 BF16 = jnp.bfloat16
 MESH = pl.DeviceIdType.MESH

time: 373 us -> 373 us (level)
  no operation moved by 1% of the time
where the time goes in v13:
time: 373 us; the launch traced here: 371 us
  Pallas kernels  371 us (99%)
    pallas_call x1, Pallas kernels, exchange(): pl.pallas_call(functools.partial(exchange_kernel, n, clusters, early, til...  338 us
    pallas_call x1, Pallas kernels, exchange_late(): pl.pallas_call(functools.partial(late_kernel, n, early, tile), in_specs=[...  22.1 us
    pallas_call x1, Pallas kernels, finish(): pl.pallas_call(functools.partial(finish_kernel, early * tile, 2 * tile),...  8.85 us

profile of v13, /device:TPU:0, one launch (start us, length us, event | category | flops | bytes accessed | tf_op | source)
XLA Modules:
  0.0 371.4 jit_solution(1051483955678839858)
XLA Ops:
  0.6 337.8 %shard_map.93 = (bf16[8192,512]{1,0:T(8,128)(2,1)S(1)}, bf16[8192,512]{1,0:T(8,128)(2,1)S(1)}, f32[2056,512]{1,0:T(8,128)S(1)}, bf16[8192,128]{1,0:T(8,128)(2,1)...) custom-call(bf16[8192,512]{1,0:T(8,128)(2,1)} %features.1, ...), custom_call_target="tpu_custom_call" | custom-call | tf_op jit(solution)/shard_map/pallas_call | solution.py:522
  338.5 8.8 %shard_map.94 = (f32[8192,512]{1,0:T(8,128)}, bf16[8192,512]{1,0:T(8,128)(2,1)}, f32[2048,512]{1,0:T(8,128)}, f32[1,512]{1,0:T(1,128)}) custom-call(bf16[8192,512]{1,0:T(8,128)(2,1)S(1)} %get-tuple-element.17.activations, bf16[8192,512]{1,0:T(8,128)(2,1)S(1)} %get-tuple-element.18.scaled, f32[2056,512]{1,0:T(8,128)S(1)} %get-tuple-element.19.total, ...), custom_call_target="tpu_custom_call" | custom-call | flops 1073741824 | bytes 29360128 | tf_op jit(solution)/shard_map/pallas_call | solution.py:622
  347.3 22.1 %shard_map.95.scaled = bf16[1536,512]{1,0:T(8,128)(2,1)S(1)} custom-call(bf16[8192,512]{1,0:T(8,128)(2,1)} %get-tuple-element.22.refs_0_, bf16[8192,512]{1,0:T(8,128)(2,1)} %get-tuple-element.23.refs_1_, bf16[8192,512]{1,0:T(8,128)(2,1)} %get-tuple-element.24.refs_2_, bf16[8192,512]{1,0:T(8,128)(2,1)} %get-tuple-element.25.refs_3_, ...), custom_call_target="tpu_custom_call" | custom-call | tf_op jit(solution)/shard_map/pallas_call | solution.py:780
  369.4 1.9 shard_map.96
